TPU v7x, 128 devices: a whole 4x4x4 slice. The times are simulated.
128 devices in a mesh: dp: 2 (over x_hi), pipe: 4 (over z), tensor: 16 (over x_lo, y, core).
Axes of the slice: x: 4 (x_hi: 2, x_lo: 2; x = x_hi * 2 + x_lo), y: 4, z: 4, core: 2. Of those that a mesh axis runs over, the one named last changes fastest.
Arguments:
- inputs: bfloat16 [4, 3072, 8192], P('pipe', 'dp', 'tensor'), may hold values from -6 to 6
- upstream: bfloat16 [4, 3072, 8192], P('pipe', 'dp', 'tensor'), may hold values from -6 to 6
- factor_one: bfloat16 [4, 32, 4, 256, 256], P('pipe', 'tensor'), may hold values from -0.375 to 0.375
- factor_two: bfloat16 [4, 128, 256, 256], P('pipe', 'tensor'), may hold values from -0.375 to 0.375
- factor_three: bfloat16 [4, 128, 256, 256], P('pipe', 'tensor'), may hold values from -0.375 to 0.375
- factor_four: bfloat16 [4, 32, 4, 256, 256], P('pipe', 'tensor'), may hold values from -0.1875 to 0.1875
Outputs:
- y_next: bfloat16 [4, 3072, 8192], P('pipe', 'dp', 'tensor')
- dx_prev: bfloat16 [4, 3072, 8192], P('pipe', 'dp', 'tensor')
- grad_one: float32 [4, 32, 4, 256, 256], P('pipe', 'tensor')
- grad_two: float32 [4, 128, 256, 256], P('pipe', 'tensor')
- grad_three: float32 [4, 128, 256, 256], P('pipe', 'tensor')
- grad_four: float32 [4, 32, 4, 256, 256], P('pipe', 'tensor')
All inputs are finite; a program needn't handle non-finite values.
Results may differ from a plain program's by a relative error of at most 0.0068.
Values may be sent and summed in bfloat16 or wider, within the bound.
No kernel may reach another device: no remote copies, remote signals or barrier semaphores. Data moves between devices by JAX's collectives and lax.ppermute only.
A program may use at most 192 MiB of HBM per device.

v0:
```python
import jax
import jax.numpy as jnp
from jax import lax
from jax.sharding import PartitionSpec as P


def shifted(value, axis, steps):
    count = lax.axis_size(axis)
    leading, last = (max(0, -steps), min(count, count - steps))
    return lax.ppermute(value, axis, [(source, source + steps) for source in range(leading, last)])


def to_peers(blocks, parts):
    rows, local, width = blocks.shape
    inner = width // (parts * local)
    shaped = blocks.reshape(rows, local, parts, local, inner)
    return shaped.transpose(0, 2, 1, 3, 4).reshape(rows, parts, local * local * inner)


def from_peers(received, local):
    rows, parts, flat = received.shape
    inner = flat // (local * local)
    shaped = received.reshape(rows, parts, local, local, inner)
    return shaped.transpose(0, 3, 1, 2, 4).reshape(rows, local, parts * local * inner)


def shards(inputs, upstream, factor_one, factor_two, factor_three, factor_four):
    parts = lax.axis_size("tensor")
    acts = inputs[0]
    grad_out = upstream[0]
    first = factor_one[0]
    second = factor_two[0]
    third = factor_three[0]
    fourth = factor_four[0]
    groups, expand, bsize = (first.shape[0], first.shape[1], first.shape[2])
    local = groups * expand
    rows = acts.shape[0]
    grouped = acts.reshape(rows, groups, bsize)
    lifted = (
        jnp.einsum("tgi,gkij->tgkj", grouped, first, preferred_element_type=jnp.float32)
        .astype(jnp.bfloat16)
        .reshape(rows, local, bsize)
    )
    outbound = to_peers(lifted, parts)
    mixed = from_peers(
        lax.all_to_all(outbound, "tensor", split_axis=1, concat_axis=1, tiled=True), local
    )
    preact = jnp.einsum("tcj,cjn->tcn", mixed, second, preferred_element_type=jnp.float32)
    active = jax.nn.gelu(preact).astype(jnp.bfloat16)
    mixed, preact, active = (mixed, preact, active)
    narrowed = jnp.einsum("tcn,cno->tco", active, third, preferred_element_type=jnp.float32).astype(
        jnp.bfloat16
    )
    outbound = to_peers(narrowed, parts)
    spread = from_peers(
        lax.all_to_all(outbound, "tensor", split_axis=1, concat_axis=1, tiled=True), local
    )
    count = spread.shape[0]
    output = jnp.einsum(
        "tgkr,gkro->tgo",
        spread.reshape(count, groups, expand, bsize),
        fourth,
        preferred_element_type=jnp.float32,
    ).astype(jnp.bfloat16)
    spread, output = (spread, output.reshape(count, groups * bsize))
    y_next = shifted(output[None], "pipe", 1)
    grad_grouped = grad_out.reshape(rows, groups, bsize)
    spread_four = spread.reshape(rows, groups, expand, bsize)
    grad_spread = (
        jnp.einsum("tgo,gkro->tgkr", grad_grouped, fourth, preferred_element_type=jnp.float32)
        .astype(jnp.bfloat16)
        .reshape(rows, local, bsize)
    )
    grad_four = jnp.einsum(
        "tgkr,tgo->gkro", spread_four, grad_grouped, preferred_element_type=jnp.float32
    )
    outbound = to_peers(grad_spread, parts)
    grad_narrow = from_peers(
        lax.all_to_all(outbound, "tensor", split_axis=1, concat_axis=1, tiled=True), local
    )
    grad_active = jnp.einsum("tco,cno->tcn", grad_narrow, third, preferred_element_type=jnp.float32)
    grad_narrow, grad_active = (grad_narrow, grad_active)
    grad_three = jnp.einsum("tcn,tco->cno", active, grad_narrow, preferred_element_type=jnp.float32)
    pulled = jax.vjp(jax.nn.gelu, preact)[1]
    grad_pre = pulled(grad_active)[0].astype(jnp.bfloat16)
    grad_two = jnp.einsum("tcj,tcn->cjn", mixed, grad_pre, preferred_element_type=jnp.float32)
    grad_mixed = jnp.einsum(
        "tcn,cjn->tcj", grad_pre, second, preferred_element_type=jnp.float32
    ).astype(jnp.bfloat16)
    outbound = to_peers(grad_mixed, parts)
    grad_lift = from_peers(
        lax.all_to_all(outbound, "tensor", split_axis=1, concat_axis=1, tiled=True), local
    )
    count = grad_lift.shape[0]
    grad_input = jnp.einsum(
        "tgkj,gkij->tgi",
        grad_lift.reshape(count, groups, expand, bsize),
        first,
        preferred_element_type=jnp.float32,
    ).astype(jnp.bfloat16)
    grad_lift, grad_input = (grad_lift, grad_input.reshape(count, groups * bsize))
    dx_prev = shifted(grad_input[None], "pipe", -1)
    grad_one = jnp.einsum(
        "tgi,tgkj->gkij",
        grouped,
        grad_lift.reshape(rows, groups, expand, bsize),
        preferred_element_type=jnp.float32,
    )
    grad_one, grad_two, grad_three, grad_four = lax.psum(
        (grad_one, grad_two, grad_three, grad_four), "dp"
    )
    return (y_next, dx_prev, grad_one[None], grad_two[None], grad_three[None], grad_four[None])


def solution(mesh):
    return jax.shard_map(
        shards,
        mesh=mesh,
        in_specs=(
            P("pipe", "dp", "tensor"),
            P("pipe", "dp", "tensor"),
            P("pipe", "tensor", None, None, None),
            P("pipe", "tensor", None, None),
            P("pipe", "tensor", None, None),
            P("pipe", "tensor", None, None, None),
        ),
        out_specs=(
            P("pipe", "dp", "tensor"),
            P("pipe", "dp", "tensor"),
            P("pipe", "tensor", None, None, None),
            P("pipe", "tensor", None, None),
            P("pipe", "tensor", None, None),
            P("pipe", "tensor", None, None, None),
        ),
        check_vma=False,
    )
```

profile of v0, /device:TPU:1, one launch (start us, length us, event | category | flops | bytes accessed | tf_op | source)
XLA Modules:
  0.0 716.5 jit_solution(1809731829033732592)
XLA Ops:
  9.7 6.5 convert_bitcast_fusion.3
  16.1 13.3 %reshape_reshape.14 = bf16[1536,8,16,8,2]{0,4,3,2,1:T(2,128)(2,1)} reshape(bf16[1536,2,4,256]{0,3,2,1:T(8,128)(2,1)} %convert_bitcast_fusion.3) | data formatting | bytes 12582912 | tf_op jit(solution)/shard_map/reshape;reshape | solution.py:16
  29.5 9.5 %copy.53 = bf16[1536,8,16,8,2]{0,2,4,3,1:T(8,128)(2,1)S(1)} copy(bf16[1536,8,16,8,2]{0,4,3,2,1:T(2,128)(2,1)} %reshape_reshape.14) | data formatting | bytes 12582912 | tf_op jit(solution)/shard_map/reshape;reshape | solution.py:16
  38.9 6.1 copy.54
  45.1 7.5 %all-to-all-start = ((bf16[1536,16,128]{0,2,1:T(8,128)(2,1)}), bf16[1536,16,128]{0,2,1:T(8,128)(2,1)}, u32[]{:S(2)}, u32[]{:S(2)}) async-start(bf16[1536,16,128]{0,2,1:T(8,128)(2,1)} %copy.54), calls=%async_computation | async-start | bytes 12582912 | tf_op jit(solution)/shard_map/all_to_all | solution.py:46
  55.0 6.2 convert_bitcast_fusion.1
  61.2 13.1 %reshape_reshape.16 = bf16[1536,8,16,8,2]{0,4,3,2,1:T(2,128)(2,1)} reshape(bf16[1536,2,4,256]{0,3,2,1:T(8,128)(2,1)} %convert_bitcast_fusion.1) | data formatting | bytes 12582912 | tf_op jit(solution)/shard_map/reshape;reshape | solution.py:16
  74.3 9.5 %copy.67 = bf16[1536,8,16,8,2]{0,2,4,3,1:T(8,128)(2,1)S(1)} copy(bf16[1536,8,16,8,2]{0,4,3,2,1:T(2,128)(2,1)} %reshape_reshape.16) | data formatting | bytes 12582912 | tf_op jit(solution)/shard_map/reshape;reshape | solution.py:16
  83.8 6.1 copy.68
  90.0 51.1 %all-to-all-done = bf16[1536,16,128]{0,2,1:T(8,128)(2,1)} async-done(((bf16[1536,16,128]{0,2,1:T(8,128)(2,1)}), bf16[1536,16,128]{0,2,1:T(8,128)(2,1)}, u32[]{:S(2)}, u32[]{:S(2)}) %all-to-all-start) | async-done | bytes 6291488 | tf_op jit(solution)/shard_map/all_to_all | solution.py:46
  141.0 12.0 %all-to-all-start.2 = ((bf16[1536,16,128]{0,2,1:T(8,128)(2,1)}), bf16[1536,16,128]{0,2,1:T(8,128)(2,1)}, u32[]{:S(2)}, u32[]{:S(2)}) async-start(bf16[1536,16,128]{0,2,1:T(8,128)(2,1)} %copy.68), calls=%async_computation.2 | async-start | bytes 12582912 | tf_op jit(solution)/shard_map/all_to_all | solution.py:79
  153.1 6.3 copy.55
  159.4 3.5 copy.56
  162.9 9.2 %fusion.11 = f32[8,1536,256]{2,1,0:T(8,128)} fusion(bf16[1536,8,256]{0,1,2:T(8,128)(2,1)S(1)} %bitcast.136, bf16[1,8,256,256]{3,2,1,0:T(8,128)(2,1)S(1)} %copy-done.3), kind=kOutput, calls=%fused_computation.20 | convolution fusion | flops 1610612736 | bytes 19922944 | tf_op jit(solution)/shard_map/tcj,cjn->tcn/dot_general | solution.py:48
  172.1 9.8 %convert_bitcast_fusion.2 = bf16[1536,8,256]{0,2,1:T(8,128)(2,1)} fusion(bf16[1,8,256,256]{3,2,1,0:T(8,128)(2,1)S(1)} %copy-done, f32[8,1536,256]{2,1,0:T(8,128)} %fusion.11), kind=kOutput, calls=%fused_computation.18 | convolution fusion | flops 1642070016 | bytes 19922944 | tf_op jit(solution)/shard_map/tcn,cno->tco/dot_general | solution.py:51
  181.9 13.1 %reshape.51 = bf16[1536,8,16,8,2]{0,4,3,2,1:T(2,128)(2,1)} reshape(bf16[1536,8,256]{0,2,1:T(8,128)(2,1)} %convert_bitcast_fusion.2) | data formatting | bytes 12582912 | tf_op jit(solution)/shard_map/reshape | solution.py:16
  195.0 9.5 %copy.59 = bf16[1536,8,16,8,2]{0,2,4,3,1:T(8,128)(2,1)S(1)} copy(bf16[1536,8,16,8,2]{0,4,3,2,1:T(2,128)(2,1)} %reshape.51) | data formatting | bytes 12582912 | tf_op jit(solution)/shard_map/reshape | solution.py:16
  204.5 6.2 copy.60
  210.7 30.8 %all-to-all-done.2 = bf16[1536,16,128]{0,2,1:T(8,128)(2,1)} async-done(((bf16[1536,16,128]{0,2,1:T(8,128)(2,1)}), bf16[1536,16,128]{0,2,1:T(8,128)(2,1)}, u32[]{:S(2)}, u32[]{:S(2)}) %all-to-all-start.2) | async-done | bytes 6291488 | tf_op jit(solution)/shard_map/all_to_all | solution.py:79
  241.5 12.3 %all-to-all-start.1 = ((bf16[1536,16,128]{0,2,1:T(8,128)(2,1)}), bf16[1536,16,128]{0,2,1:T(8,128)(2,1)}, u32[]{:S(2)}, u32[]{:S(2)}) async-start(bf16[1536,16,128]{0,2,1:T(8,128)(2,1)} %copy.60), calls=%async_computation.1 | async-start | bytes 12582912 | tf_op jit(solution)/shard_map/all_to_all | solution.py:56
  253.8 6.3 copy.69
  260.1 6.1 copy.70
  266.2 9.1 %copy.71 = bf16[1536,8,256]{2,0,1:T(8,128)(2,1)} copy(bf16[1536,8,256]{0,1,2:T(8,128)(2,1)} %bitcast.143) | data formatting | bytes 12582912 | tf_op jit(solution)/shard_map/reshape | solution.py:24
  275.3 13.8 %fusion.6 = bf16[1536,8,256]{2,0,1:T(8,128)(2,1)S(1)} fusion(f32[8,1536,256]{2,1,0:T(8,128)} %fusion.11, bf16[1536,8,256]{2,0,1:T(8,128)(2,1)} %copy.71, bf16[1,8,256,256]{3,2,1,0:T(8,128)(2,1)S(1)} %copy-done), kind=kOutput, calls=%fused_computation.8 | convolution fusion | flops 1673527296 | bytes 26214400 | tf_op jit(solution)/shard_map/tco,cno->tcn/dot_general | solution.py:81
  291.7 4.5 convert_bitcast_fusion
  296.2 13.3 %reshape.57 = bf16[1536,8,16,8,2]{0,4,3,2,1:T(2,128)(2,1)} reshape(bf16[1536,8,256]{0,2,1:T(8,128)(2,1)} %convert_bitcast_fusion) | data formatting | bytes 12582912 | tf_op jit(solution)/shard_map/reshape | solution.py:16
  309.5 9.5 %copy.72 = bf16[1536,8,16,8,2]{0,2,4,3,1:T(8,128)(2,1)S(1)} copy(bf16[1536,8,16,8,2]{0,4,3,2,1:T(2,128)(2,1)} %reshape.57) | data formatting | bytes 12582912 | tf_op jit(solution)/shard_map/reshape | solution.py:16
  319.0 6.1 copy.73
  325.1 17.1 %all-to-all-done.1 = bf16[1536,16,128]{0,2,1:T(8,128)(2,1)} async-done(((bf16[1536,16,128]{0,2,1:T(8,128)(2,1)}), bf16[1536,16,128]{0,2,1:T(8,128)(2,1)}, u32[]{:S(2)}, u32[]{:S(2)}) %all-to-all-start.1) | async-done | bytes 6291488 | tf_op jit(solution)/shard_map/all_to_all | solution.py:56
  342.2 11.7 %all-to-all-start.3 = ((bf16[1536,16,128]{0,2,1:T(8,128)(2,1)}), bf16[1536,16,128]{0,2,1:T(8,128)(2,1)}, u32[]{:S(2)}, u32[]{:S(2)}) async-start(bf16[1536,16,128]{0,2,1:T(8,128)(2,1)} %copy.73), calls=%async_computation.3 | async-start | bytes 12582912 | tf_op jit(solution)/shard_map/all_to_all | solution.py:92
  354.4 8.2 %fusion.17 = f32[1,8,256,256]{3,2,1,0:T(8,128)} fusion(bf16[1536,8,256]{2,0,1:T(8,128)(2,1)} %copy-done.4, bf16[1536,8,256]{0,1,2:T(8,128)(2,1)} %bitcast.137), kind=kOutput, calls=%fused_computation.28 | convolution fusion | flops 1610612736 | bytes 14680064 | tf_op jit(solution)/shard_map/tcj,tcn->cjn/dot_general | solution.py:86
  362.6 12.5 %convolution_bitcast_fusion.3 = f32[1,8,256,256]{3,2,1,0:T(8,128)} fusion(bf16[1536,8,256]{2,0,1:T(8,128)(2,1)} %copy.71, f32[8,1536,256]{2,1,0:T(8,128)} %fusion.11), kind=kOutput, calls=%fused_computation.30 | convolution fusion | flops 1638924288 | bytes 20971520 | tf_op jit(solution)/shard_map/tcn,tco->cno/dot_general | solution.py:83
  375.2 6.3 copy.61
  381.4 7.4 %copy.62 = bf16[1536,8,16,8,2]{0,4,3,2,1:T(2,128)(2,1)} copy(bf16[1536,8,16,8,2]{0,2,4,1,3:T(8,128)(2,1)S(1)} %bitcast.145) | data formatting | bytes 12582912 | tf_op jit(solution)/shard_map/transpose | solution.py:24
  388.8 13.6 %reshape_reshape.15 = bf16[1536,2,4,256]{0,3,2,1:T(8,128)(2,1)} reshape(bf16[1536,8,16,8,2]{0,4,3,2,1:T(2,128)(2,1)} %copy.62) | data formatting | bytes 12582912 | tf_op jit(solution)/shard_map/reshape;reshape | solution.py:61
  402.4 40.1 %all-to-all-done.3 = bf16[1536,16,128]{0,2,1:T(8,128)(2,1)} async-done(((bf16[1536,16,128]{0,2,1:T(8,128)(2,1)}), bf16[1536,16,128]{0,2,1:T(8,128)(2,1)}, u32[]{:S(2)}, u32[]{:S(2)}) %all-to-all-start.3) | async-done | bytes 6291488 | tf_op jit(solution)/shard_map/all_to_all | solution.py:92
  442.5 6.3 copy.74
  448.8 7.1 copy.75
  455.9 13.7 %reshape_reshape.17 = bf16[1536,2,4,256]{0,3,2,1:T(8,128)(2,1)} reshape(bf16[1536,8,16,8,2]{0,4,3,2,1:T(2,128)(2,1)} %copy.75) | data formatting | bytes 12582912 | tf_op jit(solution)/shard_map/reshape;reshape | solution.py:97
  469.6 6.0 convolution_bitcast_fusion.4
  475.6 5.9 convolution_bitcast_fusion.2
  482.8 4.6 fusion.15
  489.0 3.6 collective-permute-start
  492.6 6.1 fusion.16
  502.8 22.9 %collective-permute-done = bf16[1,1536,512]{2,1,0:T(8,128)(2,1)S(1)} collective-permute-done((bf16[1,1536,512]{2,1,0:T(8,128)(2,1)}, bf16[1,1536,512]{2,1,0:T(8,128)(2,1)S(1)}, u32[]{:S(2)}, u32[]{:S(2)}) %collective-permute-start) | collective-permute-done | bytes 1572896 | tf_op jit(solution)/shard_map/ppermute | solution.py:10
  525.6 13.1 %collective-permute-done.1 = bf16[1,1536,512]{2,1,0:T(8,128)(2,1)} collective-permute-done((bf16[1,1536,512]{2,1,0:T(8,128)(2,1)}, bf16[1,1536,512]{2,1,0:T(8,128)(2,1)}, u32[]{:S(2)}, u32[]{:S(2)}) %collective-permute-start.1) | collective-permute-done | bytes 1572896 | tf_op jit(solution)/shard_map/ppermute | solution.py:10
  538.7 158.1 %all-reduce.3.cloned.1.call-done = (f32[1,2,4,256,256]{3,4,2,1,0:T(8,128)}, f32[1,8,256,256]{3,2,1,0:T(8,128)}, f32[1,8,256,256]{3,2,1,0:T(8,128)}, f32[1,2,4,256,256]{4,3,2,1,0:T(8,128)}) async-done(((f32[1,2,4,256,256]{3,4,2,1,0:T(8,128)}, f32[1,8,256,256]{3,2,1,0:T(8,128)}, f32[1,8,256,256]{3,2,1,0:T(8,128)}, f32[1,2,4,256,256]{4,3,2,1,0:T(8,128)}), (f32[1,2,4,256,256]{3,4,2,1,0:T(8,128)}, ...) | async-done | bytes 8388624 | tf_op jit(solution)/shard_map/psum | solution.py:109
  696.8 3.0 copy.83
  (40 shorter events, 24.3 us)
Async XLA Ops:
  7.2 165.0 %copy-start = (bf16[1,8,256,256]{3,2,1,0:T(8,128)(2,1)S(1)}, bf16[1,8,256,256]{3,2,1,0:T(8,128)(2,1)}, u32[]{:S(2)}) copy-start(bf16[1,8,256,256]{3,2,1,0:T(8,128)(2,1)} %param.10) | copy-start | bytes 3145732
  9.6 19.8 %copy-start.5 = (bf16[1536,2,256]{2,1,0:T(2,128)(2,1)}, bf16[1536,2,256]{2,1,0:T(2,128)(2,1)S(1)}, u32[]{:S(2)}) copy-start(bf16[1536,2,256]{2,1,0:T(2,128)(2,1)S(1)} %reshape_squeeze.6) | copy-start | bytes 4718596
  45.1 96.0 %all-to-all-start = ((bf16[1536,16,128]{0,2,1:T(8,128)(2,1)}), bf16[1536,16,128]{0,2,1:T(8,128)(2,1)}, u32[]{:S(2)}, u32[]{:S(2)}) async-start(bf16[1536,16,128]{0,2,1:T(8,128)(2,1)} %copy.54), calls=%async_computation | async-start | bytes 12582912 | tf_op jit(solution)/shard_map/all_to_all | solution.py:46
  55.0 19.4 %copy-start.7 = (bf16[1536,2,256]{2,1,0:T(2,128)(2,1)}, bf16[1536,2,256]{2,1,0:T(2,128)(2,1)S(1)}, u32[]{:S(2)}) copy-start(bf16[1536,2,256]{2,1,0:T(2,128)(2,1)S(1)} %reshape_squeeze.7) | copy-start | bytes 4718596
  141.0 100.5 %all-to-all-start.2 = ((bf16[1536,16,128]{0,2,1:T(8,128)(2,1)}), bf16[1536,16,128]{0,2,1:T(8,128)(2,1)}, u32[]{:S(2)}, u32[]{:S(2)}) async-start(bf16[1536,16,128]{0,2,1:T(8,128)(2,1)} %copy.68), calls=%async_computation.2 | async-start | bytes 12582912 | tf_op jit(solution)/shard_map/all_to_all | solution.py:79
  159.3 3.5 copy-start.3
  162.8 9.3 %copy-start.2 = (bf16[1536,8,16,8,2]{0,1,4,3,2:T(8,128)(2,1)}, bf16[1536,8,16,8,2]{0,1,4,3,2:T(8,128)(2,1)S(1)}, u32[]{:S(2)}) copy-start(bf16[1536,8,16,8,2]{0,1,4,3,2:T(8,128)(2,1)S(1)} %copy.56) | copy-start | bytes 18874372
  241.5 100.7 %all-to-all-start.1 = ((bf16[1536,16,128]{0,2,1:T(8,128)(2,1)}), bf16[1536,16,128]{0,2,1:T(8,128)(2,1)}, u32[]{:S(2)}, u32[]{:S(2)}) async-start(bf16[1536,16,128]{0,2,1:T(8,128)(2,1)} %copy.60), calls=%async_computation.1 | async-start | bytes 12582912 | tf_op jit(solution)/shard_map/all_to_all | solution.py:56
  289.1 2.6 copy-start.4
  342.2 100.3 %all-to-all-start.3 = ((bf16[1536,16,128]{0,2,1:T(8,128)(2,1)}), bf16[1536,16,128]{0,2,1:T(8,128)(2,1)}, u32[]{:S(2)}, u32[]{:S(2)}) async-start(bf16[1536,16,128]{0,2,1:T(8,128)(2,1)} %copy.73), calls=%async_computation.3 | async-start | bytes 12582912 | tf_op jit(solution)/shard_map/all_to_all | solution.py:92
  354.0 342.9 %all-reduce.3.cloned.1.call-start = ((), (), s32[]{:S(2)}) async-start(), calls=%async_computation.4 | async-start | bytes 16777216 | tf_op jit(solution)/shard_map/psum | solution.py:109
  455.9 13.7 %copy-start.6 = (bf16[1536,2,256]{2,1,0:T(2,128)(2,1)S(1)}, bf16[1536,2,256]{2,1,0:T(2,128)(2,1)}, u32[]{:S(2)}) copy-start(bf16[1536,2,256]{2,1,0:T(2,128)(2,1)} %copy-done.5) | copy-start | bytes 4718596
  469.6 6.0 copy-start.8
  481.5 1.2 copy-start.13
  489.0 36.7 %collective-permute-start = (bf16[1,1536,512]{2,1,0:T(8,128)(2,1)}, bf16[1,1536,512]{2,1,0:T(8,128)(2,1)S(1)}, u32[]{:S(2)}, u32[]{:S(2)}) collective-permute-start(bf16[1,1536,512]{2,1,0:T(8,128)(2,1)} %copy.65), channel_id=1, source_target_pairs={{0,16},{16,32},{32,48},{1,17},{17,33},{33,49},{2,18},{18,34},{34,5... | collective-permute-start | bytes 4718600 | tf_op jit(solution)/shard_map/ppermute | solution.py:10
  501.5 37.3 %collective-permute-start.1 = (bf16[1,1536,512]{2,1,0:T(8,128)(2,1)}, bf16[1,1536,512]{2,1,0:T(8,128)(2,1)}, u32[]{:S(2)}, u32[]{:S(2)}) collective-permute-start(bf16[1,1536,512]{2,1,0:T(8,128)(2,1)} %copy.77), channel_id=1, source_target_pairs={{16,0},{32,16},{48,32},{17,1},{33,17},{49,33},{18,2},{34,18},{50,3... | collective-permute-start | bytes 4718600 | tf_op jit(solution)/shard_map/ppermute | solution.py:10
  525.6 13.1 %copy-start.12 = (bf16[1,1536,512]{2,1,0:T(8,128)(2,1)}, bf16[1,1536,512]{2,1,0:T(8,128)(2,1)S(1)}, u32[]{:S(2)}) copy-start(bf16[1,1536,512]{2,1,0:T(8,128)(2,1)S(1)} %collective-permute-done) | copy-start | bytes 4718596
  696.8 8.6 %copy-start.11 = (f32[1,8,256,256]{3,2,1,0:T(8,128)S(1)}, f32[1,8,256,256]{3,2,1,0:T(8,128)}, u32[]{:S(2)}) copy-start(f32[1,8,256,256]{3,2,1,0:T(8,128)} %get-tuple-element.37) | copy-start | bytes 6291460
  699.9 6.9 copy-start.10
  702.7 5.5 copy-start.9
  702.7 6.8 copy-start.1
Sparse Core Ops, SparseCore 0:
  481.7 215.1 all-reduce.2
where the time goes:
time: 723 us; the launch traced here: 716 us
  waiting for transfers between devices  333 us (46%)
  local copies, waits for them, and re-layouts  227 us (31%)
  matrix products  93.4 us (13%)
  starting transfers between devices  48.9 us (7%)
  between operations  14.4 us (2%)
    psum x1, waiting for transfers between devices, shards(): lax.psum((grad_one, grad_two, grad_three, grad_four), 'dp')  158 us
    all_to_all x4, waiting for transfers between devices, shards(): lax.all_to_all(outbound, 'tensor', split_axis=1, concat_axis=1, tiled=True)  139 us
    reshape x4, local copies, waits for them, and re-layouts, to_peers(): shaped = blocks.reshape(rows, local, parts, local, inner)  45.4 us
    another operation x4, local copies, waits for them, and re-layouts, to_peers(): shaped = blocks.reshape(rows, local, parts, local, inner)  45.4 us
    all_to_all x4, starting transfers between devices, shards(): lax.all_to_all(outbound, 'tensor', split_axis=1, concat_axis=1, tiled=True)  43.6 us
    ppermute x2, waiting for transfers between devices, shifted(): lax.ppermute(value, axis, [(source, source + steps) for source in range(l...  36 us
    all_to_all x4, local copies, waits for them, and re-layouts, shards(): lax.all_to_all(outbound, 'tensor', split_axis=1, concat_axis=1, tiled=True)  25 us
    reshape x4, local copies, waits for them, and re-layouts, to_peers(): shaped.transpose(0, 2, 1, 3, 4).reshape(rows, parts, local * local * inner)  24.6 us
  transfers between devices with their start and end apart: 7, of which 7 were waited for; matrix products, arithmetic and copies ran while one was open for 32% of the time, Pallas kernels for 0%

commit v1 on v0

v1 whole, which is shorter than its diff:
```python
import functools
import math

import jax
import jax.numpy as jnp
from jax import lax
from jax.experimental import pallas as pl
from jax.experimental.pallas import tpu as pltpu
from jax.sharding import Mesh, PartitionSpec as P

BF = jnp.bfloat16
F32 = jnp.float32
GELU_A = math.sqrt(2.0 / math.pi)
GELU_B = 0.044715
YC = ("y", "core")


def params(mib):
    return pltpu.CompilerParams(vmem_limit_bytes=mib * 1024 * 1024)


def cost(flops, nbytes, trans=0):
    return pl.CostEstimate(flops=int(flops), bytes_accessed=int(nbytes), transcendentals=int(trans))


def mm(a, b, dims):
    return lax.dot_general(a, b, (dims, ((), ())), preferred_element_type=F32)


def one_hot(shape, row_dim, group, k, sub):
    row = lax.broadcasted_iota(jnp.int32, shape, row_dim)
    col = lax.broadcasted_iota(jnp.int32, shape, 1 - row_dim)
    per = sub // 2
    first = group * per + k * 2
    inside = row % sub
    hit = ((row // sub) == (col // 2)) & (inside == first + col % 2)
    return jnp.where(hit, 1.0, 0.0).astype(BF)


def lift_body(swap, side_ref, x_ref, f_ref, out_ref, a_ref):
    groups, expand = f_ref.shape[0], f_ref.shape[1]
    rows, width = a_ref.shape
    wide = width // groups
    sub = groups * expand * 2
    cols = 2 * rows // sub

    @pl.when(pl.program_id(0) == 0)
    def _():
        for g in range(groups):
            total = jnp.zeros((rows, wide), F32)
            for k in range(expand):
                pick = one_hot((rows, cols), 0, g, k, sub)
                total += mm(pick, f_ref[g, k], ((1,), (1,)) if swap else ((1,), (0,)))
            a_ref[:, g * wide : (g + 1) * wide] = total.astype(BF)

    value = mm(a_ref[...], x_ref[...], ((1,), (1,))).astype(BF)
    out_ref[...] = value.reshape(out_ref.shape)


def lift(x, factor, side, peers, swap, tile):
    tokens, width = x.shape
    groups, expand, bsize = factor.shape[0], factor.shape[1], factor.shape[2 if swap else 3]
    local = groups * expand
    rows = peers * local * local * 2
    cols = peers * local * 2
    if swap:
        block, where = (groups, expand, bsize, cols), lambda i, s: (0, 0, 0, s[0])
    else:
        block, where = (groups, expand, cols, bsize), lambda i, s: (0, 0, s[0], 0)
    return pl.pallas_call(
        functools.partial(lift_body, swap),
        grid_spec=pltpu.PrefetchScalarGridSpec(
            num_scalar_prefetch=1,
            grid=(tokens // tile,),
            in_specs=[
                pl.BlockSpec((tile, width), lambda i, s: (i, 0)),
                pl.BlockSpec(block, where),
            ],
            out_specs=[
                pl.BlockSpec((peers, rows // peers, tile), lambda i, s: (0, 0, i)),
                pl.BlockSpec((rows, width), lambda i, s: (0, 0)),
            ],
        ),
        out_shape=[
            jax.ShapeDtypeStruct((peers, rows // peers, tokens), BF),
            jax.ShapeDtypeStruct((rows, width), BF),
        ],
        compiler_params=params(40),
        cost_estimate=cost(4 * rows * width * tokens, 2 * tokens * (width + rows)),
        name="lift",
    )(side, x, factor)


def gather_rows(scratch, side, own, peer):
    half = scratch.shape[0] // 2
    mine = pl.multiple_of(side * half, half)
    theirs = pl.multiple_of((1 - side) * half, half)
    scratch[pl.ds(mine, half), :] = own[...].reshape(half, scratch.shape[1])
    scratch[pl.ds(theirs, half), :] = peer[...].reshape(half, scratch.shape[1])


def split_rows(scratch, side, own, peer):
    half = scratch.shape[0] // 2
    mine = pl.multiple_of(side * half, half)
    theirs = pl.multiple_of((1 - side) * half, half)
    own[...] = scratch[pl.ds(mine, half), :].reshape(own.shape)
    peer[...] = scratch[pl.ds(theirs, half), :].reshape(peer.shape)


def forward_body(side_ref, ro_ref, rp_ref, w2_ref, w3_ref, no_ref, np_ref, mixed, narrow):
    side = side_ref[0]
    gather_rows(mixed, side, ro_ref, rp_ref)
    pre = mm(w2_ref[0], mixed[...], ((0,), (0,)))
    act = (0.5 * pre * (1.0 + jnp.tanh(GELU_A * (pre + GELU_B * (pre * pre * pre))))).astype(BF)
    narrow[...] = mm(w3_ref[0], act, ((0,), (0,))).astype(BF)
    split_rows(narrow, side, no_ref, np_ref)


def middle_specs(peers, local, sub, bsize, tile):
    piece = pl.BlockSpec((peers, 1, sub, tile), lambda c, i, s: (0, c, 0, i))
    weight = pl.BlockSpec((1, bsize, bsize), lambda c, i, s: (c, 0, 0))
    return piece, weight


def forward(side, own, peer, second, third, tile):
    peers, local, sub, tokens = own.shape
    bsize = second.shape[1]
    piece, weight = middle_specs(peers, local, sub, bsize, tile)
    shape = jax.ShapeDtypeStruct(own.shape, BF)
    return pl.pallas_call(
        forward_body,
        grid_spec=pltpu.PrefetchScalarGridSpec(
            num_scalar_prefetch=1,
            grid=(local, tokens // tile),
            in_specs=[piece, piece, weight, weight],
            out_specs=[piece, piece],
            scratch_shapes=[pltpu.VMEM((bsize, tile), BF), pltpu.VMEM((bsize, tile), BF)],
        ),
        out_shape=[shape, shape],
        compiler_params=params(32),
        cost_estimate=cost(
            4 * local * bsize * bsize * tokens, 4 * local * bsize * tokens, local * bsize * tokens
        ),
        name="forward",
    )(side, own, peer, second, third)


def backward_body(
    side_ref, ro_ref, rp_ref, go_ref, gp_ref, w2_ref, w3_ref,
    mo_ref, mp_ref, g2_ref, g3_ref, mixed, gnar, gmix, acc2, acc3,
):
    side = side_ref[0]
    step = pl.program_id(1)
    gather_rows(mixed, side, ro_ref, rp_ref)
    gather_rows(gnar, side, go_ref, gp_ref)
    pre = mm(w2_ref[0], mixed[...], ((0,), (0,)))
    square = pre * pre
    th = jnp.tanh(GELU_A * (pre + GELU_B * (square * pre)))
    half = 0.5 * (1.0 + th)
    act = (pre * half).astype(BF)
    slope = half + (0.5 * GELU_A) * pre * (1.0 - th * th) * (1.0 + (3.0 * GELU_B) * square)
    grad_act = mm(w3_ref[0], gnar[...], ((1,), (0,)))
    grad_pre = (grad_act * slope).astype(BF)
    gmix[...] = mm(w2_ref[0], grad_pre, ((1,), (0,))).astype(BF)
    split_rows(gmix, side, mo_ref, mp_ref)
    add3 = mm(act, gnar[...], ((1,), (1,)))
    add2 = mm(mixed[...], grad_pre, ((1,), (1,)))

    @pl.when(step == 0)
    def _():
        acc2[...] = add2
        acc3[...] = add3

    @pl.when(step > 0)
    def _():
        acc2[...] += add2
        acc3[...] += add3

    @pl.when(step == pl.num_programs(1) - 1)
    def _():
        g2_ref[0] = acc2[...].astype(BF)
        g3_ref[0] = acc3[...].astype(BF)


def backward(side, own, peer, grad_own, grad_peer, second, third, tile):
    peers, local, sub, tokens = own.shape
    bsize = second.shape[1]
    piece, weight = middle_specs(peers, local, sub, bsize, tile)
    shape = jax.ShapeDtypeStruct(own.shape, BF)
    grads = jax.ShapeDtypeStruct(second.shape, BF)
    return pl.pallas_call(
        backward_body,
        grid_spec=pltpu.PrefetchScalarGridSpec(
            num_scalar_prefetch=1,
            grid=(local, tokens // tile),
            in_specs=[piece] * 4 + [weight] * 2,
            out_specs=[piece, piece, weight, weight],
            scratch_shapes=[pltpu.VMEM((bsize, tile), BF)] * 3
            + [pltpu.VMEM((bsize, bsize), F32)] * 2,
        ),
        out_shape=[shape, shape, grads, grads],
        compiler_params=params(40),
        cost_estimate=cost(
            10 * local * bsize * bsize * tokens, 6 * local * bsize * tokens, local * bsize * tokens
        ),
        name="backward",
    )(side, own, peer, grad_own, grad_peer, second, third)


def drop_body(swap, add, groups, expand, s_ref, a_ref, x_ref, *rest):
    if add:
        prev_ref, out_ref, g_ref, flip, acc = rest
    else:
        out_ref, g_ref, flip, acc = rest
    step = pl.program_id(0)
    rows, width = a_ref.shape
    wide = width // groups
    sub = groups * expand * 2
    cols = 2 * rows // sub

    @pl.when(step == 0)
    def _():
        flip[...] = a_ref[...].T

    value = mm(flip[...], s_ref[...], ((1,), (0,))).T
    if add:
        value = value + prev_ref[...].astype(F32)
    out_ref[...] = value.astype(BF)
    more = mm(s_ref[...], x_ref[...], ((1,), (0,)))

    @pl.when(step == 0)
    def _():
        acc[...] = more

    @pl.when(step > 0)
    def _():
        acc[...] += more

    @pl.when(step == pl.num_programs(0) - 1)
    def _():
        for g in range(groups):
            part = acc[:, g * wide : (g + 1) * wide].astype(BF)
            if swap:
                part = part.T
            for k in range(expand):
                if swap:
                    got = mm(part, one_hot((rows, cols), 0, g, k, sub), ((1,), (0,)))
                else:
                    got = mm(one_hot((cols, rows), 1, g, k, sub), part, ((1,), (0,)))
                g_ref[g, k] = got.astype(BF)


def drop(s, a, x, prev, groups, expand, swap, tile):
    rows, width = a.shape
    tokens = x.shape[0]
    bsize = width // groups
    cols = rows // (groups * expand)
    grads = (groups, expand, bsize, cols) if swap else (groups, expand, cols, bsize)
    add = prev is not None
    wide = pl.BlockSpec((tile, width), lambda i: (i, 0))
    args = (s, a, x) + ((prev,) if add else ())
    return pl.pallas_call(
        functools.partial(drop_body, swap, add, groups, expand),
        grid=(tokens // tile,),
        in_specs=[
            pl.BlockSpec((rows, tile), lambda i: (0, i)),
            pl.BlockSpec((rows, width), lambda i: (0, 0)),
            wide,
        ]
        + ([wide] if add else []),
        out_specs=[wide, pl.BlockSpec(grads, lambda i: (0, 0, 0, 0))],
        scratch_shapes=[pltpu.VMEM((width, rows), BF), pltpu.VMEM((rows, width), F32)],
        out_shape=[
            jax.ShapeDtypeStruct((tokens, width), BF),
            jax.ShapeDtypeStruct(grads, BF),
        ],
        compiler_params=params(40),
        cost_estimate=cost(4 * rows * width * tokens, 2 * tokens * (rows + 3 * width)),
        name="drop",
    )(*args)


def swapped(value, axes):
    count = lax.axis_size(axes)
    return lax.ppermute(value, axes, [(i, count - 1 - i) for i in range(count)])


def shifted(value, axis, steps):
    count = lax.axis_size(axis)
    leading, last = (max(0, -steps), min(count, count - steps))
    return lax.ppermute(value, axis, [(source, source + steps) for source in range(leading, last)])


def spread_out(value):
    return lax.all_to_all(value, YC, split_axis=0, concat_axis=0, tiled=True)


def halves(value, dim):
    size = value.shape[dim] // 2
    return lax.slice_in_dim(value, 0, size, axis=dim), lax.slice_in_dim(value, size, 2 * size, axis=dim)


def paired(own, peer, axis_dim, is_low):
    mine = own.astype(F32) + swapped(own, "dp").astype(F32)
    theirs = swapped(peer, "xlo").astype(F32) + swapped(peer, ("dp", "xlo")).astype(F32)
    low = jnp.where(is_low, mine, theirs)
    high = jnp.where(is_low, theirs, mine)
    return jnp.concatenate([low, high], axis=axis_dim)


def shards(inputs, upstream, factor_one, factor_two, factor_three, factor_four):
    x, u = inputs[0], upstream[0]
    first, second, third, fourth = factor_one[0], factor_two[0], factor_three[0], factor_four[0]
    groups, expand, bsize = first.shape[0], first.shape[1], first.shape[2]
    local = groups * expand
    tokens = x.shape[0]
    peers = lax.axis_size("y") * lax.axis_size("core")
    place = lax.axis_index("xlo")
    is_low = place == 0
    side = place.astype(jnp.int32).reshape(1)
    zero = jnp.zeros((1,), jnp.int32)
    tile = 512 if tokens % 512 == 0 else tokens

    low, high = halves(first, 3)
    first_peer = swapped(jnp.where(is_low, high, low), "xlo")
    low, high = halves(fourth, 2)
    fourth_peer = swapped(jnp.where(is_low, high, low), "xlo")
    x_peer = swapped(x, "xlo")
    u_peer = swapped(u, "xlo")

    l1o, a1o = lift(x, first, side, peers, True, tile)
    l2o, a4o = lift(u, fourth, side, peers, False, tile)
    l1p, a1p = lift(x_peer, first_peer, zero, peers, True, tile)
    l2p, a4p = lift(u_peer, fourth_peer, zero, peers, False, tile)

    def inner(value):
        return spread_out(value).reshape(peers, local, 2 * local, tokens)

    def outer(value):
        return spread_out(value.reshape(peers, 2 * local * local, tokens)).reshape(-1, tokens)

    y1o = inner(l1o)
    y2o = inner(l2o)
    y1p = inner(l1p)
    y2p = inner(l2p)
    no, np_ = forward(side, y1o, y1p, second, third, tile)
    y3p = outer(np_)
    y3o = outer(no)
    mo, mp, g2, g3 = backward(side, y1o, y1p, y2o, y2p, second, third, tile)
    y4p = outer(mp)
    y4o = outer(mo)

    out_p, g4p = drop(y3p, a4p, u_peer, None, groups, expand, False, tile)
    out_o, g4o = drop(y3o, a4o, u, swapped(out_p, "xlo"), groups, expand, False, tile)
    y_next = shifted(out_o, "pipe", 1)
    in_p, g1p = drop(y4p, a1p, x_peer, None, groups, expand, True, tile)
    in_o, g1o = drop(y4o, a1o, x, swapped(in_p, "xlo"), groups, expand, True, tile)
    dx_prev = shifted(in_o, "pipe", -1)

    grad_two = g2.astype(F32) + swapped(g2, "dp").astype(F32)
    grad_three = g3.astype(F32) + swapped(g3, "dp").astype(F32)
    grad_four = paired(g4o, g4p, 2, is_low)
    grad_one = paired(g1o, g1p, 3, is_low)
    return (
        y_next[None], dx_prev[None], grad_one[None], grad_two[None], grad_three[None], grad_four[None],
    )


def solution(mesh):
    parts = mesh.shape["tensor"]
    devices = mesh.devices.reshape(mesh.shape["dp"], mesh.shape["pipe"], 2, parts // 4, 2)
    fine = Mesh(devices, ("dp", "pipe", "xlo", "y", "core"))
    wide = ("xlo", "y", "core")
    acts = P("pipe", "dp", wide)
    five = P("pipe", wide, None, None, None)
    four = P("pipe", wide, None, None)
    return jax.shard_map(
        shards,
        mesh=fine,
        in_specs=(acts, acts, five, four, four, five),
        out_specs=(acts, acts, five, four, four, five),
        check_vma=False,
    )
```

time: 723 us -> 556 us (0.77)
  local copies, waits for them, and re-layouts: 227 us -> 38.2 us
  blocking collectives: 0 us -> 129 us
  matrix products: 93.4 us -> 0 us
  waiting for transfers between devices: 333 us -> 240 us
  Pallas kernels: 0 us -> 85.2 us
  other arithmetic: 0 us -> 13.8 us
  between operations: 14.4 us -> 0.86 us
    ppermute x0 -> x14, waiting for transfers between devices: none -> 197 us  [swapped(): return lax.ppermute(value, axes, [(i, count - 1 - i) for i in range(count)])]
    psum x1 -> x0, waiting for transfers between devices: 158 us -> none  [shards(): lax.psum((grad_one, grad_two, grad_three, grad_four), 'dp')]
    all_to_all x0 -> x3, blocking collectives: none -> 129 us  [spread_out(): return lax.all_to_all(value, YC, split_axis=0, concat_axis=0, tiled=True)]
    all_to_all x4 -> x5, waiting for transfers between devices: 139 us -> 43.4 us  [spread_out(): return lax.all_to_all(value, YC, split_axis=0, concat_axis=0, tiled=True)]
    dot_general x12 -> x0, matrix products: 93.4 us -> none  [the longest x1 13.8 us: shards(): jnp.einsum('tco,cno->tcn', grad_narrow, third, preferred_element_type=jnp...]
    pallas_call x0 -> x10, Pallas kernels: none -> 85.2 us  [the longest x4 27.4 us: drop(): pl.pallas_call(functools.partial(drop_body, swap, add, groups, expand), g...]
    another operation x10 -> x0, local copies, waits for them, and re-layouts: 81.9 us -> none  [the longest x4 45.4 us: to_peers(): shaped = blocks.reshape(rows, local, parts, local, inner)]
    reshape x9 -> x0, local copies, waits for them, and re-layouts: 79.1 us -> none  [the longest x4 45.4 us: to_peers(): shaped = blocks.reshape(rows, local, parts, local, inner)]
  transfers between devices with their start and end apart: 7 -> 21, of which waited for: 7 -> 12; matrix products, arithmetic and copies ran while one was open for 32% -> 2% of each run, Pallas kernels for 0% -> 10%
where the time goes in v1:
time: 556 us; the launch traced here: 555 us
  waiting for transfers between devices  240 us (43%)
  blocking collectives  129 us (23%)
  Pallas kernels  85.2 us (15%)
  starting transfers between devices  47.6 us (9%)
  local copies, waits for them, and re-layouts  38.2 us (7%)
  other arithmetic  13.8 us (2%)
    ppermute x14, waiting for transfers between devices, swapped(): return lax.ppermute(value, axes, [(i, count - 1 - i) for i in range(count)])  197 us
    all_to_all x3, blocking collectives, spread_out(): return lax.all_to_all(value, YC, split_axis=0, concat_axis=0, tiled=True)  129 us
    all_to_all x5, waiting for transfers between devices, spread_out(): return lax.all_to_all(value, YC, split_axis=0, concat_axis=0, tiled=True)  43.4 us
    unnamed x76, local copies, waits for them, and re-layouts  38.2 us
    pallas_call x4, Pallas kernels, drop(): pl.pallas_call(functools.partial(drop_body, swap, add, groups, expand), g...  27.4 us
    all_to_all x5, starting transfers between devices, spread_out(): return lax.all_to_all(value, YC, split_axis=0, concat_axis=0, tiled=True)  26.6 us
    pallas_call x1, Pallas kernels, backward(): pl.pallas_call(backward_body, grid_spec=pltpu.PrefetchScalarGridSpec(num_...  26.6 us
    pallas_call x4, Pallas kernels, lift(): pl.pallas_call(functools.partial(lift_body, swap), grid_spec=pltpu.Prefet...  16.1 us
  transfers between devices with their start and end apart: 21, of which 12 were waited for; matrix products, arithmetic and copies ran while one was open for 2% of the time, Pallas kernels for 10%

profile of v1, /device:TPU:1, one launch (start us, length us, event | category | flops | bytes accessed | tf_op | source)
XLA Modules:
  0.0 554.7 jit_solution(12015524333823445676)
XLA Ops:
  3.3 3.8 lift.4
  7.1 1.6 copy-done.9
  9.7 6.0 %all-to-all-start = ((bf16[8,128,1536]{2,1,0:T(8,128)(2,1)}), bf16[8,128,1536]{2,1,0:T(8,128)(2,1)S(1)}, u32[]{:S(2)}, u32[]{:S(2)}) async-start(bf16[8,128,1536]{2,1,0:T(8,128)(2,1)} %copy-done.9), calls=%async_computation | async-start | bytes 6291456 | tf_op jit(solution)/shard_map/all_to_all | solution.py:295
  18.3 3.7 lift.6
  22.0 1.6 copy-done.1
  24.6 28.6 %all-to-all-done = bf16[8,128,1536]{2,1,0:T(8,128)(2,1)S(1)} async-done(((bf16[8,128,1536]{2,1,0:T(8,128)(2,1)}), bf16[8,128,1536]{2,1,0:T(8,128)(2,1)S(1)}, u32[]{:S(2)}, u32[]{:S(2)}) %all-to-all-start) | async-done | bytes 3145760 | tf_op jit(solution)/shard_map/all_to_all | solution.py:295
  53.2 5.2 all-to-all-start.4
  61.2 44.4 %collective-permute-done.3.f_ref = bf16[2,4,128,256]{3,2,1,0:T(8,128)(2,1)S(1)} collective-permute-done((bf16[2,4,128,256]{3,2,1,0:T(8,128)(2,1)S(1)}, bf16[2,4,128,256]{3,2,1,0:T(8,128)(2,1)S(1)}, u32[]{:S(2)}, u32[]{:S(2)}) %collective-permute-start.3) | collective-permute-done | bytes 524320 | tf_op jit(solution)/shard_map/ppermute | solution.py:285
  105.7 4.9 lift.7
  110.6 1.7 copy-done.2
  113.3 5.5 all-to-all-start.5
  121.6 44.6 %collective-permute-done.1.f_ref = bf16[2,4,256,128]{3,2,1,0:T(8,128)(2,1)S(1)} collective-permute-done((bf16[2,4,256,128]{3,2,1,0:T(8,128)(2,1)S(1)}, bf16[2,4,256,128]{3,2,1,0:T(8,128)(2,1)S(1)}, u32[]{:S(2)}, u32[]{:S(2)}) %collective-permute-start.1) | collective-permute-done | bytes 524320 | tf_op jit(solution)/shard_map/ppermute | solution.py:285
  166.2 3.7 lift.5
  169.9 1.6 copy-done.10
  173.7 43.4 %all_to_all.40 = bf16[8,128,1536]{2,1,0:T(8,128)(2,1)} all-to-all(bf16[8,128,1536]{2,1,0:T(8,128)(2,1)} %copy-done.10), channel_id=1, replica_groups=mesh['dp'=2,'pipe'=4,'xlo'=2,'y'=4,'core'=2] {'y','core'}, dimensions={0} | all-to-all | bytes 6291456 | tf_op jit(solution)/shard_map/all_to_all | solution.py:295
  217.1 26.6 %backward.1 = (bf16[8,8,16,1536]{3,2,1,0:T(8,128)(2,1)}, bf16[8,8,16,1536]{3,2,1,0:T(8,128)(2,1)S(1)}, bf16[8,256,256]{2,1,0:T(8,128)(2,1)}, bf16[8,256,256]{2,1,0:T(8,128)(2,1)}) custom-call(s32[1]{0:T(128)} %bitcast.side_ref, bf16[8,8,16,1536]{3,2,1,0:T(8,128)(2,1)S(1)} %bitcast.29, bf16[8,8,16,1536]{3,2,1,0:T(8,128)(2,1)} %bitcast.33, ...), custom_call_target="tpu_custom_call" | custom-call | flops 8053063680 | bytes 18874368 | tf_op jit(solution)/shard_map/backward/pallas_call | solution.py:191
  243.7 1.7 copy-done.4
  245.4 5.4 all-to-all-start.7
  250.8 1.9 copy-done.3
  255.1 15.2 %forward.1 = (bf16[8,8,16,1536]{3,2,1,0:T(8,128)(2,1)S(1)}, bf16[8,8,16,1536]{3,2,1,0:T(8,128)(2,1)S(1)}) custom-call(s32[1]{0:T(128)} %bitcast.side_ref, bf16[8,8,16,1536]{3,2,1,0:T(8,128)(2,1)S(1)} %bitcast.30, bf16[8,8,16,1536]{3,2,1,0:T(8,128)(2,1)S(1)} %bitcast.34, bf16[8,256,256]{2,1,0:T(8,128)(2,1)S(1)} %bitcast.50, bf16[8,256,256]{2,1,0:T(8,128)(2,1)S(1)} %bitcast.52), custom_call_target="tpu_custom_call" | custom-call | flops 3221225472 | bytes 12582912 | tf_op jit(solution)/shard_map/forward/pallas_call | solution.py:130
  270.3 1.7 copy-done.6
  272.1 1.6 copy-done.8
  273.7 14.8 %all-to-all-done.7 = bf16[8,128,1536]{2,1,0:T(8,128)(2,1)} async-done(((bf16[8,128,1536]{2,1,0:T(8,128)(2,1)}), bf16[8,128,1536]{2,1,0:T(8,128)(2,1)}, u32[]{:S(2)}, u32[]{:S(2)}) %all-to-all-start.7) | async-done | bytes 3145760 | tf_op jit(solution)/shard_map/all_to_all | solution.py:295
  288.5 43.4 %all_to_all.41 = bf16[8,128,1536]{2,1,0:T(8,128)(2,1)} all-to-all(bf16[8,128,1536]{2,1,0:T(8,128)(2,1)} %bitcast.38), channel_id=1, replica_groups=mesh['dp'=2,'pipe'=4,'xlo'=2,'y'=4,'core'=2] {'y','core'}, dimensions={0} | all-to-all | bytes 6291456 | tf_op jit(solution)/shard_map/all_to_all | solution.py:295
  331.9 42.1 %all_to_all.42 = bf16[8,128,1536]{2,1,0:T(8,128)(2,1)} all-to-all(bf16[8,128,1536]{2,1,0:T(8,128)(2,1)S(1)} %bitcast.37), channel_id=1, replica_groups=mesh['dp'=2,'pipe'=4,'xlo'=2,'y'=4,'core'=2] {'y','core'}, dimensions={0} | all-to-all | bytes 6291456 | tf_op jit(solution)/shard_map/all_to_all | solution.py:295
  374.0 4.6 all-to-all-start.6
  378.6 1.9 copy-done.5
  381.7 7.5 %drop.4 = (bf16[1536,512]{1,0:T(8,128)(2,1)S(1)}, bf16[2,4,128,256]{3,2,1,0:T(8,128)(2,1)}) custom-call(bf16[1024,1536]{1,0:T(8,128)(2,1)S(1)} %bitcast.36, bf16[1024,512]{1,0:T(8,128)(2,1)S(1)} %copy-done.34, bf16[1536,512]{1,0:T(8,128)(2,1)} %collective-permute-done.2.x_ref), custom_call_target="tpu_custom_call" | custom-call | flops 3221225472 | bytes 7864320 | tf_op jit(solution)/shard_map/drop/pallas_call | solution.py:262
  390.4 7.3 %drop.6 = (bf16[1536,512]{1,0:T(8,128)(2,1)S(1)}, bf16[2,4,256,128]{3,2,1,0:T(8,128)(2,1)S(1)}) custom-call(bf16[1024,1536]{1,0:T(8,128)(2,1)} %bitcast.19.s_ref, bf16[1024,512]{1,0:T(8,128)(2,1)S(1)} %copy-done.36, bf16[1536,512]{1,0:T(8,128)(2,1)S(1)} %copy-done.20), custom_call_target="tpu_custom_call" | custom-call | flops 3221225472 | bytes 7864320 | tf_op jit(solution)/shard_map/drop/pallas_call | solution.py:262
  398.1 2.7 collective-permute-start.11
  401.1 2.5 collective-permute-start.15
  403.6 21.3 %collective-permute-done.4.rest_0_ = bf16[1536,512]{1,0:T(8,128)(2,1)S(1)} collective-permute-done((bf16[1536,512]{1,0:T(8,128)(2,1)S(1)}, bf16[1536,512]{1,0:T(8,128)(2,1)S(1)}, u32[]{:S(2)}, u32[]{:S(2)}) %collective-permute-start.4) | collective-permute-done | bytes 1572896 | tf_op jit(solution)/shard_map/ppermute | solution.py:285
  426.1 6.4 %drop.5 = (bf16[1536,512]{1,0:T(8,128)(2,1)S(1)}, bf16[2,4,128,256]{3,2,1,0:T(8,128)(2,1)}) custom-call(bf16[1024,1536]{1,0:T(8,128)(2,1)S(1)} %bitcast.32, bf16[1024,512]{1,0:T(8,128)(2,1)S(1)} %copy-done.32, bf16[1536,512]{1,0:T(8,128)(2,1)S(1)} %bitcast.45, bf16[1536,512]{1,0:T(8,128)(2,1)S(1)} %collective-permute-done.4.rest_0_), custom_call_target="tpu_custom_call" | custom-call | flops 3221225472 | bytes 7864320 | tf_op jit(solution)/shard_map/drop/pallas_call | solution.py:262
  433.7 24.9 %collective-permute-done.6.rest_0_ = bf16[1536,512]{1,0:T(8,128)(2,1)S(1)} collective-permute-done((bf16[1536,512]{1,0:T(8,128)(2,1)S(1)}, bf16[1536,512]{1,0:T(8,128)(2,1)S(1)}, u32[]{:S(2)}, u32[]{:S(2)}) %collective-permute-start.6) | collective-permute-done | bytes 1572896 | tf_op jit(solution)/shard_map/ppermute | solution.py:285
  459.7 2.7 collective-permute-start.13
  466.5 6.2 %drop.7 = (bf16[1536,512]{1,0:T(8,128)(2,1)S(1)}, bf16[2,4,256,128]{3,2,1,0:T(8,128)(2,1)S(1)}) custom-call(bf16[1024,1536]{1,0:T(8,128)(2,1)S(1)} %bitcast.31, bf16[1024,512]{1,0:T(8,128)(2,1)S(1)} %copy-done.30, bf16[1536,512]{1,0:T(8,128)(2,1)S(1)} %bitcast.48, bf16[1536,512]{1,0:T(8,128)(2,1)S(1)} %copy-done.22), custom_call_target="tpu_custom_call" | custom-call | flops 3221225472 | bytes 7864320 | tf_op jit(solution)/shard_map/drop/pallas_call | solution.py:262
  472.7 10.6 %collective-permute-done.11 = bf16[8,256,256]{2,1,0:T(8,128)(2,1)} collective-permute-done((bf16[8,256,256]{2,1,0:T(8,128)(2,1)}, bf16[8,256,256]{2,1,0:T(8,128)(2,1)}, u32[]{:S(2)}, u32[]{:S(2)}) %collective-permute-start.11) | collective-permute-done | bytes 1048608 | tf_op jit(solution)/shard_map/ppermute | solution.py:285
  483.4 3.6 collective-permute-start.5
  487.0 18.8 %collective-permute-done.12 = bf16[8,256,256]{2,1,0:T(8,128)(2,1)} collective-permute-done((bf16[8,256,256]{2,1,0:T(8,128)(2,1)}, bf16[8,256,256]{2,1,0:T(8,128)(2,1)}, u32[]{:S(2)}, u32[]{:S(2)}) %collective-permute-start.12) | collective-permute-done | bytes 1048608 | tf_op jit(solution)/shard_map/ppermute | solution.py:285
  507.3 3.1 add_bitcast_fusion.1
  510.6 4.3 collective-permute-done.14
  516.1 12.3 %collective-permute-done.13 = bf16[2,4,128,256]{3,2,1,0:T(8,128)(2,1)} collective-permute-done((bf16[2,4,128,256]{3,2,1,0:T(8,128)(2,1)}, bf16[2,4,128,256]{3,2,1,0:T(8,128)(2,1)}, u32[]{:S(2)}, u32[]{:S(2)}) %collective-permute-start.13) | collective-permute-done | bytes 524320 | tf_op jit(solution)/shard_map/ppermute | solution.py:285
  528.9 3.1 add_bitcast_fusion
  532.0 1.8 fusion.3
  533.8 1.5 maximum_bitcast_fusion.1
  535.3 1.9 collective-permute-done.9
  537.3 13.4 %collective-permute-done.8 = bf16[2,4,256,128]{3,2,1,0:T(8,128)(2,1)S(1)} collective-permute-done((bf16[2,4,256,128]{3,2,1,0:T(8,128)(2,1)S(1)}, bf16[2,4,256,128]{3,2,1,0:T(8,128)(2,1)S(1)}, u32[]{:S(2)}, u32[]{:S(2)}) %collective-permute-start.8) | collective-permute-done | bytes 524320 | tf_op jit(solution)/shard_map/ppermute | solution.py:285
  551.0 1.5 maximum_bitcast_fusion
  (91 shorter events, 34.9 us)
Async XLA Ops:
  0.6 1.2 copy-start.12
  1.9 1.4 copy-start.15
  7.0 1.7 copy-start.9
  9.7 43.5 %all-to-all-start = ((bf16[8,128,1536]{2,1,0:T(8,128)(2,1)}), bf16[8,128,1536]{2,1,0:T(8,128)(2,1)S(1)}, u32[]{:S(2)}, u32[]{:S(2)}) async-start(bf16[8,128,1536]{2,1,0:T(8,128)(2,1)} %copy-done.9), calls=%async_computation | async-start | bytes 6291456 | tf_op jit(solution)/shard_map/all_to_all | solution.py:295
  15.7 1.2 copy-start.11
  16.9 1.4 copy-start.13
  22.0 1.6 copy-start.1
  53.2 60.1 %all-to-all-start.4 = ((bf16[8,128,1536]{2,1,0:T(8,128)(2,1)}), bf16[8,128,1536]{2,1,0:T(8,128)(2,1)}, u32[]{:S(2)}, u32[]{:S(2)}) async-start(bf16[8,128,1536]{2,1,0:T(8,128)(2,1)} %copy-done.1), calls=%async_computation.4 | async-start | bytes 6291456 | tf_op jit(solution)/shard_map/all_to_all | solution.py:295
  58.4 47.2 %collective-permute-start.2 = (bf16[1536,512]{1,0:T(8,128)(2,1)}, bf16[1536,512]{1,0:T(8,128)(2,1)}, u32[]{:S(2)}, u32[]{:S(2)}) collective-permute-start(bf16[1536,512]{1,0:T(8,128)(2,1)} %bitcast.43), channel_id=1, source_target_pairs={{0,8},{8,0},{1,9},{9,1},{2,10},{10,2},{3,11},{11,3},{4,12},{12,4},... | collective-permute-start | bytes 4718600 | tf_op jit(solution)/shard_map/ppermute | solution.py:285
  60.9 44.8 %collective-permute-start.3 = (bf16[2,4,128,256]{3,2,1,0:T(8,128)(2,1)S(1)}, bf16[2,4,128,256]{3,2,1,0:T(8,128)(2,1)S(1)}, u32[]{:S(2)}, u32[]{:S(2)}) collective-permute-start(bf16[2,4,128,256]{3,2,1,0:T(8,128)(2,1)S(1)} %slice_select_fusion), channel_id=1, source_target_pairs={{0,8},{8,0},{1,9},{9,1},{2,10},{10,2},{3,11},{11,3},{4,12},{12,4},... | collective-permute-start | bytes 1572872 | tf_op jit(solution)/shard_map/ppermute | solution.py:285
  110.6 1.8 copy-start.2
  113.3 60.4 %all-to-all-start.5 = ((bf16[8,128,1536]{2,1,0:T(8,128)(2,1)}), bf16[8,128,1536]{2,1,0:T(8,128)(2,1)}, u32[]{:S(2)}, u32[]{:S(2)}) async-start(bf16[8,128,1536]{2,1,0:T(8,128)(2,1)} %copy-done.2), calls=%async_computation.5 | async-start | bytes 6291456 | tf_op jit(solution)/shard_map/all_to_all | solution.py:295
  118.8 47.4 %collective-permute-start = (bf16[1536,512]{1,0:T(8,128)(2,1)}, bf16[1536,512]{1,0:T(8,128)(2,1)S(1)}, u32[]{:S(2)}, u32[]{:S(2)}) collective-permute-start(bf16[1536,512]{1,0:T(8,128)(2,1)} %bitcast.46), channel_id=1, source_target_pairs={{0,8},{8,0},{1,9},{9,1},{2,10},{10,2},{3,11},{11,3},{4,12},{12,4},... | collective-permute-start | bytes 4718600 | tf_op jit(solution)/shard_map/ppermute | solution.py:285
  121.3 44.9 %collective-permute-start.1 = (bf16[2,4,256,128]{3,2,1,0:T(8,128)(2,1)S(1)}, bf16[2,4,256,128]{3,2,1,0:T(8,128)(2,1)S(1)}, u32[]{:S(2)}, u32[]{:S(2)}) collective-permute-start(bf16[2,4,256,128]{3,2,1,0:T(8,128)(2,1)S(1)} %slice_select_fusion.1), channel_id=1, source_target_pairs={{0,8},{8,0},{1,9},{9,1},{2,10},{10,2},{3,11},{11,3},{4,12},{12,4},... | collective-permute-start | bytes 1572872 | tf_op jit(solution)/shard_map/ppermute | solution.py:285
  169.9 1.6 copy-start.10
  173.7 43.4 %copy-start.23 = (bf16[1,8,256,256]{3,2,1,0:T(8,128)(2,1)S(1)}, bf16[1,8,256,256]{3,2,1,0:T(8,128)(2,1)}, u32[]{:S(2)}) copy-start(bf16[1,8,256,256]{3,2,1,0:T(8,128)(2,1)} %param.9) | copy-start | bytes 3145732
  173.7 43.4 %copy-start.25 = (bf16[1,8,256,256]{3,2,1,0:T(8,128)(2,1)S(1)}, bf16[1,8,256,256]{3,2,1,0:T(8,128)(2,1)}, u32[]{:S(2)}) copy-start(bf16[1,8,256,256]{3,2,1,0:T(8,128)(2,1)} %param.10) | copy-start | bytes 3145732
  243.7 1.7 copy-start.4
  245.4 43.1 %all-to-all-start.7 = ((bf16[8,128,1536]{2,1,0:T(8,128)(2,1)}), bf16[8,128,1536]{2,1,0:T(8,128)(2,1)}, u32[]{:S(2)}, u32[]{:S(2)}) async-start(bf16[8,128,1536]{2,1,0:T(8,128)(2,1)} %bitcast.35), calls=%async_computation.7 | async-start | bytes 6291456 | tf_op jit(solution)/shard_map/all_to_all | solution.py:295
  250.8 1.9 copy-start.3
  253.9 1.2 copy-start.26
  270.3 1.8 copy-start.6
  272.1 1.6 copy-start.8
  288.5 43.4 %copy-start.7 = (bf16[8,8,16,1536]{3,2,1,0:T(8,128)(2,1)S(1)}, bf16[8,8,16,1536]{3,2,1,0:T(8,128)(2,1)}, u32[]{:S(2)}) copy-start(bf16[8,8,16,1536]{3,2,1,0:T(8,128)(2,1)} %copy-done.6) | copy-start | bytes 9437188
  374.0 88.5 %all-to-all-start.6 = ((bf16[8,128,1536]{2,1,0:T(8,128)(2,1)}), bf16[8,128,1536]{2,1,0:T(8,128)(2,1)S(1)}, u32[]{:S(2)}, u32[]{:S(2)}) async-start(bf16[8,128,1536]{2,1,0:T(8,128)(2,1)} %bitcast.16), calls=%async_computation.6 | async-start | bytes 6291456 | tf_op jit(solution)/shard_map/all_to_all | solution.py:295
  378.6 1.9 copy-start.5
  381.7 8.7 %copy-start.20 = (bf16[1536,512]{1,0:T(8,128)(2,1)S(1)}, bf16[1536,512]{1,0:T(8,128)(2,1)}, u32[]{:S(2)}) copy-start(bf16[1536,512]{1,0:T(8,128)(2,1)} %copy-done.19) | copy-start | bytes 4718596
  381.7 8.7 %copy-start.36 = (bf16[1024,512]{1,0:T(8,128)(2,1)S(1)}, bf16[1024,512]{1,0:T(8,128)(2,1)}, u32[]{:S(2)}) copy-start(bf16[1024,512]{1,0:T(8,128)(2,1)} %copy-done.35) | copy-start | bytes 3145732
  389.2 35.7 %collective-permute-start.4 = (bf16[1536,512]{1,0:T(8,128)(2,1)S(1)}, bf16[1536,512]{1,0:T(8,128)(2,1)S(1)}, u32[]{:S(2)}, u32[]{:S(2)}) collective-permute-start(bf16[1536,512]{1,0:T(8,128)(2,1)S(1)} %get-tuple-element.34), channel_id=1, source_target_pairs={{0,8},{8,0},{1,9},{9,1},{2,10},{10,2},{3,11},{11,3},{4,12},{12,4},... | collective-permute-start | bytes 4718600 | tf_op jit(solution)/shard_map/ppermute | solution.py:285
  390.4 35.7 %copy-start = (bf16[8,128,1536]{2,1,0:T(8,128)(2,1)S(1)}, bf16[8,128,1536]{2,1,0:T(8,128)(2,1)}, u32[]{:S(2)}) copy-start(bf16[8,128,1536]{2,1,0:T(8,128)(2,1)} %all_to_all.42) | copy-start | bytes 9437188
  390.4 35.7 %copy-start.14 = (bf16[1,1536,512]{2,1,0:T(8,128)(2,1)S(1)}, bf16[1,1536,512]{2,1,0:T(8,128)(2,1)}, u32[]{:S(2)}) copy-start(bf16[1,1536,512]{2,1,0:T(8,128)(2,1)} %param.7) | copy-start | bytes 4718596
  390.4 35.7 %copy-start.32 = (bf16[1024,512]{1,0:T(8,128)(2,1)S(1)}, bf16[1024,512]{1,0:T(8,128)(2,1)}, u32[]{:S(2)}) copy-start(bf16[1024,512]{1,0:T(8,128)(2,1)} %copy-done.31) | copy-start | bytes 3145732
  397.8 34.8 %copy-start.27 = (bf16[2,4,256,128]{3,2,1,0:T(8,128)(2,1)}, bf16[2,4,256,128]{3,2,1,0:T(8,128)(2,1)S(1)}, u32[]{:S(2)}) copy-start(bf16[2,4,256,128]{3,2,1,0:T(8,128)(2,1)S(1)} %get-tuple-element.45) | copy-start | bytes 1572868
  397.8 60.8 %collective-permute-start.6 = (bf16[1536,512]{1,0:T(8,128)(2,1)S(1)}, bf16[1536,512]{1,0:T(8,128)(2,1)S(1)}, u32[]{:S(2)}, u32[]{:S(2)}) collective-permute-start(bf16[1536,512]{1,0:T(8,128)(2,1)S(1)} %get-tuple-element.42), channel_id=1, source_target_pairs={{0,8},{8,0},{1,9},{9,1},{2,10},{10,2},{3,11},{11,3},{4,12},{12,4},... | collective-permute-start | bytes 4718600 | tf_op jit(solution)/shard_map/ppermute | solution.py:285
  398.1 85.3 %collective-permute-start.11 = (bf16[8,256,256]{2,1,0:T(8,128)(2,1)}, bf16[8,256,256]{2,1,0:T(8,128)(2,1)}, u32[]{:S(2)}, u32[]{:S(2)}) collective-permute-start(bf16[8,256,256]{2,1,0:T(8,128)(2,1)} %get-tuple-element.46), channel_id=1, source_target_pairs={{0,64},{64,0},{1,65},{65,1},{2,66},{66,2},{3,67},{67,3},{4,68},{68... | collective-permute-start | bytes 3145736 | tf_op jit(solution)/shard_map/ppermute | solution.py:285
  400.8 105.0 %collective-permute-start.12 = (bf16[8,256,256]{2,1,0:T(8,128)(2,1)}, bf16[8,256,256]{2,1,0:T(8,128)(2,1)}, u32[]{:S(2)}, u32[]{:S(2)}) collective-permute-start(bf16[8,256,256]{2,1,0:T(8,128)(2,1)} %get-tuple-element.47), channel_id=1, source_target_pairs={{0,64},{64,0},{1,65},{65,1},{2,66},{66,2},{3,67},{67,3},{4,68},{68... | collective-permute-start | bytes 3145736 | tf_op jit(solution)/shard_map/ppermute | solution.py:285
  401.1 109.3 %collective-permute-start.15 = (bf16[2,4,128,256]{3,2,1,0:T(8,128)(2,1)}, bf16[2,4,128,256]{3,2,1,0:T(8,128)(2,1)}, u32[]{:S(2)}, u32[]{:S(2)}) collective-permute-start(bf16[2,4,128,256]{3,2,1,0:T(8,128)(2,1)} %get-tuple-element.49), channel_id=1, source_target_pairs={{0,72},{8,64},{64,8},{72,0},{1,73},{9,65},{65,9},{73,1},{2,74},{10... | collective-permute-start | bytes 1572872 | tf_op jit(solution)/shard_map/ppermute | solution.py:285
  424.9 90.0 %collective-permute-start.14 = (bf16[2,4,128,256]{3,2,1,0:T(8,128)(2,1)}, bf16[2,4,128,256]{3,2,1,0:T(8,128)(2,1)}, u32[]{:S(2)}, u32[]{:S(2)}) collective-permute-start(bf16[2,4,128,256]{3,2,1,0:T(8,128)(2,1)} %get-tuple-element.49), channel_id=1, source_target_pairs={{0,8},{8,0},{1,9},{9,1},{2,10},{10,2},{3,11},{11,3},{4,12},{12,4},... | collective-permute-start | bytes 1572872 | tf_op jit(solution)/shard_map/ppermute | solution.py:285
  459.7 68.6 %collective-permute-start.13 = (bf16[2,4,128,256]{3,2,1,0:T(8,128)(2,1)}, bf16[2,4,128,256]{3,2,1,0:T(8,128)(2,1)}, u32[]{:S(2)}, u32[]{:S(2)}) collective-permute-start(bf16[2,4,128,256]{3,2,1,0:T(8,128)(2,1)} %get-tuple-element.48), channel_id=1, source_target_pairs={{0,64},{64,0},{1,65},{65,1},{2,66},{66,2},{3,67},{67,3},{4,68},{68... | collective-permute-start | bytes 1572872 | tf_op jit(solution)/shard_map/ppermute | solution.py:285
  462.5 1.4 copy-start.16
  463.9 1.4 copy-start.22
  466.5 16.8 %copy-start.18 = (bf16[1536,512]{1,0:T(8,128)(2,1)S(1)}, bf16[1536,512]{1,0:T(8,128)(2,1)}, u32[]{:S(2)}) copy-start(bf16[1536,512]{1,0:T(8,128)(2,1)} %copy-done.17) | copy-start | bytes 4718596
  483.4 69.1 %collective-permute-start.5 = (bf16[1536,512]{1,0:T(8,128)(2,1)S(1)}, bf16[1536,512]{1,0:T(8,128)(2,1)S(1)}, u32[]{:S(2)}, u32[]{:S(2)}) collective-permute-start(bf16[1536,512]{1,0:T(8,128)(2,1)S(1)} %copy-done.18), channel_id=1, source_target_pairs={{0,16},{16,32},{32,48},{1,17},{17,33},{33,49},{2,18},{18,34},{34,5... | collective-permute-start | bytes 4718600 | tf_op jit(solution)/shard_map/ppermute | solution.py:291
  505.8 4.5 copy-start.28
  505.8 46.6 %collective-permute-start.7 = (bf16[1536,512]{1,0:T(8,128)(2,1)S(1)}, bf16[1536,512]{1,0:T(8,128)(2,1)S(1)}, u32[]{:S(2)}, u32[]{:S(2)}) collective-permute-start(bf16[1536,512]{1,0:T(8,128)(2,1)S(1)} %get-tuple-element.43), channel_id=1, source_target_pairs={{16,0},{32,16},{48,32},{17,1},{33,17},{49,33},{18,2},{34,18},{50,3... | collective-permute-start | bytes 4718600 | tf_op jit(solution)/shard_map/ppermute | solution.py:291
  510.4 25.0 %collective-permute-start.10 = (bf16[2,4,256,128]{3,2,1,0:T(8,128)(2,1)S(1)}, bf16[2,4,256,128]{3,2,1,0:T(8,128)(2,1)S(1)}, u32[]{:S(2)}, u32[]{:S(2)}) collective-permute-start(bf16[2,4,256,128]{3,2,1,0:T(8,128)(2,1)S(1)} %copy-done.28), channel_id=1, source_target_pairs={{0,72},{8,64},{64,8},{72,0},{1,73},{9,65},{65,9},{73,1},{2,74},{10... | collective-permute-start | bytes 1572872 | tf_op jit(solution)/shard_map/ppermute | solution.py:285
  514.9 22.4 %collective-permute-start.9 = (bf16[2,4,256,128]{3,2,1,0:T(8,128)(2,1)S(1)}, bf16[2,4,256,128]{3,2,1,0:T(8,128)(2,1)S(1)}, u32[]{:S(2)}, u32[]{:S(2)}) collective-permute-start(bf16[2,4,256,128]{3,2,1,0:T(8,128)(2,1)S(1)} %copy-done.28), channel_id=1, source_target_pairs={{0,8},{8,0},{1,9},{9,1},{2,10},{10,2},{3,11},{11,3},{4,12},{12,4},... | collective-permute-start | bytes 1572872 | tf_op jit(solution)/shard_map/ppermute | solution.py:285
  528.3 22.4 %collective-permute-start.8 = (bf16[2,4,256,128]{3,2,1,0:T(8,128)(2,1)S(1)}, bf16[2,4,256,128]{3,2,1,0:T(8,128)(2,1)S(1)}, u32[]{:S(2)}, u32[]{:S(2)}) collective-permute-start(bf16[2,4,256,128]{3,2,1,0:T(8,128)(2,1)S(1)} %get-tuple-element.44), channel_id=1, source_target_pairs={{0,64},{64,0},{1,65},{65,1},{2,66},{66,2},{3,67},{67,3},{4,68},{68... | collective-permute-start | bytes 1572872 | tf_op jit(solution)/shard_map/ppermute | solution.py:285
  (10 other events, 11.0 us)

commit v2 on v1

v2 whole, which is shorter than its diff:
```python
import functools
import math

import jax
import jax.numpy as jnp
from jax import lax
from jax.experimental import pallas as pl
from jax.experimental.pallas import tpu as pltpu
from jax.sharding import Mesh, PartitionSpec as P

BF = jnp.bfloat16
F32 = jnp.float32
GELU_A = math.sqrt(2.0 / math.pi)
GELU_B = 0.044715
YC = ("y", "core")
VMEM_MIB = 62
COST = 0.02


def params(mib):
    return pltpu.CompilerParams(vmem_limit_bytes=mib * 1024 * 1024)


def cost(flops, nbytes, trans=0):
    return pl.CostEstimate(flops=int(flops * COST), bytes_accessed=int(nbytes * COST), transcendentals=int(trans * COST))


def mm(a, b, dims):
    return lax.dot_general(a, b, (dims, ((), ())), preferred_element_type=F32)


def hot_key(shape, row_dim, sub):
    row = lax.broadcasted_iota(jnp.int32, shape, row_dim)
    col = lax.broadcasted_iota(jnp.int32, shape, 1 - row_dim)
    return jnp.where((row // sub) == (col // 2), row % sub - col % 2, -1)


def one_hot(key, group, k, sub):
    return jnp.where(key == group * (sub // 2) + k * 2, 1.0, 0.0).astype(BF)


def spread_weights(swap, f_ref, a_ref):
    groups, expand = f_ref.shape[0], f_ref.shape[1]
    rows, width = a_ref.shape
    wide = width // groups
    sub = groups * expand * 2
    key = hot_key((rows, 2 * rows // sub), 0, sub)
    for g in range(groups):
        pick = jnp.concatenate([one_hot(key, g, k, sub) for k in range(expand)], axis=1)
        if swap:
            source = jnp.concatenate([f_ref[g, k] for k in range(expand)], axis=1)
            value = mm(pick, source, ((1,), (1,)))
        else:
            value = mm(pick, f_ref[g].reshape(-1, wide), ((1,), (0,)))
        a_ref[:, g * wide : (g + 1) * wide] = value.astype(BF)


def lift_body(swaps, steps, side_ref, *refs):
    count = len(swaps)
    x_refs, f_refs, out_ref, a_refs = refs[:count], refs[count : 2 * count], refs[2 * count], refs[2 * count + 1 :]
    step = pl.program_id(0)
    for n in range(count):

        @pl.when(step == n * steps)
        def _(n=n):
            spread_weights(swaps[n], f_refs[n], a_refs[n])

        @pl.when((step >= n * steps) & (step < (n + 1) * steps))
        def _(n=n):
            value = mm(a_refs[n][...], x_refs[n][...], ((1,), (1,))).astype(BF)
            out_ref[...] = value.reshape(out_ref.shape)


def lift(xs, factors, swaps, side, peers, tile):
    count = len(xs)
    tokens, width = xs[0].shape
    steps = tokens // tile
    groups, expand = factors[0].shape[0], factors[0].shape[1]
    bsize = width // groups
    local = groups * expand
    rows = peers * local * local * 2
    cols = peers * local * 2
    x_specs, f_specs = [], []
    for n, swap in enumerate(swaps):
        x_specs.append(
            pl.BlockSpec((tile, width), lambda i, s, n=n: (jnp.clip(i - n * steps, 0, steps - 1), 0))
        )
        if swap:
            f_specs.append(pl.BlockSpec((groups, expand, bsize, cols), lambda i, s: (0, 0, 0, s[0])))
        else:
            f_specs.append(pl.BlockSpec((groups, expand, cols, bsize), lambda i, s: (0, 0, s[0], 0)))
    return pl.pallas_call(
        functools.partial(lift_body, swaps, steps),
        grid_spec=pltpu.PrefetchScalarGridSpec(
            num_scalar_prefetch=1,
            grid=(count * steps,),
            in_specs=x_specs + f_specs,
            out_specs=[
                pl.BlockSpec((peers, 1, rows // peers, tile), lambda i, s: (0, i // steps, 0, i % steps))
            ]
            + [pl.BlockSpec((rows, width), lambda i, s: (0, 0))] * count,
        ),
        out_shape=[jax.ShapeDtypeStruct((peers, count, rows // peers, tokens), BF)]
        + [jax.ShapeDtypeStruct((rows, width), BF)] * count,
        compiler_params=params(VMEM_MIB),
        cost_estimate=cost(4 * count * rows * width * tokens, 2 * count * tokens * (width + rows)),
        name="lift",
    )(side, *xs, *factors)


def gather_rows(scratch, side, own, peer):
    half = scratch.shape[0] // 2
    mine = pl.multiple_of(side * half, half)
    theirs = pl.multiple_of((1 - side) * half, half)
    scratch[pl.ds(mine, half), :] = own[...].reshape(half, scratch.shape[1])
    scratch[pl.ds(theirs, half), :] = peer[...].reshape(half, scratch.shape[1])


def split_rows(scratch, side, own, peer):
    half = scratch.shape[0] // 2
    mine = pl.multiple_of(side * half, half)
    theirs = pl.multiple_of((1 - side) * half, half)
    own[...] = scratch[pl.ds(mine, half), :].reshape(own.shape)
    peer[...] = scratch[pl.ds(theirs, half), :].reshape(peer.shape)


def forward_body(side_ref, ro_ref, rp_ref, w2_ref, w3_ref, out_ref, mixed, narrow):
    side = side_ref[0]
    gather_rows(mixed, side, ro_ref, rp_ref)
    pre = mm(w2_ref[0], mixed[...], ((0,), (0,)))
    act = (0.5 * pre * (1.0 + jnp.tanh(GELU_A * (pre + GELU_B * (pre * pre * pre))))).astype(BF)
    narrow[...] = mm(w3_ref[0], act, ((0,), (0,))).astype(BF)
    split_rows(narrow, side, out_ref.at[:, 0], out_ref.at[:, 1])


def plane_spec(array, plane, tile, start=0):
    peers, _, _, sub, _ = array.shape
    return pl.BlockSpec((peers, 1, 1, sub, tile), lambda c, i, s: (0, plane, start + c, 0, i))


def forward(side, own, peer, second, third, tile):
    peers, _, local, sub, tokens = own[0].shape
    bsize = second.shape[1]
    weight = pl.BlockSpec((1, bsize, bsize), lambda c, i, s: (c, 0, 0))
    return pl.pallas_call(
        forward_body,
        grid_spec=pltpu.PrefetchScalarGridSpec(
            num_scalar_prefetch=1,
            grid=(local, tokens // tile),
            in_specs=[plane_spec(*own, tile), plane_spec(*peer, tile), weight, weight],
            out_specs=pl.BlockSpec((peers, 2, 1, sub, tile), lambda c, i, s: (0, 0, c, 0, i)),
            scratch_shapes=[pltpu.VMEM((bsize, tile), BF), pltpu.VMEM((bsize, tile), BF)],
        ),
        out_shape=jax.ShapeDtypeStruct((peers, 2, local, sub, tokens), BF),
        compiler_params=params(VMEM_MIB),
        cost_estimate=cost(
            4 * local * bsize * bsize * tokens, 4 * local * bsize * tokens, local * bsize * tokens
        ),
        name="forward",
    )(side, own[0], peer[0], second, third)


def backward_body(
    steps, side_ref, ro_ref, rp_ref, go_ref, gp_ref, w2_ref, w3_ref, *rest,
):
    outs, (mixed, gnar, gmix, acc2, acc3) = rest[-8 - steps : -5], rest[-5:]
    mp_ref, g2_ref, g3_ref, mo_refs = outs[0], outs[1], outs[2], outs[3:]
    side = side_ref[0]
    step = pl.program_id(1)
    gather_rows(mixed, side, ro_ref, rp_ref)
    gather_rows(gnar, side, go_ref, gp_ref)
    pre = mm(w2_ref[0], mixed[...], ((0,), (0,)))
    square = pre * pre
    th = jnp.tanh(GELU_A * (pre + GELU_B * (square * pre)))
    half = 0.5 * (1.0 + th)
    act = (pre * half).astype(BF)
    slope = half + (0.5 * GELU_A) * pre * (1.0 - th * th) * (1.0 + (3.0 * GELU_B) * square)
    grad_act = mm(w3_ref[0], gnar[...], ((1,), (0,)))
    grad_pre = (grad_act * slope).astype(BF)
    gmix[...] = mm(w2_ref[0], grad_pre, ((1,), (0,))).astype(BF)
    for i, mo_ref in enumerate(mo_refs):

        @pl.when(step == i)
        def _(mo_ref=mo_ref):
            split_rows(gmix, side, mo_ref, mp_ref)

    add3 = mm(act, gnar[...], ((1,), (1,)))
    add2 = mm(mixed[...], grad_pre, ((1,), (1,)))

    @pl.when(step == 0)
    def _():
        acc2[...] = add2
        acc3[...] = add3

    @pl.when(step > 0)
    def _():
        acc2[...] += add2
        acc3[...] += add3

    @pl.when(step == pl.num_programs(1) - 1)
    def _():
        g2_ref[0] = acc2[...].astype(BF)
        g3_ref[0] = acc3[...].astype(BF)


def backward(side, own, peer, grad_own, grad_peer, second, third, tile, start, count, into):
    peers, _, local, sub, tokens = own[0].shape
    bsize = second.shape[1]
    steps = tokens // tile
    pieces = [plane_spec(*each, tile, start) for each in (own, peer, grad_own, grad_peer)]
    piece = pl.BlockSpec((peers, 1, sub, tile), lambda c, i, s: (0, start + c, 0, i))
    part = pl.BlockSpec((peers, 1, sub, tile), lambda c, i, s: (0, start + c, 0, 0))
    weight = pl.BlockSpec((1, bsize, bsize), lambda c, i, s: (start + c, 0, 0))
    grad = pl.BlockSpec((1, bsize, bsize), lambda c, i, s: (c, 0, 0))
    grads = jax.ShapeDtypeStruct((count, bsize, bsize), BF)
    extra = () if into is None else into
    return pl.pallas_call(
        functools.partial(backward_body, steps),
        grid_spec=pltpu.PrefetchScalarGridSpec(
            num_scalar_prefetch=1,
            grid=(count, tokens // tile),
            in_specs=pieces + [weight] * 2 + [pl.BlockSpec(memory_space=pl.ANY)] * len(extra),
            out_specs=[piece, grad, grad] + [part] * steps,
            scratch_shapes=[pltpu.VMEM((bsize, tile), BF)] * 3
            + [pltpu.VMEM((bsize, bsize), F32)] * 2,
        ),
        out_shape=[jax.ShapeDtypeStruct((peers, local, sub, tokens), BF), grads, grads]
        + [jax.ShapeDtypeStruct((peers, local, sub, tile), BF)] * steps,
        input_output_aliases={7 + i: (0 if i == 0 else 2 + i) for i in range(len(extra))},
        compiler_params=params(VMEM_MIB),
        cost_estimate=cost(
            10 * count * bsize * bsize * tokens, 6 * count * bsize * tokens, count * bsize * tokens
        ),
        name="backward",
    )(side, own[0], peer[0], grad_own[0], grad_peer[0], second, third, *extra)


def emit_body(add, s_ref, a_ref, *rest):
    prev_ref, out_ref = rest if add else (None, rest[0])
    value = mm(a_ref[...], s_ref[...].reshape(a_ref.shape[1], -1), ((1,), (0,))).T
    if add:
        value = value + prev_ref[...].astype(F32)
    out_ref[...] = value.astype(BF)


def emit(s, plane, a, prev, tile, start, tokens):
    width, rows = a.shape
    peers, _, each, _ = s.shape
    first = start // tile
    add = prev is not None
    wide = pl.BlockSpec((tile, width), lambda i: (i, 0))
    return pl.pallas_call(
        functools.partial(emit_body, add),
        grid=(tokens // tile,),
        in_specs=[
            pl.BlockSpec((peers, 1, each, tile), lambda i: (0, plane, 0, first + i)),
            pl.BlockSpec((width, rows), lambda i: (0, 0)),
        ]
        + ([wide] if add else []),
        out_specs=wide,
        out_shape=jax.ShapeDtypeStruct((tokens, width), BF),
        compiler_params=params(VMEM_MIB),
        cost_estimate=cost(2 * rows * width * tokens, 2 * tokens * (rows + 2 * width)),
        name="emit",
    )(*((s, a) + ((prev,) if add else ())))


def wgrad_body(swap, groups, expand, count, *refs):
    s_refs, (x_ref, g_ref, acc) = refs[:count], refs[count:]
    step = pl.program_id(0)
    rows, width = acc.shape
    wide = width // groups
    sub = groups * expand * 2
    cols = 2 * rows // sub

    for i in range(count):

        @pl.when(step == i)
        def _(i=i):
            more = mm(s_refs[i][...].reshape(rows, -1), x_ref[...], ((1,), (0,)))
            acc[...] = more if i == 0 else acc[...] + more

    @pl.when(step == count - 1)
    def _():
        key = hot_key((rows, cols) if swap else (cols, rows), 0 if swap else 1, sub)
        for g in range(groups):
            part = acc[:, g * wide : (g + 1) * wide].astype(BF)
            if swap:
                part = part.T
            picks = [one_hot(key, g, k, sub) for k in range(expand)]
            if swap:
                got = mm(part, jnp.concatenate(picks, axis=1), ((1,), (0,))).astype(BF)
            else:
                got = mm(jnp.concatenate(picks, axis=0), part, ((1,), (0,))).astype(BF)
            for k in range(expand):
                at = slice(k * cols, (k + 1) * cols)
                g_ref[g, k] = got[:, at] if swap else got[at]


def wgrad(s, x, groups, expand, swap):
    count = len(s)
    width = x.shape[1]
    tile = x.shape[0] // count
    peers, _, each, _ = s[0][0].shape
    rows = peers * each
    bsize = width // groups
    cols = rows // (groups * expand)
    grads = (groups, expand, bsize, cols) if swap else (groups, expand, cols, bsize)
    specs = [
        pl.BlockSpec((peers, 1, each, tile), lambda i, plane=plane, at=at: (0, plane, 0, at))
        for _, plane, at in s
    ]
    return pl.pallas_call(
        functools.partial(wgrad_body, swap, groups, expand, count),
        grid=(count,),
        in_specs=specs + [pl.BlockSpec((tile, width), lambda i: (i, 0))],
        out_specs=pl.BlockSpec(grads, lambda i: (0, 0, 0, 0)),
        scratch_shapes=[pltpu.VMEM((rows, width), F32)],
        out_shape=jax.ShapeDtypeStruct(grads, BF),
        compiler_params=params(VMEM_MIB),
        cost_estimate=cost(2 * rows * width * x.shape[0], 2 * x.shape[0] * (rows + width)),
        name="wgrad",
    )(*[array for array, _, _ in s], x)


def copied(value):
    return place(value, None, 0, 1)


def swapped(value, axes):
    count = lax.axis_size(axes)
    return lax.ppermute(value, axes, [(i, count - 1 - i) for i in range(count)])


def shifted(value, axis, steps):
    count = lax.axis_size(axis)
    leading, last = (max(0, -steps), min(count, count - steps))
    return lax.ppermute(value, axis, [(source, source + steps) for source in range(leading, last)])


def spread_out(value):
    return lax.all_to_all(value, YC, split_axis=0, concat_axis=0, tiled=True)


def behind(value, after):
    return value if after is None else lax.optimization_barrier((value, after))[0]


def halves(value, dim):
    size = value.shape[dim] // 2
    return lax.slice_in_dim(value, 0, size, axis=dim), lax.slice_in_dim(value, size, 2 * size, axis=dim)


def join_body(starts, sizes, *refs):
    out_ref = refs[-1]
    at = pl.program_id(0)
    for n, (start, size) in enumerate(zip(starts, sizes)):

        @pl.when((at >= start) & (at < start + size))
        def _(n=n):
            out_ref[...] = refs[2 * n][...].astype(F32) + refs[2 * n + 1][...].astype(F32)


def join(pairs):
    sizes = [a.shape[0] for a, _ in pairs]
    starts = [sum(sizes[:n]) for n in range(len(sizes))]
    rest = pairs[0][0].shape[1:]
    specs = []
    for start, size in zip(starts, sizes):
        spec = pl.BlockSpec(
            (1,) + rest, lambda i, start=start, size=size: (jnp.clip(i - start, 0, size - 1), 0, 0)
        )
        specs += [spec, spec]
    return pl.pallas_call(
        functools.partial(join_body, starts, sizes),
        grid=(sum(sizes),),
        in_specs=specs,
        out_specs=pl.BlockSpec((1,) + rest, lambda i: (i, 0, 0)),
        out_shape=jax.ShapeDtypeStruct((sum(sizes),) + rest, F32),
        compiler_params=params(VMEM_MIB),
        cost_estimate=cost(1, 1),
        name="join",
    )(*[each for pair in pairs for each in pair])


def paired_body(side_ref, ma_ref, mb_ref, ta_ref, tb_ref, out_ref):
    step = pl.program_id(0)

    @pl.when(step == 0)
    def _():
        out_ref[...] = ma_ref[...].astype(F32) + mb_ref[...].astype(F32)

    @pl.when(step == 1)
    def _():
        out_ref[...] = ta_ref[...].astype(F32) + tb_ref[...].astype(F32)


def paired(side, mine, theirs, dim):
    shape = mine[0].shape
    whole = pl.BlockSpec(shape, lambda i, s: (0,) * len(shape))

    def where(i, s):
        half = jnp.where(i == 0, s[0], 1 - s[0])
        return tuple(half if n == dim else 0 for n in range(len(shape)))

    full = tuple(2 * size if n == dim else size for n, size in enumerate(shape))
    return pl.pallas_call(
        paired_body,
        grid_spec=pltpu.PrefetchScalarGridSpec(
            num_scalar_prefetch=1,
            grid=(2,),
            in_specs=[whole] * 4,
            out_specs=pl.BlockSpec(shape, where),
        ),
        out_shape=jax.ShapeDtypeStruct(full, F32),
        compiler_params=params(VMEM_MIB),
        cost_estimate=cost(1, 1),
        name="paired",
    )(side, *mine, *theirs)


def place_body(value_ref, *rest):
    rest[-1][...] = value_ref[...]


def place(value, into, at, count):
    rows, width = value.shape
    extra = () if into is None else (into,)
    return pl.pallas_call(
        place_body,
        grid=(1,),
        in_specs=[pl.BlockSpec((rows, width), lambda i: (0, 0))]
        + [pl.BlockSpec(memory_space=pl.ANY)] * len(extra),
        out_specs=pl.BlockSpec((rows, width), lambda i: (at, 0)),
        out_shape=jax.ShapeDtypeStruct((count * rows, width), value.dtype),
        input_output_aliases={1: 0} if extra else {},
        compiler_params=params(VMEM_MIB),
        cost_estimate=cost(1, 1),
        name="place",
    )(value, *extra)


def shards(inputs, upstream, factor_one, factor_two, factor_three, factor_four):
    x, u = inputs[0], upstream[0]
    first, second, third, fourth = factor_one[0], factor_two[0], factor_three[0], factor_four[0]
    groups, expand, bsize = first.shape[0], first.shape[1], first.shape[2]
    local = groups * expand
    tokens = x.shape[0]
    peers = lax.axis_size("y") * lax.axis_size("core")
    low_or_high = lax.axis_index("xlo")
    is_low = low_or_high == 0
    side = low_or_high.astype(jnp.int32).reshape(1)
    zero = jnp.zeros((1,), jnp.int32)
    tile = 512 if tokens % 512 == 0 else tokens
    half = tokens // 2

    low, high = halves(first, 3)
    first_peer = swapped(jnp.where(is_low, high, low), "xlo")
    x_peer = swapped(x, "xlo")
    low, high = halves(fourth, 2)
    fourth_side = jnp.where(is_low, high, low)
    early = 2 * tokens // 3
    u_early = swapped(behind(u[:early], (x_peer, first_peer)), "xlo")
    u_late = swapped(behind(u[early:], u_early), "xlo")
    fourth_peer = swapped(behind(fourth_side, u_early), "xlo")
    u_peer = jnp.concatenate([u_early, u_late], axis=0)

    def inner(value, after=None):
        return spread_out(behind(value, after)).reshape(peers, -1, local, 2 * local, tokens)

    def outer(value, after):
        value = value.reshape(peers, -1, 2 * local * local, value.shape[-1])
        return spread_out(behind(value, after))

    l12, a1o, a4o = lift([x, u], [first, fourth], [True, False], side, peers, tile)
    y12 = inner(l12)
    l1p, a1p = lift([x_peer], [first_peer], [True], zero, peers, tile)
    y1p = inner(l1p, (y12, u_early))
    l2p, a4p = lift([u_peer], [fourth_peer], [False], zero, peers, tile)
    y2p = inner(l2p, y1p)
    a1o, a4o, a1p, a4p = a1o.T, a4o.T, a1p.T, a4p.T
    n = forward(behind(side, (a1o, a4o, a1p, a4p)), (y12, 0), (y1p, 0), second, third, half)
    y3 = outer(n, y2p)

    args = ((y12, 0), (y1p, 0), (y12, 1), (y2p, 0), second, third, half)
    third_part = -(-local // 3)
    cuts = [0, third_part, 2 * third_part, local]
    into, g2, g3, d2, d3 = None, [], [], [], []
    gate = side
    for n in range(3):
        got = backward(gate, *args, cuts[n], cuts[n + 1] - cuts[n], into)
        mp, mo1, mo2 = into = (got[0], got[3], got[4])
        g2.append(got[1])
        g3.append(got[2])
        d2.append(swapped(got[1], "dp"))
        d3.append(swapped(got[2], "dp"))
        if n == 1:
            gate = behind(side, (d2[0], d3[0]))
    y4p = outer(mp, (y3, *d2, *d3))
    out_p = emit(y3, 1, a4p, None, half, 0, tokens)
    out_peer = swapped(out_p, "xlo")
    g4p = wgrad([(y3, 1, 0), (y3, 1, 1)], behind(u_peer, out_p), groups, expand, False)
    g4o = wgrad([(y3, 0, 0), (y3, 0, 1)], u, groups, expand, False)
    grad_two = join(list(zip(g2, d2)))
    grad_three = join(list(zip(g3, d3)))
    y4a = outer(mo1, (y4p, g4o, g4p, grad_two, grad_three))
    t4x = swapped(behind(g4p, out_peer), "xlo")
    t4d = swapped(behind(g4p, out_peer), ("dp", "xlo"))
    out_o = emit(y3, 0, a4o, out_peer, half, 0, tokens)
    y_next = copied(shifted(out_o, "pipe", 1))
    in_p1 = emit(y4p, 0, a1p, None, half, 0, half)
    in_p2 = emit(y4p, 0, a1p, None, half, half, half)
    in_peer1 = swapped(behind(in_p1, (t4x, t4d, out_o)), "xlo")
    in_peer2 = swapped(behind(in_p2, in_peer1), "xlo")
    g1p = wgrad([(y4p, 0, 0), (y4p, 0, 1)], behind(x_peer, in_p2), groups, expand, True)
    y4b = outer(mo2, (y4a, in_p2))
    d4o = swapped(behind(g4o, in_peer2), "dp")
    in_a = emit(y4a, 0, a1o, in_peer1, half, 0, half)
    dx1 = shifted(in_a, "pipe", -1)
    t1x = swapped(behind(g1p, in_peer2), "xlo")
    t1d = swapped(behind(g1p, in_peer2), ("dp", "xlo"))
    in_b = emit(y4b, 0, a1o, behind(in_peer2, g1p), half, 0, half)
    dx2 = shifted(in_b, "pipe", -1)
    dx_prev = place(dx1, None, 0, 2)
    g1o = wgrad(
        [(y4a, 0, 0), (y4b, 0, 0)],
        behind(x, in_b),
        groups, expand, True,
    )
    d1o = behind(swapped(g1o, "dp"), dx2)
    grad_four = paired(side, (g4o, d4o), (t4x, t4d), 2)
    grad_one = paired(side, (g1o, d1o), (t1x, t1d), 3)
    dx_prev = place(dx2, dx_prev, 1, 2)
    return (
        y_next[None], dx_prev[None], grad_one[None], grad_two[None], grad_three[None], grad_four[None],
    )


def solution(mesh):
    parts = mesh.shape["tensor"]
    devices = mesh.devices.reshape(mesh.shape["dp"], mesh.shape["pipe"], 2, parts // 4, 2)
    fine = Mesh(devices, ("dp", "pipe", "xlo", "y", "core"))
    wide = ("xlo", "y", "core")
    acts = P("pipe", "dp", wide)
    five = P("pipe", wide, None, None, None)
    four = P("pipe", wide, None, None)
    return jax.shard_map(
        shards,
        mesh=fine,
        in_specs=(acts, acts, five, four, four, five),
        out_specs=(acts, acts, five, four, four, five),
        check_vma=False,
    )
```

time: 556 us -> 409 us (0.74)
  blocking collectives: 129 us -> 0 us
  Pallas kernels: 85.2 us -> 143 us
  waiting for transfers between devices: 240 us -> 183 us
  local copies, waits for them, and re-layouts: 38.2 us -> 9.74 us
  starting transfers between devices: 47.6 us -> 69 us
  other arithmetic: 13.8 us -> 0.12 us
    all_to_all x3 -> x0, blocking collectives: 129 us -> none  [spread_out(): return lax.all_to_all(value, YC, split_axis=0, concat_axis=0, tiled=True)]
    ppermute x14 -> x20, waiting for transfers between devices: 197 us -> 129 us  [swapped(): return lax.ppermute(value, axes, [(i, count - 1 - i) for i in range(count)])]
    pallas_call x9 -> x23, Pallas kernels: 70.1 us -> 125 us  [the longest x3 30.1 us: backward(): pl.pallas_call(functools.partial(backward_body, steps), grid_spec=pltpu.P...]
    unnamed x76 -> x37, local copies, waits for them, and re-layouts: 38.2 us -> 3.37 us
    all_to_all x5 -> x7, starting transfers between devices: 26.6 us -> 37.8 us  [spread_out(): return lax.all_to_all(value, YC, split_axis=0, concat_axis=0, tiled=True)]
    ppermute x2 -> x3, waiting for transfers between devices: 0.01 us -> 11.1 us  [shifted(): lax.ppermute(value, axis, [(source, source + steps) for source in range(l...]
    broadcast_in_dim x4 -> x0, other arithmetic: 9.18 us -> none  [the longest x1 3.1 us: shards(): grad_two[None]]
    ppermute x14 -> x20, starting transfers between devices: 15.9 us -> 24.7 us  [swapped(): return lax.ppermute(value, axes, [(i, count - 1 - i) for i in range(count)])]
  transfers between devices with their start and end apart: 21 -> 30, of which waited for: 12 -> 21; matrix products, arithmetic and copies ran while one was open for 2% -> 2% of each run, Pallas kernels for 10% -> 32%
where the time goes in v2:
time: 409 us; the launch traced here: 405 us
  waiting for transfers between devices  183 us (45%)
  Pallas kernels  143 us (35%)
  starting transfers between devices  69 us (17%)
  local copies, waits for them, and re-layouts  9.74 us (2%)
    ppermute x20, waiting for transfers between devices, swapped(): return lax.ppermute(value, axes, [(i, count - 1 - i) for i in range(count)])  129 us
    all_to_all x7, waiting for transfers between devices, spread_out(): return lax.all_to_all(value, YC, split_axis=0, concat_axis=0, tiled=True)  42.9 us
    all_to_all x7, starting transfers between devices, spread_out(): return lax.all_to_all(value, YC, split_axis=0, concat_axis=0, tiled=True)  37.8 us
    pallas_call x3, Pallas kernels, backward(): pl.pallas_call(functools.partial(backward_body, steps), grid_spec=pltpu.P...  30.1 us
    pallas_call x6, Pallas kernels, emit(): pl.pallas_call(functools.partial(emit_body, add), grid=(tokens // tile,),...  25.2 us
    ppermute x20, starting transfers between devices, swapped(): return lax.ppermute(value, axes, [(i, count - 1 - i) for i in range(count)])  24.7 us
    pallas_call x3, Pallas kernels, lift(): pl.pallas_call(functools.partial(lift_body, swaps, steps), grid_spec=pltp...  23.2 us
    pallas_call x4, Pallas kernels, wgrad(): pl.pallas_call(functools.partial(wgrad_body, swap, groups, expand, count)...  21.9 us
  transfers between devices with their start and end apart: 30, of which 21 were waited for; matrix products, arithmetic and copies ran while one was open for 2% of the time, Pallas kernels for 32%

profile of v2, /device:TPU:1, one launch (start us, length us, event | category | flops | bytes accessed | tf_op | source)
XLA Modules:
  0.0 405.1 jit_solution(2421800662748267724)
XLA Ops:
  0.6 10.7 %lift.3 = (bf16[8,2,128,1536]{3,2,1,0:T(8,128)(2,1)}, bf16[1024,512]{1,0:T(8,128)(2,1)}, bf16[1024,512]{1,0:T(8,128)(2,1)}) custom-call(s32[1]{0:T(128)} %bitcast.side_ref, bf16[1536,512]{1,0:T(8,128)(2,1)} %bitcast.45, bf16[1536,512]{1,0:T(8,128)(2,1)} %bitcast.38, bf16[2,4,256,256]{3,2,1,0:T(8,128)(2,1)} %bitcast.50, bf16[2,4,256,256]{3,2,1,0:T(8,128)(2,1)} %bitcast.52), custom_call_target="tpu_custom_call" | custom-call | flops 128849016 | bytes 188743 | tf_op jit(solution)/shard_map/lift/pallas_call | solution.py:92
  11.4 6.2 %all-to-all-start = ((bf16[8,2,128,1536]{3,2,1,0:T(8,128)(2,1)}), bf16[8,2,128,1536]{3,2,1,0:T(8,128)(2,1)}, u32[]{:S(2)}, u32[]{:S(2)}) async-start(bf16[8,2,128,1536]{3,2,1,0:T(8,128)(2,1)} %get-tuple-element.57), calls=%async_computation | async-start | bytes 12582912 | tf_op jit(solution)/shard_map/all_to_all | solution.py:342
  20.2 44.7 %collective-permute-done.1.refs_1_ = bf16[2,4,256,128]{3,2,1,0:T(8,128)(2,1)} collective-permute-done((bf16[2,4,256,128]{3,2,1,0:T(8,128)(2,1)S(1)}, bf16[2,4,256,128]{3,2,1,0:T(8,128)(2,1)}, u32[]{:S(2)}, u32[]{:S(2)}) %collective-permute-start.1) | collective-permute-done | bytes 524320 | tf_op jit(solution)/shard_map/ppermute | solution.py:332
  66.2 6.2 %lift.4 = (bf16[8,1,128,1536]{3,2,1,0:T(8,128)(2,1)}, bf16[1024,512]{1,0:T(8,128)(2,1)}) custom-call(s32[1]{0:T(128)} %constant.8.clone.1.side_ref, bf16[1536,512]{1,0:T(8,128)(2,1)} %collective-permute-done.refs_0_.refs_2_, bf16[2,4,256,128]{3,2,1,0:T(8,128)(2,1)} %collective-permute-done.1.refs_1_), custom_call_target="tpu_custom_call" | custom-call | flops 64424508 | bytes 94371 | tf_op jit(solution)/shard_map/lift/pallas_call | solution.py:92
  72.4 16.4 %collective-permute-done.2 = bf16[1024,512]{1,0:T(8,128)(2,1)} collective-permute-done((bf16[1024,512]{1,0:T(8,128)(2,1)}, bf16[1024,512]{1,0:T(8,128)(2,1)}, u32[]{:S(2)}, u32[]{:S(2)}) %collective-permute-start.2) | collective-permute-done | bytes 1048608 | tf_op jit(solution)/shard_map/ppermute | solution.py:332
  89.0 6.2 %all-to-all-start.1 = ((bf16[8,1,128,1536]{3,2,1,0:T(8,128)(2,1)}), bf16[8,1,128,1536]{3,2,1,0:T(8,128)(2,1)}, u32[]{:S(2)}, u32[]{:S(2)}) async-start(bf16[8,1,128,1536]{3,2,1,0:T(8,128)(2,1)} %get-tuple-element.59), calls=%async_computation.1 | async-start | bytes 6291456 | tf_op jit(solution)/shard_map/all_to_all | solution.py:342
  99.1 9.6 %collective-permute-done.3 = bf16[512,512]{1,0:T(8,128)(2,1)S(1)} collective-permute-done((bf16[512,512]{1,0:T(8,128)(2,1)S(1)}, bf16[512,512]{1,0:T(8,128)(2,1)S(1)}, u32[]{:S(2)}, u32[]{:S(2)}) %collective-permute-start.3) | collective-permute-done | bytes 524320 | tf_op jit(solution)/shard_map/ppermute | solution.py:332
  108.8 11.2 %collective-permute-done.4.refs_1_ = bf16[2,4,128,256]{3,2,1,0:T(8,128)(2,1)} collective-permute-done((bf16[2,4,128,256]{3,2,1,0:T(8,128)(2,1)S(1)}, bf16[2,4,128,256]{3,2,1,0:T(8,128)(2,1)}, u32[]{:S(2)}, u32[]{:S(2)}) %collective-permute-start.4) | collective-permute-done | bytes 524320 | tf_op jit(solution)/shard_map/ppermute | solution.py:332
  120.0 6.2 %lift.5 = (bf16[8,1,128,1536]{3,2,1,0:T(8,128)(2,1)}, bf16[1024,512]{1,0:T(8,128)(2,1)}) custom-call(s32[1]{0:T(128)} %constant.8.clone.1.side_ref, bf16[1536,512]{1,0:T(8,128)(2,1)} %copy-done.2, bf16[2,4,128,256]{3,2,1,0:T(8,128)(2,1)} %collective-permute-done.4.refs_1_), custom_call_target="tpu_custom_call" | custom-call | flops 64424508 | bytes 94371 | tf_op jit(solution)/shard_map/lift/pallas_call | solution.py:92
  126.2 6.6 %all-to-all-done.1 = bf16[8,1,128,1536]{3,2,1,0:T(8,128)(2,1)} async-done(((bf16[8,1,128,1536]{3,2,1,0:T(8,128)(2,1)}), bf16[8,1,128,1536]{3,2,1,0:T(8,128)(2,1)}, u32[]{:S(2)}, u32[]{:S(2)}) %all-to-all-start.1) | async-done | bytes 3145760 | tf_op jit(solution)/shard_map/all_to_all | solution.py:342
  132.8 5.3 %all-to-all-start.2 = ((bf16[8,1,128,1536]{3,2,1,0:T(8,128)(2,1)}), bf16[8,1,128,1536]{3,2,1,0:T(8,128)(2,1)}, u32[]{:S(2)}, u32[]{:S(2)}) async-start(bf16[8,1,128,1536]{3,2,1,0:T(8,128)(2,1)} %get-tuple-element.61), calls=%async_computation.2 | async-start | bytes 6291456 | tf_op jit(solution)/shard_map/all_to_all | solution.py:342
  143.4 17.4 %forward.1 = bf16[8,2,8,16,1536]{4,3,2,1,0:T(8,128)(2,1)} custom-call(s32[1]{0:T(128)} %bitcast.side_ref, bf16[8,2,8,16,1536]{4,3,2,1,0:T(8,128)(2,1)} %bitcast.11.ro_ref.go_ref, bf16[8,1,8,16,1536]{4,3,2,1,0:T(8,128)(2,1)} %bitcast.12.rp_ref, bf16[8,256,256]{2,1,0:T(8,128)(2,1)} %bitcast.30, bf16[8,256,256]{2,1,0:T(8,128)(2,1)} %bitcast.34), custom_call_target="tpu_custom_call" | custom-call | flops 64424508 | bytes 251658 | tf_op jit(solution)/shard_map/forward/pallas_call | solution.py:145
  160.8 15.0 %all-to-all-done.2 = bf16[8,1,128,1536]{3,2,1,0:T(8,128)(2,1)} async-done(((bf16[8,1,128,1536]{3,2,1,0:T(8,128)(2,1)}), bf16[8,1,128,1536]{3,2,1,0:T(8,128)(2,1)}, u32[]{:S(2)}, u32[]{:S(2)}) %all-to-all-start.2) | async-done | bytes 3145760 | tf_op jit(solution)/shard_map/all_to_all | solution.py:342
  175.9 5.5 %all-to-all-start.3 = ((bf16[8,2,128,1536]{3,2,1,0:T(8,128)(2,1)}), bf16[8,2,128,1536]{3,2,1,0:T(8,128)(2,1)}, u32[]{:S(2)}, u32[]{:S(2)}) async-start(bf16[8,2,128,1536]{3,2,1,0:T(8,128)(2,1)} %bitcast.29), calls=%async_computation.3 | async-start | bytes 12582912 | tf_op jit(solution)/shard_map/all_to_all | solution.py:342
  181.4 10.9 %backward.3 = (bf16[8,8,16,1536]{3,2,1,0:T(8,128)(2,1)}, bf16[3,256,256]{2,1,0:T(8,128)(2,1)}, bf16[3,256,256]{2,1,0:T(8,128)(2,1)}, bf16[8,8,16,768]{3,2,1,0:T(8,128)(2,1)}, bf16[8,8,16,768]{3,2,1,0:T(8,128)(2,1)}) custom-call(s32[1]{0:T(128)} %bitcast.side_ref, bf16[8,2,8,16,1536]{4,3,2,1,0:T(8,128)(2,1)} %bitcast.11.ro_ref.go_ref, ...), custom_call_target="tpu_custom_call" | custom-call | flops 60397976 | bytes 141557 | tf_op jit(solution)/shard_map/backward/pallas_call | solution.py:217
  192.3 2.9 collective-permute-start.7
  195.4 11.0 %backward.4 = (bf16[8,8,16,1536]{3,2,1,0:T(8,128)(2,1)}, bf16[3,256,256]{2,1,0:T(8,128)(2,1)}, bf16[3,256,256]{2,1,0:T(8,128)(2,1)}, bf16[8,8,16,768]{3,2,1,0:T(8,128)(2,1)}, bf16[8,8,16,768]{3,2,1,0:T(8,128)(2,1)}) custom-call(s32[1]{0:T(128)} %bitcast.side_ref, ...), custom_call_target="tpu_custom_call", output_to_operand_aliasing={{0}: (7, {}), {3}: (8, {}), {4}: (9, {})} | custom-call | flops 60397976 | bytes 141557 | tf_op jit(solution)/shard_map/backward/pallas_call | solution.py:217
  206.5 2.8 collective-permute-start.11
  209.5 3.6 collective-permute-done.8.refs_1_
  213.1 8.2 %backward.5 = (bf16[8,8,16,1536]{3,2,1,0:T(8,128)(2,1)}, bf16[2,256,256]{2,1,0:T(8,128)(2,1)}, bf16[2,256,256]{2,1,0:T(8,128)(2,1)}, bf16[8,8,16,768]{3,2,1,0:T(8,128)(2,1)}, bf16[8,8,16,768]{3,2,1,0:T(8,128)(2,1)}) custom-call(s32[1]{0:T(128)} %bitcast.side_ref, ...), custom_call_target="tpu_custom_call", output_to_operand_aliasing={{0}: (7, {}), {3}: (8, {}), {4}: (9, {})} | custom-call | flops 40265320 | bytes 94371 | tf_op jit(solution)/shard_map/backward/pallas_call | solution.py:217
  221.3 3.0 collective-permute-start.10
  224.3 5.6 %collective-permute-done.9.refs_3_ = bf16[3,256,256]{2,1,0:T(8,128)(2,1)S(1)} collective-permute-done((bf16[3,256,256]{2,1,0:T(8,128)(2,1)}, bf16[3,256,256]{2,1,0:T(8,128)(2,1)S(1)}, u32[]{:S(2)}, u32[]{:S(2)}) %collective-permute-start.9) | collective-permute-done | bytes 393248 | tf_op jit(solution)/shard_map/ppermute | solution.py:332
  229.9 5.6 %collective-permute-done.10.refs_5_ = bf16[2,256,256]{2,1,0:T(8,128)(2,1)S(1)} collective-permute-done((bf16[2,256,256]{2,1,0:T(8,128)(2,1)}, bf16[2,256,256]{2,1,0:T(8,128)(2,1)S(1)}, u32[]{:S(2)}, u32[]{:S(2)}) %collective-permute-start.10) | collective-permute-done | bytes 262176 | tf_op jit(solution)/shard_map/ppermute | solution.py:332
  235.5 5.7 %collective-permute-done.12.refs_5_ = bf16[2,256,256]{2,1,0:T(8,128)(2,1)S(1)} collective-permute-done((bf16[2,256,256]{2,1,0:T(8,128)(2,1)}, bf16[2,256,256]{2,1,0:T(8,128)(2,1)S(1)}, u32[]{:S(2)}, u32[]{:S(2)}) %collective-permute-start.12) | collective-permute-done | bytes 262176 | tf_op jit(solution)/shard_map/ppermute | solution.py:332
  241.3 11.5 %all-to-all-done.3.s_ref.refs_0_.refs_1_ = bf16[8,2,128,1536]{3,2,1,0:T(8,128)(2,1)} async-done(((bf16[8,2,128,1536]{3,2,1,0:T(8,128)(2,1)}), bf16[8,2,128,1536]{3,2,1,0:T(8,128)(2,1)}, u32[]{:S(2)}, u32[]{:S(2)}) %all-to-all-start.3) | async-done | bytes 6291488 | tf_op jit(solution)/shard_map/all_to_all | solution.py:342
  252.8 5.2 %all-to-all-start.4 = ((bf16[8,1,128,1536]{3,2,1,0:T(8,128)(2,1)}), bf16[8,1,128,1536]{3,2,1,0:T(8,128)(2,1)}, u32[]{:S(2)}, u32[]{:S(2)}) async-start(bf16[8,1,128,1536]{3,2,1,0:T(8,128)(2,1)} %bitcast.28), calls=%async_computation.4 | async-start | bytes 6291456 | tf_op jit(solution)/shard_map/all_to_all | solution.py:342
  258.0 4.7 %emit.6 = bf16[1536,512]{1,0:T(8,128)(2,1)} custom-call(bf16[8,2,128,1536]{3,2,1,0:T(8,128)(2,1)} %all-to-all-done.3.s_ref.refs_0_.refs_1_, bf16[512,1024]{1,0:T(8,128)(2,1)} %bitcast.49), custom_call_target="tpu_custom_call" | custom-call | flops 32212254 | bytes 125829 | tf_op jit(solution)/shard_map/emit/pallas_call | solution.py:252
  264.0 6.2 %join.3 = f32[8,256,256]{2,1,0:T(8,128)} custom-call(bf16[3,256,256]{2,1,0:T(8,128)(2,1)} %get-tuple-element.64.refs_0_, bf16[3,256,256]{2,1,0:T(8,128)(2,1)} %copy-done.13, bf16[3,256,256]{2,1,0:T(8,128)(2,1)} %get-tuple-element.77.refs_2_, bf16[3,256,256]{2,1,0:T(8,128)(2,1)} %copy-done.15, bf16[2,256,256]{2,1,0:T(8,128)(2,1)} %get-tuple-element.78.refs_4_, ...), custom_call_target="tpu_custom_call" | custom-call | tf_op jit(solution)/shard_map/join/pallas_call | solution.py:374
  270.2 6.2 %join.2 = f32[8,256,256]{2,1,0:T(8,128)} custom-call(bf16[3,256,256]{2,1,0:T(8,128)(2,1)} %get-tuple-element.63.refs_0_, bf16[3,256,256]{2,1,0:T(8,128)(2,1)} %copy-done.12, bf16[3,256,256]{2,1,0:T(8,128)(2,1)} %get-tuple-element.75.refs_2_, bf16[3,256,256]{2,1,0:T(8,128)(2,1)} %copy-done.14, bf16[2,256,256]{2,1,0:T(8,128)(2,1)} %get-tuple-element.76.refs_4_, ...), custom_call_target="tpu_custom_call" | custom-call | tf_op jit(solution)/shard_map/join/pallas_call | solution.py:374
  276.4 5.5 %wgrad.4.ma_ref = bf16[2,4,128,256]{3,2,1,0:T(8,128)(2,1)} custom-call(bf16[8,2,128,1536]{3,2,1,0:T(8,128)(2,1)} %all-to-all-done.3.s_ref.refs_0_.refs_1_, bf16[8,2,128,1536]{3,2,1,0:T(8,128)(2,1)} %all-to-all-done.3.s_ref.refs_0_.refs_1_, bf16[1536,512]{1,0:T(8,128)(2,1)} %bitcast.39), custom_call_target="tpu_custom_call" | custom-call | flops 32212254 | bytes 94371 | tf_op jit(solution)/shard_map/wgrad/pallas_call | solution.py:313
  281.9 5.5 %wgrad.5 = bf16[2,4,128,256]{3,2,1,0:T(8,128)(2,1)} custom-call(bf16[8,2,128,1536]{3,2,1,0:T(8,128)(2,1)} %all-to-all-done.3.s_ref.refs_0_.refs_1_, bf16[8,2,128,1536]{3,2,1,0:T(8,128)(2,1)} %all-to-all-done.3.s_ref.refs_0_.refs_1_, bf16[1536,512]{1,0:T(8,128)(2,1)} %copy-done.2), custom_call_target="tpu_custom_call" | custom-call | flops 32212254 | bytes 94371 | tf_op jit(solution)/shard_map/wgrad/pallas_call | solution.py:313
  287.3 8.4 %all-to-all-done.4.s_ref.refs_0_.refs_1_ = bf16[8,1,128,1536]{3,2,1,0:T(8,128)(2,1)} async-done(((bf16[8,1,128,1536]{3,2,1,0:T(8,128)(2,1)}), bf16[8,1,128,1536]{3,2,1,0:T(8,128)(2,1)}, u32[]{:S(2)}, u32[]{:S(2)}) %all-to-all-start.4) | async-done | bytes 3145760 | tf_op jit(solution)/shard_map/all_to_all | solution.py:342
  295.7 4.4 %all-to-all-start.5 = ((bf16[8,1,128,768]{3,2,1,0:T(8,128)(2,1)}), bf16[8,1,128,768]{3,2,1,0:T(8,128)(2,1)S(1)}, u32[]{:S(2)}, u32[]{:S(2)}) async-start(bf16[8,1,128,768]{3,2,1,0:T(8,128)(2,1)} %bitcast.19), calls=%async_computation.5 | async-start | bytes 3145728 | tf_op jit(solution)/shard_map/all_to_all | solution.py:342
  303.2 5.2 %emit.7 = bf16[1536,512]{1,0:T(8,128)(2,1)} custom-call(bf16[8,2,128,1536]{3,2,1,0:T(8,128)(2,1)} %all-to-all-done.3.s_ref.refs_0_.refs_1_, bf16[512,1024]{1,0:T(8,128)(2,1)} %bitcast.48, bf16[1536,512]{1,0:T(8,128)(2,1)} %collective-permute-done.5.rest_0_), custom_call_target="tpu_custom_call" | custom-call | flops 32212254 | bytes 125829 | tf_op jit(solution)/shard_map/emit/pallas_call | solution.py:252
  308.4 3.6 emit.9
  315.9 3.6 emit.8
  321.9 5.0 %all-to-all-start.6 = ((bf16[8,1,128,768]{3,2,1,0:T(8,128)(2,1)}), bf16[8,1,128,768]{3,2,1,0:T(8,128)(2,1)}, u32[]{:S(2)}, u32[]{:S(2)}) async-start(bf16[8,1,128,768]{3,2,1,0:T(8,128)(2,1)} %bitcast.18), calls=%async_computation.6 | async-start | bytes 3145728 | tf_op jit(solution)/shard_map/all_to_all | solution.py:342
  327.0 3.9 collective-permute-start.6
  330.9 3.0 collective-permute-done.15.rest_0_
  334.2 16.5 %collective-permute-done.16.rest_0_ = bf16[768,512]{1,0:T(8,128)(2,1)S(1)} collective-permute-done((bf16[768,512]{1,0:T(8,128)(2,1)S(1)}, bf16[768,512]{1,0:T(8,128)(2,1)S(1)}, u32[]{:S(2)}, u32[]{:S(2)}) %collective-permute-start.16) | collective-permute-done | bytes 786464 | tf_op jit(solution)/shard_map/ppermute | solution.py:332
  353.7 5.5 %wgrad.6 = bf16[2,4,256,128]{3,2,1,0:T(8,128)(2,1)} custom-call(bf16[8,1,128,1536]{3,2,1,0:T(8,128)(2,1)} %all-to-all-done.4.s_ref.refs_0_.refs_1_, bf16[8,1,128,1536]{3,2,1,0:T(8,128)(2,1)} %all-to-all-done.4.s_ref.refs_0_.refs_1_, bf16[1536,512]{1,0:T(8,128)(2,1)} %collective-permute-done.refs_0_.refs_2_), custom_call_target="tpu_custom_call" | custom-call | flops 32212254 | bytes 94371 | tf_op jit(solution)/shard_map/wgrad/pallas_call | solution.py:313
  359.2 4.0 emit.11
  364.5 4.0 emit.10
  369.8 5.5 %wgrad.7.ma_ref = bf16[2,4,256,128]{3,2,1,0:T(8,128)(2,1)} custom-call(bf16[8,1,128,768]{3,2,1,0:T(8,128)(2,1)} %copy-done.1, bf16[8,1,128,768]{3,2,1,0:T(8,128)(2,1)} %all-to-all-done.6.s_ref.refs_1_, bf16[1536,512]{1,0:T(8,128)(2,1)} %bitcast.47), custom_call_target="tpu_custom_call" | custom-call | flops 32212254 | bytes 94371 | tf_op jit(solution)/shard_map/wgrad/pallas_call | solution.py:313
  378.5 2.7 place.3
  381.2 2.9 paired.3
  387.4 11.1 %collective-permute-done.17.value_ref = bf16[768,512]{1,0:T(8,128)(2,1)} collective-permute-done((bf16[768,512]{1,0:T(8,128)(2,1)}, bf16[768,512]{1,0:T(8,128)(2,1)}, u32[]{:S(2)}, u32[]{:S(2)}) %collective-permute-start.17) | collective-permute-done | bytes 786464 | tf_op jit(solution)/shard_map/ppermute | solution.py:338
  402.1 2.9 paired.2
  (82 shorter events, 40.7 us)
Async XLA Ops:
  11.4 7.5 %copy-start.3 = (bf16[1,2,4,256,256]{4,3,2,1,0:T(8,128)(2,1)S(1)}, bf16[1,2,4,256,256]{4,3,2,1,0:T(8,128)(2,1)}, u32[]{:S(2)}) copy-start(bf16[1,2,4,256,256]{4,3,2,1,0:T(8,128)(2,1)} %param.8) | copy-start | bytes 3145732
  11.4 77.6 %all-to-all-start = ((bf16[8,2,128,1536]{3,2,1,0:T(8,128)(2,1)}), bf16[8,2,128,1536]{3,2,1,0:T(8,128)(2,1)}, u32[]{:S(2)}, u32[]{:S(2)}) async-start(bf16[8,2,128,1536]{3,2,1,0:T(8,128)(2,1)} %get-tuple-element.57), calls=%async_computation | async-start | bytes 12582912 | tf_op jit(solution)/shard_map/all_to_all | solution.py:342
  17.6 1.6 copy-start
  17.6 47.3 %collective-permute-start = (bf16[1536,512]{1,0:T(8,128)(2,1)}, bf16[1536,512]{1,0:T(8,128)(2,1)}, u32[]{:S(2)}, u32[]{:S(2)}) collective-permute-start(bf16[1536,512]{1,0:T(8,128)(2,1)} %bitcast.46), channel_id=1, source_target_pairs={{0,8},{8,0},{1,9},{9,1},{2,10},{10,2},{3,11},{11,3},{4,12},{12,4},... | collective-permute-start | bytes 4718600 | tf_op jit(solution)/shard_map/ppermute | solution.py:332
  18.9 46.0 %collective-permute-start.1 = (bf16[2,4,256,128]{3,2,1,0:T(8,128)(2,1)S(1)}, bf16[2,4,256,128]{3,2,1,0:T(8,128)(2,1)}, u32[]{:S(2)}, u32[]{:S(2)}) collective-permute-start(bf16[2,4,256,128]{3,2,1,0:T(8,128)(2,1)S(1)} %slice_select_fusion.1), channel_id=1, source_target_pairs={{0,8},{8,0},{1,9},{9,1},{2,10},{10,2},{3,11},{11,3},{4,12},{12,4},... | collective-permute-start | bytes 1572872 | tf_op jit(solution)/shard_map/ppermute | solution.py:332
  64.9 23.9 %collective-permute-start.2 = (bf16[1024,512]{1,0:T(8,128)(2,1)}, bf16[1024,512]{1,0:T(8,128)(2,1)}, u32[]{:S(2)}, u32[]{:S(2)}) collective-permute-start(bf16[1024,512]{1,0:T(8,128)(2,1)} %slice_bitcast_fusion), channel_id=1, source_target_pairs={{0,8},{8,0},{1,9},{9,1},{2,10},{10,2},{3,11},{11,3},{4,12},{12,4},... | collective-permute-start | bytes 3145736 | tf_op jit(solution)/shard_map/ppermute | solution.py:332
  89.0 43.9 %all-to-all-start.1 = ((bf16[8,1,128,1536]{3,2,1,0:T(8,128)(2,1)}), bf16[8,1,128,1536]{3,2,1,0:T(8,128)(2,1)}, u32[]{:S(2)}, u32[]{:S(2)}) async-start(bf16[8,1,128,1536]{3,2,1,0:T(8,128)(2,1)} %get-tuple-element.59), calls=%async_computation.1 | async-start | bytes 6291456 | tf_op jit(solution)/shard_map/all_to_all | solution.py:342
  95.1 1.4 copy-start.4
  95.2 13.6 %collective-permute-start.3 = (bf16[512,512]{1,0:T(8,128)(2,1)S(1)}, bf16[512,512]{1,0:T(8,128)(2,1)S(1)}, u32[]{:S(2)}, u32[]{:S(2)}) collective-permute-start(bf16[512,512]{1,0:T(8,128)(2,1)S(1)} %slice_bitcast_fusion.1), channel_id=1, source_target_pairs={{0,8},{8,0},{1,9},{9,1},{2,10},{10,2},{3,11},{11,3},{4,12},{12,4},... | collective-permute-start | bytes 1572872 | tf_op jit(solution)/shard_map/ppermute | solution.py:332
  96.6 23.4 %collective-permute-start.4 = (bf16[2,4,128,256]{3,2,1,0:T(8,128)(2,1)S(1)}, bf16[2,4,128,256]{3,2,1,0:T(8,128)(2,1)}, u32[]{:S(2)}, u32[]{:S(2)}) collective-permute-start(bf16[2,4,128,256]{3,2,1,0:T(8,128)(2,1)S(1)} %slice_select_fusion), channel_id=1, source_target_pairs={{0,8},{8,0},{1,9},{9,1},{2,10},{10,2},{3,11},{11,3},{4,12},{12,4},... | collective-permute-start | bytes 1572872 | tf_op jit(solution)/shard_map/ppermute | solution.py:332
  108.8 11.2 %copy-start.2 = (bf16[1536,512]{1,0:T(8,128)(2,1)}, bf16[1536,512]{1,0:T(8,128)(2,1)S(1)}, u32[]{:S(2)}) copy-start(bf16[1536,512]{1,0:T(8,128)(2,1)S(1)} %constant_dynamic-update-slice_fusion.refs_0_.refs_2_) | copy-start | bytes 4718596
  132.8 5.4 %copy-start.7 = (bf16[1024,512]{1,0:T(8,128)(2,1)S(1)}, bf16[1024,512]{1,0:T(8,128)(2,1)}, u32[]{:S(2)}) copy-start(bf16[1024,512]{1,0:T(8,128)(2,1)} %get-tuple-element.49) | copy-start | bytes 3145732
  132.8 43.0 %all-to-all-start.2 = ((bf16[8,1,128,1536]{3,2,1,0:T(8,128)(2,1)}), bf16[8,1,128,1536]{3,2,1,0:T(8,128)(2,1)}, u32[]{:S(2)}, u32[]{:S(2)}) async-start(bf16[8,1,128,1536]{3,2,1,0:T(8,128)(2,1)} %get-tuple-element.61), calls=%async_computation.2 | async-start | bytes 6291456 | tf_op jit(solution)/shard_map/all_to_all | solution.py:342
  138.2 1.3 copy-start.6
  139.5 1.3 copy-start.8
  140.8 1.3 copy-start.9
  175.9 76.9 %all-to-all-start.3 = ((bf16[8,2,128,1536]{3,2,1,0:T(8,128)(2,1)}), bf16[8,2,128,1536]{3,2,1,0:T(8,128)(2,1)}, u32[]{:S(2)}, u32[]{:S(2)}) async-start(bf16[8,2,128,1536]{3,2,1,0:T(8,128)(2,1)} %bitcast.29), calls=%async_computation.3 | async-start | bytes 12582912 | tf_op jit(solution)/shard_map/all_to_all | solution.py:342
  192.3 17.2 %collective-permute-start.7 = (bf16[3,256,256]{2,1,0:T(8,128)(2,1)}, bf16[3,256,256]{2,1,0:T(8,128)(2,1)S(1)}, u32[]{:S(2)}, u32[]{:S(2)}) collective-permute-start(bf16[3,256,256]{2,1,0:T(8,128)(2,1)} %get-tuple-element.63.refs_0_), channel_id=1, source_target_pairs={{0,64},{64,0},{1,65},{65,1},{2,66},{66,2},{3,67},{67,3},{4,68},{68... | collective-permute-start | bytes 1179656 | tf_op jit(solution)/shard_map/ppermute | solution.py:332
  195.2 17.9 %collective-permute-start.8 = (bf16[3,256,256]{2,1,0:T(8,128)(2,1)}, bf16[3,256,256]{2,1,0:T(8,128)(2,1)S(1)}, u32[]{:S(2)}, u32[]{:S(2)}) collective-permute-start(bf16[3,256,256]{2,1,0:T(8,128)(2,1)} %get-tuple-element.64.refs_0_), channel_id=1, source_target_pairs={{0,64},{64,0},{1,65},{65,1},{2,66},{66,2},{3,67},{67,3},{4,68},{68... | collective-permute-start | bytes 1179656 | tf_op jit(solution)/shard_map/ppermute | solution.py:332
  206.5 17.9 %collective-permute-start.11 = (bf16[3,256,256]{2,1,0:T(8,128)(2,1)}, bf16[3,256,256]{2,1,0:T(8,128)(2,1)S(1)}, u32[]{:S(2)}, u32[]{:S(2)}) collective-permute-start(bf16[3,256,256]{2,1,0:T(8,128)(2,1)} %get-tuple-element.77.refs_2_), channel_id=1, source_target_pairs={{0,64},{64,0},{1,65},{65,1},{2,66},{66,2},{3,67},{67,3},{4,68},{68... | collective-permute-start | bytes 1179656 | tf_op jit(solution)/shard_map/ppermute | solution.py:332
  209.2 20.7 %collective-permute-start.9 = (bf16[3,256,256]{2,1,0:T(8,128)(2,1)}, bf16[3,256,256]{2,1,0:T(8,128)(2,1)S(1)}, u32[]{:S(2)}, u32[]{:S(2)}) collective-permute-start(bf16[3,256,256]{2,1,0:T(8,128)(2,1)} %get-tuple-element.75.refs_2_), channel_id=1, source_target_pairs={{0,64},{64,0},{1,65},{65,1},{2,66},{66,2},{3,67},{67,3},{4,68},{68... | collective-permute-start | bytes 1179656 | tf_op jit(solution)/shard_map/ppermute | solution.py:332
  209.5 11.8 %copy-start.12 = (bf16[3,256,256]{2,1,0:T(8,128)(2,1)}, bf16[3,256,256]{2,1,0:T(8,128)(2,1)S(1)}, u32[]{:S(2)}) copy-start(bf16[3,256,256]{2,1,0:T(8,128)(2,1)S(1)} %collective-permute-done.7.refs_1_) | copy-start | bytes 1179652
  213.1 8.2 %copy-start.13 = (bf16[3,256,256]{2,1,0:T(8,128)(2,1)}, bf16[3,256,256]{2,1,0:T(8,128)(2,1)S(1)}, u32[]{:S(2)}) copy-start(bf16[3,256,256]{2,1,0:T(8,128)(2,1)S(1)} %collective-permute-done.8.refs_1_) | copy-start | bytes 1179652
  221.3 14.3 %collective-permute-start.10 = (bf16[2,256,256]{2,1,0:T(8,128)(2,1)}, bf16[2,256,256]{2,1,0:T(8,128)(2,1)S(1)}, u32[]{:S(2)}, u32[]{:S(2)}) collective-permute-start(bf16[2,256,256]{2,1,0:T(8,128)(2,1)} %get-tuple-element.76.refs_4_), channel_id=1, source_target_pairs={{0,64},{64,0},{1,65},{65,1},{2,66},{66,2},{3,67},{67,3},{4,68},{68... | collective-permute-start | bytes 786440 | tf_op jit(solution)/shard_map/ppermute | solution.py:332
  224.2 17.0 %collective-permute-start.12 = (bf16[2,256,256]{2,1,0:T(8,128)(2,1)}, bf16[2,256,256]{2,1,0:T(8,128)(2,1)S(1)}, u32[]{:S(2)}, u32[]{:S(2)}) collective-permute-start(bf16[2,256,256]{2,1,0:T(8,128)(2,1)} %get-tuple-element.78.refs_4_), channel_id=1, source_target_pairs={{0,64},{64,0},{1,65},{65,1},{2,66},{66,2},{3,67},{67,3},{4,68},{68... | collective-permute-start | bytes 786440 | tf_op jit(solution)/shard_map/ppermute | solution.py:332
  224.3 28.4 %copy-start.15 = (bf16[3,256,256]{2,1,0:T(8,128)(2,1)}, bf16[3,256,256]{2,1,0:T(8,128)(2,1)S(1)}, u32[]{:S(2)}) copy-start(bf16[3,256,256]{2,1,0:T(8,128)(2,1)S(1)} %collective-permute-done.11.refs_3_) | copy-start | bytes 1179652
  229.9 22.9 %copy-start.14 = (bf16[3,256,256]{2,1,0:T(8,128)(2,1)}, bf16[3,256,256]{2,1,0:T(8,128)(2,1)S(1)}, u32[]{:S(2)}) copy-start(bf16[3,256,256]{2,1,0:T(8,128)(2,1)S(1)} %collective-permute-done.9.refs_3_) | copy-start | bytes 1179652
  235.5 17.2 %copy-start.16 = (bf16[2,256,256]{2,1,0:T(8,128)(2,1)}, bf16[2,256,256]{2,1,0:T(8,128)(2,1)S(1)}, u32[]{:S(2)}) copy-start(bf16[2,256,256]{2,1,0:T(8,128)(2,1)S(1)} %collective-permute-done.10.refs_5_) | copy-start | bytes 786436
  241.3 11.5 %copy-start.17 = (bf16[2,256,256]{2,1,0:T(8,128)(2,1)}, bf16[2,256,256]{2,1,0:T(8,128)(2,1)S(1)}, u32[]{:S(2)}) copy-start(bf16[2,256,256]{2,1,0:T(8,128)(2,1)S(1)} %collective-permute-done.12.refs_5_) | copy-start | bytes 786436
  252.8 42.9 %all-to-all-start.4 = ((bf16[8,1,128,1536]{3,2,1,0:T(8,128)(2,1)}), bf16[8,1,128,1536]{3,2,1,0:T(8,128)(2,1)}, u32[]{:S(2)}, u32[]{:S(2)}) async-start(bf16[8,1,128,1536]{3,2,1,0:T(8,128)(2,1)} %bitcast.28), calls=%async_computation.4 | async-start | bytes 6291456 | tf_op jit(solution)/shard_map/all_to_all | solution.py:342
  262.7 37.3 %collective-permute-start.5 = (bf16[1536,512]{1,0:T(8,128)(2,1)}, bf16[1536,512]{1,0:T(8,128)(2,1)}, u32[]{:S(2)}, u32[]{:S(2)}) collective-permute-start(bf16[1536,512]{1,0:T(8,128)(2,1)} %emit.6), channel_id=1, source_target_pairs={{0,8},{8,0},{1,9},{9,1},{2,10},{10,2},{3,11},{11,3},{4,12},{12,4},... | collective-permute-start | bytes 4718600 | tf_op jit(solution)/shard_map/ppermute | solution.py:332
  295.7 25.1 %all-to-all-start.5 = ((bf16[8,1,128,768]{3,2,1,0:T(8,128)(2,1)}), bf16[8,1,128,768]{3,2,1,0:T(8,128)(2,1)S(1)}, u32[]{:S(2)}, u32[]{:S(2)}) async-start(bf16[8,1,128,768]{3,2,1,0:T(8,128)(2,1)} %bitcast.19), calls=%async_computation.5 | async-start | bytes 3145728 | tf_op jit(solution)/shard_map/all_to_all | solution.py:342
  300.1 13.7 %collective-permute-start.13 = (bf16[2,4,128,256]{3,2,1,0:T(8,128)(2,1)}, bf16[2,4,128,256]{3,2,1,0:T(8,128)(2,1)}, u32[]{:S(2)}, u32[]{:S(2)}) collective-permute-start(bf16[2,4,128,256]{3,2,1,0:T(8,128)(2,1)} %wgrad.5), channel_id=1, source_target_pairs={{0,8},{8,0},{1,9},{9,1},{2,10},{10,2},{3,11},{11,3},{4,12},{12,4},... | collective-permute-start | bytes 1572872 | tf_op jit(solution)/shard_map/ppermute | solution.py:332
  301.4 14.5 %collective-permute-start.14 = (bf16[2,4,128,256]{3,2,1,0:T(8,128)(2,1)}, bf16[2,4,128,256]{3,2,1,0:T(8,128)(2,1)}, u32[]{:S(2)}, u32[]{:S(2)}) collective-permute-start(bf16[2,4,128,256]{3,2,1,0:T(8,128)(2,1)} %wgrad.5), channel_id=1, source_target_pairs={{0,72},{8,64},{64,8},{72,0},{1,73},{9,65},{65,9},{73,1},{2,74},{10... | collective-permute-start | bytes 1572872 | tf_op jit(solution)/shard_map/ppermute | solution.py:332
  315.9 18.0 %collective-permute-start.15 = (bf16[768,512]{1,0:T(8,128)(2,1)}, bf16[768,512]{1,0:T(8,128)(2,1)}, u32[]{:S(2)}, u32[]{:S(2)}) collective-permute-start(bf16[768,512]{1,0:T(8,128)(2,1)} %emit.9), channel_id=1, source_target_pairs={{0,8},{8,0},{1,9},{9,1},{2,10},{10,2},{3,11},{11,3},{4,12},{12,4},... | collective-permute-start | bytes 2359304 | tf_op jit(solution)/shard_map/ppermute | solution.py:332
  320.8 1.1 copy-start.1
  320.8 13.1 %copy-start.10 = (bf16[768,512]{1,0:T(8,128)(2,1)S(1)}, bf16[768,512]{1,0:T(8,128)(2,1)}, u32[]{:S(2)}) copy-start(bf16[768,512]{1,0:T(8,128)(2,1)} %emit.8) | copy-start | bytes 2359300
  321.9 42.5 %all-to-all-start.6 = ((bf16[8,1,128,768]{3,2,1,0:T(8,128)(2,1)}), bf16[8,1,128,768]{3,2,1,0:T(8,128)(2,1)}, u32[]{:S(2)}, u32[]{:S(2)}) async-start(bf16[8,1,128,768]{3,2,1,0:T(8,128)(2,1)} %bitcast.18), calls=%async_computation.6 | async-start | bytes 3145728 | tf_op jit(solution)/shard_map/all_to_all | solution.py:342
  327.0 49.1 %collective-permute-start.6 = (bf16[1536,512]{1,0:T(8,128)(2,1)}, bf16[1536,512]{1,0:T(8,128)(2,1)S(1)}, u32[]{:S(2)}, u32[]{:S(2)}) collective-permute-start(bf16[1536,512]{1,0:T(8,128)(2,1)} %emit.7), channel_id=1, source_target_pairs={{0,16},{16,32},{32,48},{1,17},{17,33},{33,49},{2,18},{18,34},{34,5... | collective-permute-start | bytes 4718600 | tf_op jit(solution)/shard_map/ppermute | solution.py:338
  333.9 16.8 %collective-permute-start.16 = (bf16[768,512]{1,0:T(8,128)(2,1)S(1)}, bf16[768,512]{1,0:T(8,128)(2,1)S(1)}, u32[]{:S(2)}, u32[]{:S(2)}) collective-permute-start(bf16[768,512]{1,0:T(8,128)(2,1)S(1)} %copy-done.10), channel_id=1, source_target_pairs={{0,8},{8,0},{1,9},{9,1},{2,10},{10,2},{3,11},{11,3},{4,12},{12,4},... | collective-permute-start | bytes 2359304 | tf_op jit(solution)/shard_map/ppermute | solution.py:332
  350.7 0.9 copy-start.11
  351.6 25.1 %collective-permute-start.22 = (bf16[2,4,128,256]{3,2,1,0:T(8,128)(2,1)}, bf16[2,4,128,256]{3,2,1,0:T(8,128)(2,1)}, u32[]{:S(2)}, u32[]{:S(2)}) collective-permute-start(bf16[2,4,128,256]{3,2,1,0:T(8,128)(2,1)} %wgrad.4.ma_ref), channel_id=1, source_target_pairs={{0,64},{64,0},{1,65},{65,1},{2,66},{66,2},{3,67},{67,3},{4,68},{68... | collective-permute-start | bytes 1572872 | tf_op jit(solution)/shard_map/ppermute | solution.py:332
  363.2 20.9 %collective-permute-start.18 = (bf16[768,512]{1,0:T(8,128)(2,1)}, bf16[768,512]{1,0:T(8,128)(2,1)}, u32[]{:S(2)}, u32[]{:S(2)}) collective-permute-start(bf16[768,512]{1,0:T(8,128)(2,1)} %emit.11), channel_id=1, source_target_pairs={{16,0},{32,16},{48,32},{17,1},{33,17},{49,33},{18,2},{34,18},{50,3... | collective-permute-start | bytes 2359304 | tf_op jit(solution)/shard_map/ppermute | solution.py:338
  368.5 30.0 %collective-permute-start.17 = (bf16[768,512]{1,0:T(8,128)(2,1)}, bf16[768,512]{1,0:T(8,128)(2,1)}, u32[]{:S(2)}, u32[]{:S(2)}) collective-permute-start(bf16[768,512]{1,0:T(8,128)(2,1)} %emit.10), channel_id=1, source_target_pairs={{16,0},{32,16},{48,32},{17,1},{33,17},{49,33},{18,2},{34,18},{50,3... | collective-permute-start | bytes 2359304 | tf_op jit(solution)/shard_map/ppermute | solution.py:338
  375.2 12.2 %collective-permute-start.19 = (bf16[2,4,256,128]{3,2,1,0:T(8,128)(2,1)}, bf16[2,4,256,128]{3,2,1,0:T(8,128)(2,1)}, u32[]{:S(2)}, u32[]{:S(2)}) collective-permute-start(bf16[2,4,256,128]{3,2,1,0:T(8,128)(2,1)} %wgrad.7.ma_ref), channel_id=1, source_target_pairs={{0,64},{64,0},{1,65},{65,1},{2,66},{66,2},{3,67},{67,3},{4,68},{68... | collective-permute-start | bytes 1572872 | tf_op jit(solution)/shard_map/ppermute | solution.py:332
  376.1 2.4 copy-start.5
  376.1 24.4 %collective-permute-start.20 = (bf16[2,4,256,128]{3,2,1,0:T(8,128)(2,1)}, bf16[2,4,256,128]{3,2,1,0:T(8,128)(2,1)}, u32[]{:S(2)}, u32[]{:S(2)}) collective-permute-start(bf16[2,4,256,128]{3,2,1,0:T(8,128)(2,1)} %wgrad.6), channel_id=1, source_target_pairs={{0,8},{8,0},{1,9},{9,1},{2,10},{10,2},{3,11},{11,3},{4,12},{12,4},... | collective-permute-start | bytes 1572872 | tf_op jit(solution)/shard_map/ppermute | solution.py:332
  376.7 25.5 %collective-permute-start.21 = (bf16[2,4,256,128]{3,2,1,0:T(8,128)(2,1)}, bf16[2,4,256,128]{3,2,1,0:T(8,128)(2,1)}, u32[]{:S(2)}, u32[]{:S(2)}) collective-permute-start(bf16[2,4,256,128]{3,2,1,0:T(8,128)(2,1)} %wgrad.6), channel_id=1, source_target_pairs={{0,72},{8,64},{64,8},{72,0},{1,73},{9,65},{65,9},{73,1},{2,74},{10... | collective-permute-start | bytes 1572872 | tf_op jit(solution)/shard_map/ppermute | solution.py:332

commit v3 on v2

--- a/solution.py
+++ b/solution.py
@@ -124,13 +124,13 @@
     peer[...] = scratch[pl.ds(theirs, half), :].reshape(peer.shape)
 
 
-def forward_body(side_ref, ro_ref, rp_ref, w2_ref, w3_ref, out_ref, mixed, narrow):
+def forward_body(side_ref, ro_ref, rp_ref, w2_ref, w3_ref, own_ref, peer_ref, mixed, narrow):
     side = side_ref[0]
     gather_rows(mixed, side, ro_ref, rp_ref)
     pre = mm(w2_ref[0], mixed[...], ((0,), (0,)))
     act = (0.5 * pre * (1.0 + jnp.tanh(GELU_A * (pre + GELU_B * (pre * pre * pre))))).astype(BF)
     narrow[...] = mm(w3_ref[0], act, ((0,), (0,))).astype(BF)
-    split_rows(narrow, side, out_ref.at[:, 0], out_ref.at[:, 1])
+    split_rows(narrow, side, own_ref, peer_ref)
 
 
 def plane_spec(array, plane, tile, start=0):
@@ -148,10 +148,10 @@
             num_scalar_prefetch=1,
             grid=(local, tokens // tile),
             in_specs=[plane_spec(*own, tile), plane_spec(*peer, tile), weight, weight],
-            out_specs=pl.BlockSpec((peers, 2, 1, sub, tile), lambda c, i, s: (0, 0, c, 0, i)),
+            out_specs=[pl.BlockSpec((peers, 1, sub, tile), lambda c, i, s: (0, c, 0, i))] * 2,
             scratch_shapes=[pltpu.VMEM((bsize, tile), BF), pltpu.VMEM((bsize, tile), BF)],
         ),
-        out_shape=jax.ShapeDtypeStruct((peers, 2, local, sub, tokens), BF),
+        out_shape=[jax.ShapeDtypeStruct((peers, local, sub, tokens), BF)] * 2,
         compiler_params=params(VMEM_MIB),
         cost_estimate=cost(
             4 * local * bsize * bsize * tokens, 4 * local * bsize * tokens, local * bsize * tokens
@@ -163,8 +163,8 @@
 def backward_body(
     steps, side_ref, ro_ref, rp_ref, go_ref, gp_ref, w2_ref, w3_ref, *rest,
 ):
-    outs, (mixed, gnar, gmix, acc2, acc3) = rest[-8 - steps : -5], rest[-5:]
-    mp_ref, g2_ref, g3_ref, mo_refs = outs[0], outs[1], outs[2], outs[3:]
+    outs, (mixed, gnar, gmix, acc2, acc3) = rest[-7 - steps : -5], rest[-5:]
+    mp_ref, g_ref, mo_refs = outs[0], outs[1], outs[2:]
     side = side_ref[0]
     step = pl.program_id(1)
     gather_rows(mixed, side, ro_ref, rp_ref)
@@ -199,8 +199,8 @@
 
     @pl.when(step == pl.num_programs(1) - 1)
     def _():
-        g2_ref[0] = acc2[...].astype(BF)
-        g3_ref[0] = acc3[...].astype(BF)
+        g_ref[0, 0] = acc2[...].astype(BF)
+        g_ref[1, 0] = acc3[...].astype(BF)
 
 
 def backward(side, own, peer, grad_own, grad_peer, second, third, tile, start, count, into):
@@ -211,8 +211,8 @@
     piece = pl.BlockSpec((peers, 1, sub, tile), lambda c, i, s: (0, start + c, 0, i))
     part = pl.BlockSpec((peers, 1, sub, tile), lambda c, i, s: (0, start + c, 0, 0))
     weight = pl.BlockSpec((1, bsize, bsize), lambda c, i, s: (start + c, 0, 0))
-    grad = pl.BlockSpec((1, bsize, bsize), lambda c, i, s: (c, 0, 0))
-    grads = jax.ShapeDtypeStruct((count, bsize, bsize), BF)
+    grad = pl.BlockSpec((2, 1, bsize, bsize), lambda c, i, s: (0, c, 0, 0))
+    grads = jax.ShapeDtypeStruct((2, count, bsize, bsize), BF)
     extra = () if into is None else into
     return pl.pallas_call(
         functools.partial(backward_body, steps),
@@ -220,13 +220,13 @@
             num_scalar_prefetch=1,
             grid=(count, tokens // tile),
             in_specs=pieces + [weight] * 2 + [pl.BlockSpec(memory_space=pl.ANY)] * len(extra),
-            out_specs=[piece, grad, grad] + [part] * steps,
+            out_specs=[piece, grad] + [part] * steps,
             scratch_shapes=[pltpu.VMEM((bsize, tile), BF)] * 3
             + [pltpu.VMEM((bsize, bsize), F32)] * 2,
         ),
-        out_shape=[jax.ShapeDtypeStruct((peers, local, sub, tokens), BF), grads, grads]
+        out_shape=[jax.ShapeDtypeStruct((peers, local, sub, tokens), BF), grads]
         + [jax.ShapeDtypeStruct((peers, local, sub, tile), BF)] * steps,
-        input_output_aliases={7 + i: (0 if i == 0 else 2 + i) for i in range(len(extra))},
+        input_output_aliases={7 + i: (0 if i == 0 else 1 + i) for i in range(len(extra))},
         compiler_params=params(VMEM_MIB),
         cost_estimate=cost(
             10 * count * bsize * bsize * tokens, 6 * count * bsize * tokens, count * bsize * tokens
@@ -351,36 +351,31 @@
     return lax.slice_in_dim(value, 0, size, axis=dim), lax.slice_in_dim(value, size, 2 * size, axis=dim)
 
 
-def join_body(starts, sizes, *refs):
-    out_ref = refs[-1]
-    at = pl.program_id(0)
-    for n, (start, size) in enumerate(zip(starts, sizes)):
-
-        @pl.when((at >= start) & (at < start + size))
-        def _(n=n):
-            out_ref[...] = refs[2 * n][...].astype(F32) + refs[2 * n + 1][...].astype(F32)
+def join_body(count, *refs):
+    out_refs = refs[2 * count :]
+    start = 0
+    for n in range(count):
+        size = refs[2 * n].shape[1]
+        for which, out_ref in enumerate(out_refs):
+            out_ref[start : start + size] = refs[2 * n][which].astype(F32) + refs[2 * n + 1][which].astype(F32)
+        start += size
 
 
 def join(pairs):
-    sizes = [a.shape[0] for a, _ in pairs]
-    starts = [sum(sizes[:n]) for n in range(len(sizes))]
-    rest = pairs[0][0].shape[1:]
-    specs = []
-    for start, size in zip(starts, sizes):
-        spec = pl.BlockSpec(
-            (1,) + rest, lambda i, start=start, size=size: (jnp.clip(i - start, 0, size - 1), 0, 0)
-        )
-        specs += [spec, spec]
-    return pl.pallas_call(
-        functools.partial(join_body, starts, sizes),
-        grid=(sum(sizes),),
-        in_specs=specs,
-        out_specs=pl.BlockSpec((1,) + rest, lambda i: (i, 0, 0)),
-        out_shape=jax.ShapeDtypeStruct((sum(sizes),) + rest, F32),
+    arrays = [each for pair in pairs for each in pair]
+    results = arrays[0].shape[0]
+    rest = arrays[0].shape[2:]
+    total = (sum(a.shape[1] for a, _ in pairs),) + rest
+    return pl.pallas_call(
+        functools.partial(join_body, len(pairs)),
+        grid=(1,),
+        in_specs=[pl.BlockSpec(each.shape, lambda i: (0, 0, 0, 0)) for each in arrays],
+        out_specs=[pl.BlockSpec(total, lambda i: (0, 0, 0))] * results,
+        out_shape=[jax.ShapeDtypeStruct(total, F32)] * results,
         compiler_params=params(VMEM_MIB),
         cost_estimate=cost(1, 1),
         name="join",
-    )(*[each for pair in pairs for each in pair])
+    )(*arrays)
 
 
 def paired_body(side_ref, ma_ref, mb_ref, ta_ref, tb_ref, out_ref):
@@ -451,15 +446,15 @@
     is_low = low_or_high == 0
     side = low_or_high.astype(jnp.int32).reshape(1)
     zero = jnp.zeros((1,), jnp.int32)
-    tile = 512 if tokens % 512 == 0 else tokens
     half = tokens // 2
+    tile = half
 
     low, high = halves(first, 3)
     first_peer = swapped(jnp.where(is_low, high, low), "xlo")
     x_peer = swapped(x, "xlo")
     low, high = halves(fourth, 2)
     fourth_side = jnp.where(is_low, high, low)
-    early = 2 * tokens // 3
+    early = half
     u_early = swapped(behind(u[:early], (x_peer, first_peer)), "xlo")
     u_late = swapped(behind(u[early:], u_early), "xlo")
     fourth_peer = swapped(behind(fourth_side, u_early), "xlo")
@@ -479,58 +474,50 @@
     l2p, a4p = lift([u_peer], [fourth_peer], [False], zero, peers, tile)
     y2p = inner(l2p, y1p)
     a1o, a4o, a1p, a4p = a1o.T, a4o.T, a1p.T, a4p.T
-    n = forward(behind(side, (a1o, a4o, a1p, a4p)), (y12, 0), (y1p, 0), second, third, half)
-    y3 = outer(n, y2p)
-
+    no, np_ = forward(behind(side, (a1o, a4o, a1p, a4p)), (y12, 0), (y1p, 0), second, third, half)
+    y3p = outer(np_, y2p)
     args = ((y12, 0), (y1p, 0), (y12, 1), (y2p, 0), second, third, half)
-    third_part = -(-local // 3)
-    cuts = [0, third_part, 2 * third_part, local]
-    into, g2, g3, d2, d3 = None, [], [], [], []
-    gate = side
-    for n in range(3):
-        got = backward(gate, *args, cuts[n], cuts[n + 1] - cuts[n], into)
-        mp, mo1, mo2 = into = (got[0], got[3], got[4])
-        g2.append(got[1])
-        g3.append(got[2])
-        d2.append(swapped(got[1], "dp"))
-        d3.append(swapped(got[2], "dp"))
-        if n == 1:
-            gate = behind(side, (d2[0], d3[0]))
-    y4p = outer(mp, (y3, *d2, *d3))
-    out_p = emit(y3, 1, a4p, None, half, 0, tokens)
+    first_cut, second_cut = 3 * local // 8, local // 2
+    mp, ga, mo1, mo2 = backward(side, *args, 0, first_cut, None)
+    da = swapped(ga, "dp")
+    mp, gb, mo1, mo2 = backward(side, *args, first_cut, second_cut - first_cut, (mp, mo1, mo2))
+    mp, gc, mo1, mo2 = backward(side, *args, second_cut, local - second_cut, (mp, mo1, mo2))
+    y3o = outer(no, (y3p, mp, da))
+    out_p = emit(y3p, 0, a4p, None, half, 0, tokens)
     out_peer = swapped(out_p, "xlo")
-    g4p = wgrad([(y3, 1, 0), (y3, 1, 1)], behind(u_peer, out_p), groups, expand, False)
-    g4o = wgrad([(y3, 0, 0), (y3, 0, 1)], u, groups, expand, False)
-    grad_two = join(list(zip(g2, d2)))
-    grad_three = join(list(zip(g3, d3)))
-    y4a = outer(mo1, (y4p, g4o, g4p, grad_two, grad_three))
-    t4x = swapped(behind(g4p, out_peer), "xlo")
-    t4d = swapped(behind(g4p, out_peer), ("dp", "xlo"))
-    out_o = emit(y3, 0, a4o, out_peer, half, 0, tokens)
+    g4p = wgrad([(y3p, 0, 0), (y3p, 0, 1)], behind(u_peer, out_p), groups, expand, False)
+    y4p = outer(mp, (y3o, g4p, out_peer))
+    db = swapped(behind(gb, out_peer), "dp")
+    dc = swapped(behind(gc, out_peer), "dp")
+    t4x, t4d = swapped(behind(g4p, out_peer), "xlo"), swapped(behind(g4p, out_peer), ("dp", "xlo"))
+    out_o = emit(y3o, 0, a4o, out_peer, half, 0, tokens)
     y_next = copied(shifted(out_o, "pipe", 1))
+    g4o = wgrad([(y3o, 0, 0), (y3o, 0, 1)], behind(u, out_o), groups, expand, False)
+    y4a = outer(mo1, (y4p, g4o, db, dc, t4x, t4d))
+    grad_two, grad_three = join([(ga, da), (gb, db), (gc, dc)])
     in_p1 = emit(y4p, 0, a1p, None, half, 0, half)
+    in_peer1 = swapped(behind(in_p1, out_peer), "xlo")
     in_p2 = emit(y4p, 0, a1p, None, half, half, half)
-    in_peer1 = swapped(behind(in_p1, (t4x, t4d, out_o)), "xlo")
-    in_peer2 = swapped(behind(in_p2, in_peer1), "xlo")
+    in_peer2 = swapped(in_p2, "xlo")
     g1p = wgrad([(y4p, 0, 0), (y4p, 0, 1)], behind(x_peer, in_p2), groups, expand, True)
-    y4b = outer(mo2, (y4a, in_p2))
-    d4o = swapped(behind(g4o, in_peer2), "dp")
-    in_a = emit(y4a, 0, a1o, in_peer1, half, 0, half)
+    d4o = swapped(g4o, "dp")
+    y4b = outer(mo2, (y4a, g1p, y_next, d4o))
+    in_a = emit(y4a, 0, a1o, behind(in_peer1, g1p), half, 0, half)
     dx1 = shifted(in_a, "pipe", -1)
-    t1x = swapped(behind(g1p, in_peer2), "xlo")
-    t1d = swapped(behind(g1p, in_peer2), ("dp", "xlo"))
-    in_b = emit(y4b, 0, a1o, behind(in_peer2, g1p), half, 0, half)
-    dx2 = shifted(in_b, "pipe", -1)
+    late = (in_peer2, in_a, grad_two, grad_three)
+    t1x, t1d = swapped(behind(g1p, late), "xlo"), swapped(behind(g1p, late), ("dp", "xlo"))
+    in_b = emit(y4b, 0, a1o, in_peer2, half, 0, half)
+    dx2 = shifted(behind(in_b, dx1), "pipe", -1)
     dx_prev = place(dx1, None, 0, 2)
     g1o = wgrad(
         [(y4a, 0, 0), (y4b, 0, 0)],
         behind(x, in_b),
         groups, expand, True,
     )
-    d1o = behind(swapped(g1o, "dp"), dx2)
+    d1o = swapped(behind(g1o, (t1x, t1d)), "dp")
     grad_four = paired(side, (g4o, d4o), (t4x, t4d), 2)
-    grad_one = paired(side, (g1o, d1o), (t1x, t1d), 3)
     dx_prev = place(dx2, dx_prev, 1, 2)
+    grad_one = paired(side, (behind(g1o, (dx_prev, grad_four)), d1o), (t1x, t1d), 3)
     return (
         y_next[None], dx_prev[None], grad_one[None], grad_two[None], grad_three[None], grad_four[None],
     )

time: 409 us -> 405 us (level)
  Pallas kernels: 143 us -> 132 us
    ppermute x20 -> x17, waiting for transfers between devices: 129 us -> 145 us  [swapped(): return lax.ppermute(value, axes, [(i, count - 1 - i) for i in range(count)])]
    all_to_all x7 -> x8, waiting for transfers between devices: 42.9 us -> 28.2 us  [spread_out(): return lax.all_to_all(value, YC, split_axis=0, concat_axis=0, tiled=True)]
    pallas_call x2 -> x1, Pallas kernels: 12.3 us -> 4.49 us  [join(): pl.pallas_call(functools.partial(join_body, len(pairs)), grid=(1,), in_sp...]
    all_to_all x7 -> x8, starting transfers between devices: 37.8 us -> 42.9 us  [spread_out(): return lax.all_to_all(value, YC, split_axis=0, concat_axis=0, tiled=True)]
    ppermute x20 -> x17, starting transfers between devices: 24.7 us -> 22.6 us  [swapped(): return lax.ppermute(value, axes, [(i, count - 1 - i) for i in range(count)])]
  transfers between devices with their start and end apart: 30 -> 28, of which waited for: 21 -> 16; matrix products, arithmetic and copies ran while one was open for 2% -> 2% of each run, Pallas kernels for 32% -> 30%
where the time goes in v3:
time: 405 us; the launch traced here: 402 us
  waiting for transfers between devices  181 us (45%)
  Pallas kernels  132 us (33%)
  starting transfers between devices  72.9 us (18%)
  local copies, waits for them, and re-layouts  13.7 us (3%)
    ppermute x17, waiting for transfers between devices, swapped(): return lax.ppermute(value, axes, [(i, count - 1 - i) for i in range(count)])  145 us
    all_to_all x8, starting transfers between devices, spread_out(): return lax.all_to_all(value, YC, split_axis=0, concat_axis=0, tiled=True)  42.9 us
    pallas_call x3, Pallas kernels, backward(): pl.pallas_call(functools.partial(backward_body, steps), grid_spec=pltpu.P...  30 us
    all_to_all x8, waiting for transfers between devices, spread_out(): return lax.all_to_all(value, YC, split_axis=0, concat_axis=0, tiled=True)  28.2 us
    pallas_call x6, Pallas kernels, emit(): pl.pallas_call(functools.partial(emit_body, add), grid=(tokens // tile,),...  25.2 us
    ppermute x17, starting transfers between devices, swapped(): return lax.ppermute(value, axes, [(i, count - 1 - i) for i in range(count)])  22.6 us
    pallas_call x4, Pallas kernels, wgrad(): pl.pallas_call(functools.partial(wgrad_body, swap, groups, expand, count)...  21.8 us
    pallas_call x3, Pallas kernels, lift(): pl.pallas_call(functools.partial(lift_body, swaps, steps), grid_spec=pltp...  20.7 us
  transfers between devices with their start and end apart: 28, of which 16 were waited for; matrix products, arithmetic and copies ran while one was open for 2% of the time, Pallas kernels for 30%

profile of v3, /device:TPU:1, one launch (start us, length us, event | category | flops | bytes accessed | tf_op | source)
XLA Modules:
  0.0 402.2 jit_solution(9637292591017798604)
XLA Ops:
  0.6 9.5 %lift.3 = (bf16[8,2,128,1536]{3,2,1,0:T(8,128)(2,1)}, bf16[1024,512]{1,0:T(8,128)(2,1)}, bf16[1024,512]{1,0:T(8,128)(2,1)}) custom-call(s32[1]{0:T(128)} %bitcast.side_ref, bf16[1536,512]{1,0:T(8,128)(2,1)} %bitcast.45, bf16[1536,512]{1,0:T(8,128)(2,1)} %bitcast.38, bf16[2,4,256,256]{3,2,1,0:T(8,128)(2,1)} %bitcast.49, bf16[2,4,256,256]{3,2,1,0:T(8,128)(2,1)} %bitcast.51), custom_call_target="tpu_custom_call" | custom-call | flops 128849016 | bytes 188743 | tf_op jit(solution)/shard_map/lift/pallas_call | solution.py:92
  10.1 6.1 %all-to-all-start = ((bf16[8,2,128,1536]{3,2,1,0:T(8,128)(2,1)}), bf16[8,2,128,1536]{3,2,1,0:T(8,128)(2,1)}, u32[]{:S(2)}, u32[]{:S(2)}) async-start(bf16[8,2,128,1536]{3,2,1,0:T(8,128)(2,1)} %get-tuple-element.61), calls=%async_computation | async-start | bytes 12582912 | tf_op jit(solution)/shard_map/all_to_all | solution.py:342
  20.4 43.2 %collective-permute-done.1.refs_1_ = bf16[2,4,256,128]{3,2,1,0:T(8,128)(2,1)S(1)} collective-permute-done((bf16[2,4,256,128]{3,2,1,0:T(8,128)(2,1)S(1)}, bf16[2,4,256,128]{3,2,1,0:T(8,128)(2,1)S(1)}, u32[]{:S(2)}, u32[]{:S(2)}) %collective-permute-start.1) | collective-permute-done | bytes 524320 | tf_op jit(solution)/shard_map/ppermute | solution.py:332
  65.7 5.6 %lift.4 = (bf16[8,1,128,1536]{3,2,1,0:T(8,128)(2,1)}, bf16[1024,512]{1,0:T(8,128)(2,1)}) custom-call(s32[1]{0:T(128)} %constant.8.clone.1.side_ref, bf16[1536,512]{1,0:T(8,128)(2,1)} %copy-done.3, bf16[2,4,256,128]{3,2,1,0:T(8,128)(2,1)} %copy-done.17), custom_call_target="tpu_custom_call" | custom-call | flops 64424508 | bytes 94371 | tf_op jit(solution)/shard_map/lift/pallas_call | solution.py:92
  71.3 11.5 %collective-permute-done.2 = bf16[768,512]{1,0:T(8,128)(2,1)} collective-permute-done((bf16[768,512]{1,0:T(8,128)(2,1)}, bf16[768,512]{1,0:T(8,128)(2,1)}, u32[]{:S(2)}, u32[]{:S(2)}) %collective-permute-start.2) | collective-permute-done | bytes 786464 | tf_op jit(solution)/shard_map/ppermute | solution.py:332
  82.8 4.8 %all-to-all-done = bf16[8,2,128,1536]{3,2,1,0:T(8,128)(2,1)} async-done(((bf16[8,2,128,1536]{3,2,1,0:T(8,128)(2,1)}), bf16[8,2,128,1536]{3,2,1,0:T(8,128)(2,1)}, u32[]{:S(2)}, u32[]{:S(2)}) %all-to-all-start) | async-done | bytes 6291488 | tf_op jit(solution)/shard_map/all_to_all | solution.py:342
  87.6 5.3 %all-to-all-start.1 = ((bf16[8,1,128,1536]{3,2,1,0:T(8,128)(2,1)}), bf16[8,1,128,1536]{3,2,1,0:T(8,128)(2,1)}, u32[]{:S(2)}, u32[]{:S(2)}) async-start(bf16[8,1,128,1536]{3,2,1,0:T(8,128)(2,1)} %get-tuple-element.63), calls=%async_computation.1 | async-start | bytes 6291456 | tf_op jit(solution)/shard_map/all_to_all | solution.py:342
  95.7 16.5 %collective-permute-done.3 = bf16[768,512]{1,0:T(8,128)(2,1)S(1)} collective-permute-done((bf16[768,512]{1,0:T(8,128)(2,1)}, bf16[768,512]{1,0:T(8,128)(2,1)S(1)}, u32[]{:S(2)}, u32[]{:S(2)}) %collective-permute-start.3) | collective-permute-done | bytes 786464 | tf_op jit(solution)/shard_map/ppermute | solution.py:332
  112.3 11.2 %collective-permute-done.4.refs_1_ = bf16[2,4,128,256]{3,2,1,0:T(8,128)(2,1)} collective-permute-done((bf16[2,4,128,256]{3,2,1,0:T(8,128)(2,1)S(1)}, bf16[2,4,128,256]{3,2,1,0:T(8,128)(2,1)}, u32[]{:S(2)}, u32[]{:S(2)}) %collective-permute-start.4) | collective-permute-done | bytes 524320 | tf_op jit(solution)/shard_map/ppermute | solution.py:332
  123.4 5.6 %lift.5 = (bf16[8,1,128,1536]{3,2,1,0:T(8,128)(2,1)}, bf16[1024,512]{1,0:T(8,128)(2,1)}) custom-call(s32[1]{0:T(128)} %constant.8.clone.1.side_ref, bf16[1536,512]{1,0:T(8,128)(2,1)} %copy-done.2, bf16[2,4,128,256]{3,2,1,0:T(8,128)(2,1)} %collective-permute-done.4.refs_1_), custom_call_target="tpu_custom_call" | custom-call | flops 64424508 | bytes 94371 | tf_op jit(solution)/shard_map/lift/pallas_call | solution.py:92
  130.6 5.3 %all-to-all-start.2 = ((bf16[8,1,128,1536]{3,2,1,0:T(8,128)(2,1)}), bf16[8,1,128,1536]{3,2,1,0:T(8,128)(2,1)}, u32[]{:S(2)}, u32[]{:S(2)}) async-start(bf16[8,1,128,1536]{3,2,1,0:T(8,128)(2,1)} %get-tuple-element.67), calls=%async_computation.2 | async-start | bytes 6291456 | tf_op jit(solution)/shard_map/all_to_all | solution.py:342
  141.3 17.4 %forward.1 = (bf16[8,8,16,1536]{3,2,1,0:T(8,128)(2,1)}, bf16[8,8,16,1536]{3,2,1,0:T(8,128)(2,1)}) custom-call(s32[1]{0:T(128)} %bitcast.side_ref, bf16[8,2,8,16,1536]{4,3,2,1,0:T(8,128)(2,1)} %bitcast.11.ro_ref.go_ref, bf16[8,1,8,16,1536]{4,3,2,1,0:T(8,128)(2,1)} %bitcast.12.rp_ref, bf16[8,256,256]{2,1,0:T(8,128)(2,1)} %bitcast.30, bf16[8,256,256]{2,1,0:T(8,128)(2,1)} %bitcast.34), custom_call_target="tpu_custom_call" | custom-call | flops 64424508 | bytes 251658 | tf_op jit(solution)/shard_map/forward/pallas_call | solution.py:145
  158.7 15.0 %all-to-all-done.2 = bf16[8,1,128,1536]{3,2,1,0:T(8,128)(2,1)} async-done(((bf16[8,1,128,1536]{3,2,1,0:T(8,128)(2,1)}), bf16[8,1,128,1536]{3,2,1,0:T(8,128)(2,1)}, u32[]{:S(2)}, u32[]{:S(2)}) %all-to-all-start.2) | async-done | bytes 3145760 | tf_op jit(solution)/shard_map/all_to_all | solution.py:342
  173.7 5.2 %all-to-all-start.3 = ((bf16[8,1,128,1536]{3,2,1,0:T(8,128)(2,1)}), bf16[8,1,128,1536]{3,2,1,0:T(8,128)(2,1)}, u32[]{:S(2)}, u32[]{:S(2)}) async-start(bf16[8,1,128,1536]{3,2,1,0:T(8,128)(2,1)} %bitcast.55), calls=%async_computation.3 | async-start | bytes 6291456 | tf_op jit(solution)/shard_map/all_to_all | solution.py:342
  178.9 11.0 %backward.3 = (bf16[8,8,16,1536]{3,2,1,0:T(8,128)(2,1)}, bf16[2,3,256,256]{3,2,1,0:T(8,128)(2,1)}, bf16[8,8,16,768]{3,2,1,0:T(8,128)(2,1)}, bf16[8,8,16,768]{3,2,1,0:T(8,128)(2,1)}) custom-call(s32[1]{0:T(128)} %bitcast.side_ref, bf16[8,2,8,16,1536]{4,3,2,1,0:T(8,128)(2,1)} %bitcast.11.ro_ref.go_ref, bf16[8,1,8,16,1536]{4,3,2,1,0:T(8,128)(2,1)} %bitcast.12.rp_ref, ...), custom_call_target="tpu_custom_call" | custom-call | flops 60397976 | bytes 141557 | tf_op jit(solution)/shard_map/backward/pallas_call | solution.py:217
  189.8 3.0 collective-permute-start.5
  192.9 5.0 %backward.4 = (bf16[8,8,16,1536]{3,2,1,0:T(8,128)(2,1)}, bf16[2,1,256,256]{3,2,1,0:T(8,128)(2,1)}, bf16[8,8,16,768]{3,2,1,0:T(8,128)(2,1)}, bf16[8,8,16,768]{3,2,1,0:T(8,128)(2,1)}) custom-call(s32[1]{0:T(128)} %bitcast.side_ref, bf16[8,2,8,16,1536]{4,3,2,1,0:T(8,128)(2,1)} %bitcast.11.ro_ref.go_ref, ...), custom_call_target="tpu_custom_call", output_to_operand_aliasing={{0}: (7, {}), {2}: (8, {}), {3}: (9, {})} | custom-call | flops 20132660 | bytes 47185 | tf_op jit(solution)/shard_map/backward/pallas_call | solution.py:217
  197.9 14.1 %backward.5 = (bf16[8,8,16,1536]{3,2,1,0:T(8,128)(2,1)}, bf16[2,4,256,256]{3,2,1,0:T(8,128)(2,1)}, bf16[8,8,16,768]{3,2,1,0:T(8,128)(2,1)}, bf16[8,8,16,768]{3,2,1,0:T(8,128)(2,1)}) custom-call(s32[1]{0:T(128)} %bitcast.side_ref, bf16[8,2,8,16,1536]{4,3,2,1,0:T(8,128)(2,1)} %bitcast.11.ro_ref.go_ref, ...), custom_call_target="tpu_custom_call", output_to_operand_aliasing={{0}: (7, {}), {2}: (8, {}), {3}: (9, {})} | custom-call | flops 80530640 | bytes 188743 | tf_op jit(solution)/shard_map/backward/pallas_call | solution.py:217
  211.9 4.6 %all-to-all-done.3.s_ref.refs_0_.refs_1_ = bf16[8,1,128,1536]{3,2,1,0:T(8,128)(2,1)} async-done(((bf16[8,1,128,1536]{3,2,1,0:T(8,128)(2,1)}), bf16[8,1,128,1536]{3,2,1,0:T(8,128)(2,1)}, u32[]{:S(2)}, u32[]{:S(2)}) %all-to-all-start.3) | async-done | bytes 3145760 | tf_op jit(solution)/shard_map/all_to_all | solution.py:342
  216.6 5.2 %all-to-all-start.4 = ((bf16[8,1,128,1536]{3,2,1,0:T(8,128)(2,1)}), bf16[8,1,128,1536]{3,2,1,0:T(8,128)(2,1)}, u32[]{:S(2)}, u32[]{:S(2)}) async-start(bf16[8,1,128,1536]{3,2,1,0:T(8,128)(2,1)} %bitcast.54), calls=%async_computation.4 | async-start | bytes 6291456 | tf_op jit(solution)/shard_map/all_to_all | solution.py:342
  221.8 4.7 %emit.6 = bf16[1536,512]{1,0:T(8,128)(2,1)} custom-call(bf16[8,1,128,1536]{3,2,1,0:T(8,128)(2,1)} %all-to-all-done.3.s_ref.refs_0_.refs_1_, bf16[512,1024]{1,0:T(8,128)(2,1)} %bitcast.53), custom_call_target="tpu_custom_call" | custom-call | flops 32212254 | bytes 125829 | tf_op jit(solution)/shard_map/emit/pallas_call | solution.py:252
  227.7 5.4 %wgrad.4 = bf16[2,4,128,256]{3,2,1,0:T(8,128)(2,1)} custom-call(bf16[8,1,128,1536]{3,2,1,0:T(8,128)(2,1)} %all-to-all-done.3.s_ref.refs_0_.refs_1_, bf16[8,1,128,1536]{3,2,1,0:T(8,128)(2,1)} %all-to-all-done.3.s_ref.refs_0_.refs_1_, bf16[1536,512]{1,0:T(8,128)(2,1)} %copy-done.2), custom_call_target="tpu_custom_call" | custom-call | flops 32212254 | bytes 94371 | tf_op jit(solution)/shard_map/wgrad/pallas_call | solution.py:313
  233.2 29.3 %collective-permute-done.6.rest_0_ = bf16[1536,512]{1,0:T(8,128)(2,1)S(1)} collective-permute-done((bf16[1536,512]{1,0:T(8,128)(2,1)}, bf16[1536,512]{1,0:T(8,128)(2,1)S(1)}, u32[]{:S(2)}, u32[]{:S(2)}) %collective-permute-start.6) | collective-permute-done | bytes 1572896 | tf_op jit(solution)/shard_map/ppermute | solution.py:332
  263.7 5.4 %all-to-all-start.5 = ((bf16[8,1,128,1536]{3,2,1,0:T(8,128)(2,1)}), bf16[8,1,128,1536]{3,2,1,0:T(8,128)(2,1)}, u32[]{:S(2)}, u32[]{:S(2)}) async-start(bf16[8,1,128,1536]{3,2,1,0:T(8,128)(2,1)} %bitcast.29), calls=%async_computation.5 | async-start | bytes 6291456 | tf_op jit(solution)/shard_map/all_to_all | solution.py:342
  269.1 2.8 collective-permute-start.9
  272.8 2.4 collective-permute-start.8
  275.2 5.2 %emit.7 = bf16[1536,512]{1,0:T(8,128)(2,1)} custom-call(bf16[8,1,128,1536]{3,2,1,0:T(8,128)(2,1)} %all-to-all-done.4.s_ref.refs_0_.refs_1_, bf16[512,1024]{1,0:T(8,128)(2,1)} %bitcast.48, bf16[1536,512]{1,0:T(8,128)(2,1)} %copy-done.5), custom_call_target="tpu_custom_call" | custom-call | flops 32212254 | bytes 125829 | tf_op jit(solution)/shard_map/emit/pallas_call | solution.py:252
  280.4 4.8 %collective-permute-start.7 = (bf16[1536,512]{1,0:T(8,128)(2,1)}, bf16[1536,512]{1,0:T(8,128)(2,1)}, u32[]{:S(2)}, u32[]{:S(2)}) collective-permute-start(bf16[1536,512]{1,0:T(8,128)(2,1)} %emit.7), channel_id=1, source_target_pairs={{0,16},{16,32},{32,48},{1,17},{17,33},{33,49},{2,18},{18,34},{34,5... | collective-permute-start | bytes 4718600 | tf_op jit(solution)/shard_map/ppermute | solution.py:338
  285.2 5.5 %wgrad.5.ma_ref = bf16[2,4,128,256]{3,2,1,0:T(8,128)(2,1)} custom-call(bf16[8,1,128,1536]{3,2,1,0:T(8,128)(2,1)} %all-to-all-done.4.s_ref.refs_0_.refs_1_, bf16[8,1,128,1536]{3,2,1,0:T(8,128)(2,1)} %all-to-all-done.4.s_ref.refs_0_.refs_1_, bf16[1536,512]{1,0:T(8,128)(2,1)} %bitcast.39), custom_call_target="tpu_custom_call" | custom-call | flops 32212254 | bytes 94371 | tf_op jit(solution)/shard_map/wgrad/pallas_call | solution.py:313
  290.6 21.9 %collective-permute-done.8.refs_3_ = bf16[2,1,256,256]{3,2,1,0:T(8,128)(2,1)} collective-permute-done((bf16[2,1,256,256]{3,2,1,0:T(8,128)(2,1)S(1)}, bf16[2,1,256,256]{3,2,1,0:T(8,128)(2,1)}, u32[]{:S(2)}, u32[]{:S(2)}) %collective-permute-start.8) | collective-permute-done | bytes 262176 | tf_op jit(solution)/shard_map/ppermute | solution.py:332
  313.7 5.3 %all-to-all-start.6 = ((bf16[8,1,128,768]{3,2,1,0:T(8,128)(2,1)}), bf16[8,1,128,768]{3,2,1,0:T(8,128)(2,1)S(1)}, u32[]{:S(2)}, u32[]{:S(2)}) async-start(bf16[8,1,128,768]{3,2,1,0:T(8,128)(2,1)} %bitcast.20), calls=%async_computation.6 | async-start | bytes 3145728 | tf_op jit(solution)/shard_map/all_to_all | solution.py:342
  319.0 2.8 collective-permute-start.12
  321.8 3.6 emit.10
  325.8 2.7 place.3
  328.4 3.6 emit.8
  332.1 5.5 %wgrad.6 = bf16[2,4,256,128]{3,2,1,0:T(8,128)(2,1)} custom-call(bf16[8,1,128,1536]{3,2,1,0:T(8,128)(2,1)} %all-to-all-done.5.s_ref.refs_0_.refs_1_, bf16[8,1,128,1536]{3,2,1,0:T(8,128)(2,1)} %all-to-all-done.5.s_ref.refs_0_.refs_1_, bf16[1536,512]{1,0:T(8,128)(2,1)} %copy-done.3), custom_call_target="tpu_custom_call" | custom-call | flops 32212254 | bytes 94371 | tf_op jit(solution)/shard_map/wgrad/pallas_call | solution.py:313
  337.5 2.2 all-to-all-done.6.s_ref.refs_0_
  340.8 5.0 %all-to-all-start.7 = ((bf16[8,1,128,768]{3,2,1,0:T(8,128)(2,1)}), bf16[8,1,128,768]{3,2,1,0:T(8,128)(2,1)}, u32[]{:S(2)}, u32[]{:S(2)}) async-start(bf16[8,1,128,768]{3,2,1,0:T(8,128)(2,1)} %bitcast.19), calls=%async_computation.7 | async-start | bytes 3145728 | tf_op jit(solution)/shard_map/all_to_all | solution.py:342
  347.2 4.2 %collective-permute-done.14.rest_0_ = bf16[768,512]{1,0:T(8,128)(2,1)} collective-permute-done((bf16[768,512]{1,0:T(8,128)(2,1)}, bf16[768,512]{1,0:T(8,128)(2,1)}, u32[]{:S(2)}, u32[]{:S(2)}) %collective-permute-start.14) | collective-permute-done | bytes 786464 | tf_op jit(solution)/shard_map/ppermute | solution.py:332
  351.4 4.0 emit.11
  356.7 4.5 %join.1 = (f32[8,256,256]{2,1,0:T(8,128)}, f32[8,256,256]{2,1,0:T(8,128)}) custom-call(bf16[2,3,256,256]{3,2,1,0:T(8,128)(2,1)} %get-tuple-element.76.refs_0_, bf16[2,3,256,256]{3,2,1,0:T(8,128)(2,1)} %copy-done.11, bf16[2,1,256,256]{3,2,1,0:T(8,128)(2,1)} %get-tuple-element.84.refs_2_, bf16[2,1,256,256]{3,2,1,0:T(8,128)(2,1)} %collective-permute-done.8.refs_3_, ...), custom_call_target="tpu_custom_call" | custom-call | tf_op jit(solution)/shard_map/join/pallas_call | solution.py:369
  361.2 7.0 %collective-permute-done.13.rest_0_ = bf16[768,512]{1,0:T(8,128)(2,1)S(1)} collective-permute-done((bf16[768,512]{1,0:T(8,128)(2,1)}, bf16[768,512]{1,0:T(8,128)(2,1)S(1)}, u32[]{:S(2)}, u32[]{:S(2)}) %collective-permute-start.13) | collective-permute-done | bytes 786464 | tf_op jit(solution)/shard_map/ppermute | solution.py:332
  370.3 4.0 emit.9
  377.1 5.5 %wgrad.7.ma_ref = bf16[2,4,256,128]{3,2,1,0:T(8,128)(2,1)} custom-call(bf16[8,1,128,768]{3,2,1,0:T(8,128)(2,1)} %copy-done.1, bf16[8,1,128,768]{3,2,1,0:T(8,128)(2,1)} %all-to-all-done.7.s_ref.refs_1_, bf16[1536,512]{1,0:T(8,128)(2,1)} %bitcast.47), custom_call_target="tpu_custom_call" | custom-call | flops 32212254 | bytes 94371 | tf_op jit(solution)/shard_map/wgrad/pallas_call | solution.py:313
  384.4 2.9 paired.2
  387.3 2.1 place.4.rest_0_
  389.4 6.1 %collective-permute-done.16.value_ref = bf16[768,512]{1,0:T(8,128)(2,1)S(1)} collective-permute-done((bf16[768,512]{1,0:T(8,128)(2,1)}, bf16[768,512]{1,0:T(8,128)(2,1)S(1)}, u32[]{:S(2)}, u32[]{:S(2)}) %collective-permute-start.16) | collective-permute-done | bytes 786464 | tf_op jit(solution)/shard_map/ppermute | solution.py:338
  399.3 2.9 paired.3
  (78 shorter events, 35.1 us)
Async XLA Ops:
  10.1 77.5 %all-to-all-start = ((bf16[8,2,128,1536]{3,2,1,0:T(8,128)(2,1)}), bf16[8,2,128,1536]{3,2,1,0:T(8,128)(2,1)}, u32[]{:S(2)}, u32[]{:S(2)}) async-start(bf16[8,2,128,1536]{3,2,1,0:T(8,128)(2,1)} %get-tuple-element.61), calls=%async_computation | async-start | bytes 12582912 | tf_op jit(solution)/shard_map/all_to_all | solution.py:342
  16.2 2.9 copy-start
  16.2 47.3 %collective-permute-start = (bf16[1536,512]{1,0:T(8,128)(2,1)}, bf16[1536,512]{1,0:T(8,128)(2,1)S(1)}, u32[]{:S(2)}, u32[]{:S(2)}) collective-permute-start(bf16[1536,512]{1,0:T(8,128)(2,1)} %bitcast.46), channel_id=1, source_target_pairs={{0,8},{8,0},{1,9},{9,1},{2,10},{10,2},{3,11},{11,3},{4,12},{12,4},... | collective-permute-start | bytes 4718600 | tf_op jit(solution)/shard_map/ppermute | solution.py:332
  18.8 44.8 %collective-permute-start.1 = (bf16[2,4,256,128]{3,2,1,0:T(8,128)(2,1)S(1)}, bf16[2,4,256,128]{3,2,1,0:T(8,128)(2,1)S(1)}, u32[]{:S(2)}, u32[]{:S(2)}) collective-permute-start(bf16[2,4,256,128]{3,2,1,0:T(8,128)(2,1)S(1)} %slice_select_fusion.1), channel_id=1, source_target_pairs={{0,8},{8,0},{1,9},{9,1},{2,10},{10,2},{3,11},{11,3},{4,12},{12,4},... | collective-permute-start | bytes 1572872 | tf_op jit(solution)/shard_map/ppermute | solution.py:332
  63.6 0.8 copy-start.17
  64.4 1.3 copy-start.3
  64.4 18.4 %collective-permute-start.2 = (bf16[768,512]{1,0:T(8,128)(2,1)}, bf16[768,512]{1,0:T(8,128)(2,1)}, u32[]{:S(2)}, u32[]{:S(2)}) collective-permute-start(bf16[768,512]{1,0:T(8,128)(2,1)} %get-tuple-element.56), channel_id=1, source_target_pairs={{0,8},{8,0},{1,9},{9,1},{2,10},{10,2},{3,11},{11,3},{4,12},{12,4},... | collective-permute-start | bytes 2359304 | tf_op jit(solution)/shard_map/ppermute | solution.py:332
  87.6 6.6 %copy-start.4 = (bf16[1,2,4,256,256]{4,3,2,1,0:T(8,128)(2,1)S(1)}, bf16[1,2,4,256,256]{4,3,2,1,0:T(8,128)(2,1)}, u32[]{:S(2)}) copy-start(bf16[1,2,4,256,256]{4,3,2,1,0:T(8,128)(2,1)} %param.11) | copy-start | bytes 3145732
  87.6 43.0 %all-to-all-start.1 = ((bf16[8,1,128,1536]{3,2,1,0:T(8,128)(2,1)}), bf16[8,1,128,1536]{3,2,1,0:T(8,128)(2,1)}, u32[]{:S(2)}, u32[]{:S(2)}) async-start(bf16[8,1,128,1536]{3,2,1,0:T(8,128)(2,1)} %get-tuple-element.63), calls=%async_computation.1 | async-start | bytes 6291456 | tf_op jit(solution)/shard_map/all_to_all | solution.py:342
  92.9 19.3 %collective-permute-start.3 = (bf16[768,512]{1,0:T(8,128)(2,1)}, bf16[768,512]{1,0:T(8,128)(2,1)S(1)}, u32[]{:S(2)}, u32[]{:S(2)}) collective-permute-start(bf16[768,512]{1,0:T(8,128)(2,1)} %get-tuple-element.57), channel_id=1, source_target_pairs={{0,8},{8,0},{1,9},{9,1},{2,10},{10,2},{3,11},{11,3},{4,12},{12,4},... | collective-permute-start | bytes 2359304 | tf_op jit(solution)/shard_map/ppermute | solution.py:332
  94.3 29.1 %collective-permute-start.4 = (bf16[2,4,128,256]{3,2,1,0:T(8,128)(2,1)S(1)}, bf16[2,4,128,256]{3,2,1,0:T(8,128)(2,1)}, u32[]{:S(2)}, u32[]{:S(2)}) collective-permute-start(bf16[2,4,128,256]{3,2,1,0:T(8,128)(2,1)S(1)} %slice_select_fusion), channel_id=1, source_target_pairs={{0,8},{8,0},{1,9},{9,1},{2,10},{10,2},{3,11},{11,3},{4,12},{12,4},... | collective-permute-start | bytes 1572872 | tf_op jit(solution)/shard_map/ppermute | solution.py:332
  112.3 11.2 %copy-start.2 = (bf16[1536,512]{1,0:T(8,128)(2,1)}, bf16[1536,512]{1,0:T(8,128)(2,1)S(1)}, u32[]{:S(2)}) copy-start(bf16[1536,512]{1,0:T(8,128)(2,1)S(1)} %constant_dynamic-update-slice_fusion.refs_0_.refs_2_) | copy-start | bytes 4718596
  130.6 5.3 %copy-start.7 = (bf16[1024,512]{1,0:T(8,128)(2,1)S(1)}, bf16[1024,512]{1,0:T(8,128)(2,1)}, u32[]{:S(2)}) copy-start(bf16[1024,512]{1,0:T(8,128)(2,1)} %get-tuple-element.53) | copy-start | bytes 3145732
  130.6 43.0 %all-to-all-start.2 = ((bf16[8,1,128,1536]{3,2,1,0:T(8,128)(2,1)}), bf16[8,1,128,1536]{3,2,1,0:T(8,128)(2,1)}, u32[]{:S(2)}, u32[]{:S(2)}) async-start(bf16[8,1,128,1536]{3,2,1,0:T(8,128)(2,1)} %get-tuple-element.67), calls=%async_computation.2 | async-start | bytes 6291456 | tf_op jit(solution)/shard_map/all_to_all | solution.py:342
  136.0 1.3 copy-start.6
  137.3 1.4 copy-start.8
  138.6 1.3 copy-start.9
  173.7 42.9 %all-to-all-start.3 = ((bf16[8,1,128,1536]{3,2,1,0:T(8,128)(2,1)}), bf16[8,1,128,1536]{3,2,1,0:T(8,128)(2,1)}, u32[]{:S(2)}, u32[]{:S(2)}) async-start(bf16[8,1,128,1536]{3,2,1,0:T(8,128)(2,1)} %bitcast.55), calls=%async_computation.3 | async-start | bytes 6291456 | tf_op jit(solution)/shard_map/all_to_all | solution.py:342
  189.8 22.1 %collective-permute-start.5 = (bf16[2,3,256,256]{3,2,1,0:T(8,128)(2,1)}, bf16[2,3,256,256]{3,2,1,0:T(8,128)(2,1)S(1)}, u32[]{:S(2)}, u32[]{:S(2)}) collective-permute-start(bf16[2,3,256,256]{3,2,1,0:T(8,128)(2,1)} %get-tuple-element.76.refs_0_), channel_id=1, source_target_pairs={{0,64},{64,0},{1,65},{65,1},{2,66},{66,2},{3,67},{67,3},{4,68},{68... | collective-permute-start | bytes 2359304 | tf_op jit(solution)/shard_map/ppermute | solution.py:332
  211.9 4.6 %copy-start.11 = (bf16[2,3,256,256]{3,2,1,0:T(8,128)(2,1)}, bf16[2,3,256,256]{3,2,1,0:T(8,128)(2,1)S(1)}, u32[]{:S(2)}) copy-start(bf16[2,3,256,256]{3,2,1,0:T(8,128)(2,1)S(1)} %collective-permute-done.5.refs_1_) | copy-start | bytes 2359300
  216.6 46.0 %all-to-all-start.4 = ((bf16[8,1,128,1536]{3,2,1,0:T(8,128)(2,1)}), bf16[8,1,128,1536]{3,2,1,0:T(8,128)(2,1)}, u32[]{:S(2)}, u32[]{:S(2)}) async-start(bf16[8,1,128,1536]{3,2,1,0:T(8,128)(2,1)} %bitcast.54), calls=%async_computation.4 | async-start | bytes 6291456 | tf_op jit(solution)/shard_map/all_to_all | solution.py:342
  226.5 36.1 %collective-permute-start.6 = (bf16[1536,512]{1,0:T(8,128)(2,1)}, bf16[1536,512]{1,0:T(8,128)(2,1)S(1)}, u32[]{:S(2)}, u32[]{:S(2)}) collective-permute-start(bf16[1536,512]{1,0:T(8,128)(2,1)} %emit.6), channel_id=1, source_target_pairs={{0,8},{8,0},{1,9},{9,1},{2,10},{10,2},{3,11},{11,3},{4,12},{12,4},... | collective-permute-start | bytes 4718600 | tf_op jit(solution)/shard_map/ppermute | solution.py:332
  262.5 1.1 copy-start.5
  262.5 10.2 %copy-start.18 = (bf16[2,1,256,256]{3,2,1,0:T(8,128)(2,1)S(1)}, bf16[2,1,256,256]{3,2,1,0:T(8,128)(2,1)}, u32[]{:S(2)}) copy-start(bf16[2,1,256,256]{3,2,1,0:T(8,128)(2,1)} %get-tuple-element.84.refs_2_) | copy-start | bytes 786436
  263.7 48.9 %all-to-all-start.5 = ((bf16[8,1,128,1536]{3,2,1,0:T(8,128)(2,1)}), bf16[8,1,128,1536]{3,2,1,0:T(8,128)(2,1)}, u32[]{:S(2)}, u32[]{:S(2)}) async-start(bf16[8,1,128,1536]{3,2,1,0:T(8,128)(2,1)} %bitcast.29), calls=%async_computation.5 | async-start | bytes 6291456 | tf_op jit(solution)/shard_map/all_to_all | solution.py:342
  269.1 43.4 %collective-permute-start.9 = (bf16[2,4,256,256]{3,2,1,0:T(8,128)(2,1)}, bf16[2,4,256,256]{3,2,1,0:T(8,128)(2,1)S(1)}, u32[]{:S(2)}, u32[]{:S(2)}) collective-permute-start(bf16[2,4,256,256]{3,2,1,0:T(8,128)(2,1)} %get-tuple-element.86.refs_4_), channel_id=1, source_target_pairs={{0,64},{64,0},{1,65},{65,1},{2,66},{66,2},{3,67},{67,3},{4,68},{68... | collective-permute-start | bytes 3145736 | tf_op jit(solution)/shard_map/ppermute | solution.py:332
  271.9 40.6 %collective-permute-start.10 = (bf16[2,4,128,256]{3,2,1,0:T(8,128)(2,1)}, bf16[2,4,128,256]{3,2,1,0:T(8,128)(2,1)S(1)}, u32[]{:S(2)}, u32[]{:S(2)}) collective-permute-start(bf16[2,4,128,256]{3,2,1,0:T(8,128)(2,1)} %wgrad.4), channel_id=1, source_target_pairs={{0,8},{8,0},{1,9},{9,1},{2,10},{10,2},{3,11},{11,3},{4,12},{12,4},... | collective-permute-start | bytes 1572872 | tf_op jit(solution)/shard_map/ppermute | solution.py:332
  272.2 40.3 %collective-permute-start.11 = (bf16[2,4,128,256]{3,2,1,0:T(8,128)(2,1)}, bf16[2,4,128,256]{3,2,1,0:T(8,128)(2,1)}, u32[]{:S(2)}, u32[]{:S(2)}) collective-permute-start(bf16[2,4,128,256]{3,2,1,0:T(8,128)(2,1)} %wgrad.4), channel_id=1, source_target_pairs={{0,72},{8,64},{64,8},{72,0},{1,73},{9,65},{65,9},{73,1},{2,74},{10... | collective-permute-start | bytes 1572872 | tf_op jit(solution)/shard_map/ppermute | solution.py:332
  272.8 39.7 %collective-permute-start.8 = (bf16[2,1,256,256]{3,2,1,0:T(8,128)(2,1)S(1)}, bf16[2,1,256,256]{3,2,1,0:T(8,128)(2,1)}, u32[]{:S(2)}, u32[]{:S(2)}) collective-permute-start(bf16[2,1,256,256]{3,2,1,0:T(8,128)(2,1)S(1)} %copy-done.18), channel_id=1, source_target_pairs={{0,64},{64,0},{1,65},{65,1},{2,66},{66,2},{3,67},{67,3},{4,68},{68... | collective-permute-start | bytes 786440 | tf_op jit(solution)/shard_map/ppermute | solution.py:332
  280.4 45.4 %collective-permute-start.7 = (bf16[1536,512]{1,0:T(8,128)(2,1)}, bf16[1536,512]{1,0:T(8,128)(2,1)}, u32[]{:S(2)}, u32[]{:S(2)}) collective-permute-start(bf16[1536,512]{1,0:T(8,128)(2,1)} %emit.7), channel_id=1, source_target_pairs={{0,16},{16,32},{32,48},{1,17},{17,33},{33,49},{2,18},{18,34},{34,5... | collective-permute-start | bytes 4718600 | tf_op jit(solution)/shard_map/ppermute | solution.py:338
  312.5 0.8 copy-start.15
  312.5 1.2 copy-start.10
  313.7 26.0 %all-to-all-start.6 = ((bf16[8,1,128,768]{3,2,1,0:T(8,128)(2,1)}), bf16[8,1,128,768]{3,2,1,0:T(8,128)(2,1)S(1)}, u32[]{:S(2)}, u32[]{:S(2)}) async-start(bf16[8,1,128,768]{3,2,1,0:T(8,128)(2,1)} %bitcast.20), calls=%async_computation.6 | async-start | bytes 3145728 | tf_op jit(solution)/shard_map/all_to_all | solution.py:342
  319.0 18.5 %collective-permute-start.12 = (bf16[2,4,128,256]{3,2,1,0:T(8,128)(2,1)}, bf16[2,4,128,256]{3,2,1,0:T(8,128)(2,1)}, u32[]{:S(2)}, u32[]{:S(2)}) collective-permute-start(bf16[2,4,128,256]{3,2,1,0:T(8,128)(2,1)} %wgrad.5.ma_ref), channel_id=1, source_target_pairs={{0,64},{64,0},{1,65},{65,1},{2,66},{66,2},{3,67},{67,3},{4,68},{68... | collective-permute-start | bytes 1572872 | tf_op jit(solution)/shard_map/ppermute | solution.py:332
  325.4 25.9 %collective-permute-start.14 = (bf16[768,512]{1,0:T(8,128)(2,1)}, bf16[768,512]{1,0:T(8,128)(2,1)}, u32[]{:S(2)}, u32[]{:S(2)}) collective-permute-start(bf16[768,512]{1,0:T(8,128)(2,1)} %emit.10), channel_id=1, source_target_pairs={{0,8},{8,0},{1,9},{9,1},{2,10},{10,2},{3,11},{11,3},{4,12},{12,4},... | collective-permute-start | bytes 2359304 | tf_op jit(solution)/shard_map/ppermute | solution.py:332
  339.7 1.1 copy-start.1
  340.8 29.4 %all-to-all-start.7 = ((bf16[8,1,128,768]{3,2,1,0:T(8,128)(2,1)}), bf16[8,1,128,768]{3,2,1,0:T(8,128)(2,1)}, u32[]{:S(2)}, u32[]{:S(2)}) async-start(bf16[8,1,128,768]{3,2,1,0:T(8,128)(2,1)} %bitcast.19), calls=%async_computation.7 | async-start | bytes 3145728 | tf_op jit(solution)/shard_map/all_to_all | solution.py:342
  345.9 22.2 %collective-permute-start.13 = (bf16[768,512]{1,0:T(8,128)(2,1)}, bf16[768,512]{1,0:T(8,128)(2,1)S(1)}, u32[]{:S(2)}, u32[]{:S(2)}) collective-permute-start(bf16[768,512]{1,0:T(8,128)(2,1)} %emit.8), channel_id=1, source_target_pairs={{0,8},{8,0},{1,9},{9,1},{2,10},{10,2},{3,11},{11,3},{4,12},{12,4},... | collective-permute-start | bytes 2359304 | tf_op jit(solution)/shard_map/ppermute | solution.py:332
  355.4 20.4 %collective-permute-start.15 = (bf16[768,512]{1,0:T(8,128)(2,1)}, bf16[768,512]{1,0:T(8,128)(2,1)S(1)}, u32[]{:S(2)}, u32[]{:S(2)}) collective-permute-start(bf16[768,512]{1,0:T(8,128)(2,1)} %emit.11), channel_id=1, source_target_pairs={{16,0},{32,16},{48,32},{17,1},{33,17},{49,33},{18,2},{34,18},{50,3... | collective-permute-start | bytes 2359304 | tf_op jit(solution)/shard_map/ppermute | solution.py:338
  368.1 2.1 copy-start.12
  368.1 14.4 %collective-permute-start.17 = (bf16[2,4,256,128]{3,2,1,0:T(8,128)(2,1)}, bf16[2,4,256,128]{3,2,1,0:T(8,128)(2,1)}, u32[]{:S(2)}, u32[]{:S(2)}) collective-permute-start(bf16[2,4,256,128]{3,2,1,0:T(8,128)(2,1)} %wgrad.6), channel_id=1, source_target_pairs={{0,8},{8,0},{1,9},{9,1},{2,10},{10,2},{3,11},{11,3},{4,12},{12,4},... | collective-permute-start | bytes 1572872 | tf_op jit(solution)/shard_map/ppermute | solution.py:332
  369.3 13.9 %collective-permute-start.18 = (bf16[2,4,256,128]{3,2,1,0:T(8,128)(2,1)}, bf16[2,4,256,128]{3,2,1,0:T(8,128)(2,1)}, u32[]{:S(2)}, u32[]{:S(2)}) collective-permute-start(bf16[2,4,256,128]{3,2,1,0:T(8,128)(2,1)} %wgrad.6), channel_id=1, source_target_pairs={{0,72},{8,64},{64,8},{72,0},{1,73},{9,65},{65,9},{73,1},{2,74},{10... | collective-permute-start | bytes 1572872 | tf_op jit(solution)/shard_map/ppermute | solution.py:332
  375.8 6.8 %copy-start.13 = (bf16[768,512]{1,0:T(8,128)(2,1)}, bf16[768,512]{1,0:T(8,128)(2,1)S(1)}, u32[]{:S(2)}) copy-start(bf16[768,512]{1,0:T(8,128)(2,1)S(1)} %collective-permute-done.15.value_ref) | copy-start | bytes 2359300
  375.8 19.7 %collective-permute-start.16 = (bf16[768,512]{1,0:T(8,128)(2,1)}, bf16[768,512]{1,0:T(8,128)(2,1)S(1)}, u32[]{:S(2)}, u32[]{:S(2)}) collective-permute-start(bf16[768,512]{1,0:T(8,128)(2,1)} %emit.9), channel_id=1, source_target_pairs={{16,0},{32,16},{48,32},{17,1},{33,17},{49,33},{18,2},{34,18},{50,3... | collective-permute-start | bytes 2359304 | tf_op jit(solution)/shard_map/ppermute | solution.py:338
  383.2 15.3 %collective-permute-start.19 = (bf16[2,4,256,128]{3,2,1,0:T(8,128)(2,1)}, bf16[2,4,256,128]{3,2,1,0:T(8,128)(2,1)S(1)}, u32[]{:S(2)}, u32[]{:S(2)}) collective-permute-start(bf16[2,4,256,128]{3,2,1,0:T(8,128)(2,1)} %wgrad.7.ma_ref), channel_id=1, source_target_pairs={{0,64},{64,0},{1,65},{65,1},{2,66},{66,2},{3,67},{67,3},{4,68},{68... | collective-permute-start | bytes 1572872 | tf_op jit(solution)/shard_map/ppermute | solution.py:332
  395.5 0.9 copy-start.14
  398.4 0.8 copy-start.16

commit v4 on v3

--- a/solution.py
+++ b/solution.py
@@ -378,19 +378,22 @@
     )(*arrays)
 
 
-def paired_body(side_ref, ma_ref, mb_ref, ta_ref, tb_ref, out_ref):
+def paired_body(side_ref, ma_ref, mb_ref, ta_ref, tb_ref, *rest):
     step = pl.program_id(0)
+    out_ref = rest[0] if len(rest) == 1 else rest[2]
 
     @pl.when(step == 0)
     def _():
         out_ref[...] = ma_ref[...].astype(F32) + mb_ref[...].astype(F32)
+        if len(rest) > 1:
+            rest[3][...] = rest[0][...]
 
     @pl.when(step == 1)
     def _():
         out_ref[...] = ta_ref[...].astype(F32) + tb_ref[...].astype(F32)
 
 
-def paired(side, mine, theirs, dim):
+def paired(side, mine, theirs, dim, value=None, into=None):
     shape = mine[0].shape
     whole = pl.BlockSpec(shape, lambda i, s: (0,) * len(shape))
 
@@ -399,19 +402,25 @@
         return tuple(half if n == dim else 0 for n in range(len(shape)))
 
     full = tuple(2 * size if n == dim else size for n, size in enumerate(shape))
+    in_specs, out_specs = [whole] * 4, [pl.BlockSpec(shape, where)]
+    out_shape, extra = [jax.ShapeDtypeStruct(full, F32)], ()
+    if value is not None:
+        extra = (value, into)
+        last = into.shape[0] // value.shape[0] - 1
+        in_specs += [pl.BlockSpec(value.shape, lambda i, s: (0, 0)), pl.BlockSpec(memory_space=pl.ANY)]
+        out_specs.append(pl.BlockSpec(value.shape, lambda i, s: (last, 0)))
+        out_shape.append(jax.ShapeDtypeStruct(into.shape, into.dtype))
     return pl.pallas_call(
         paired_body,
         grid_spec=pltpu.PrefetchScalarGridSpec(
-            num_scalar_prefetch=1,
-            grid=(2,),
-            in_specs=[whole] * 4,
-            out_specs=pl.BlockSpec(shape, where),
+            num_scalar_prefetch=1, grid=(2,), in_specs=in_specs, out_specs=out_specs
         ),
-        out_shape=jax.ShapeDtypeStruct(full, F32),
+        out_shape=out_shape,
+        input_output_aliases={6: 1} if extra else {},
         compiler_params=params(VMEM_MIB),
         cost_estimate=cost(1, 1),
         name="paired",
-    )(side, *mine, *theirs)
+    )(side, *mine, *theirs, *extra)
 
 
 def place_body(value_ref, *rest):
@@ -515,9 +524,9 @@
         groups, expand, True,
     )
     d1o = swapped(behind(g1o, (t1x, t1d)), "dp")
-    grad_four = paired(side, (g4o, d4o), (t4x, t4d), 2)
-    dx_prev = place(dx2, dx_prev, 1, 2)
-    grad_one = paired(side, (behind(g1o, (dx_prev, grad_four)), d1o), (t1x, t1d), 3)
+    (grad_four,) = paired(side, (g4o, d4o), (t4x, t4d), 2)
+    mine = (behind(g1o, grad_four), d1o)
+    grad_one, dx_prev = paired(side, mine, (t1x, t1d), 3, dx2, dx_prev)
     return (
         y_next[None], dx_prev[None], grad_one[None], grad_two[None], grad_three[None], grad_four[None],
     )

time: 405 us -> 405 us (level)
    ppermute x17, waiting for transfers between devices: 145 us -> 152 us  [swapped(): return lax.ppermute(value, axes, [(i, count - 1 - i) for i in range(count)])]
    ppermute x3, waiting for transfers between devices: 7.68 us -> 1.57 us  [shifted(): lax.ppermute(value, axis, [(source, source + steps) for source in range(l...]
  transfers between devices with their start and end apart: 28 -> 28, of which waited for: 16 -> 16; matrix products, arithmetic and copies ran while one was open for 2% -> 2% of each run, Pallas kernels for 30% -> 29%
where the time goes in v4:
time: 405 us; the launch traced here: 402 us
  waiting for transfers between devices  182 us (45%)
  Pallas kernels  131 us (32%)
  starting transfers between devices  72.9 us (18%)
  local copies, waits for them, and re-layouts  13.7 us (3%)
    ppermute x17, waiting for transfers between devices, swapped(): return lax.ppermute(value, axes, [(i, count - 1 - i) for i in range(count)])  152 us
    all_to_all x8, starting transfers between devices, spread_out(): return lax.all_to_all(value, YC, split_axis=0, concat_axis=0, tiled=True)  42.9 us
    pallas_call x3, Pallas kernels, backward(): pl.pallas_call(functools.partial(backward_body, steps), grid_spec=pltpu.P...  30 us
    all_to_all x8, waiting for transfers between devices, spread_out(): return lax.all_to_all(value, YC, split_axis=0, concat_axis=0, tiled=True)  28.2 us
    pallas_call x6, Pallas kernels, emit(): pl.pallas_call(functools.partial(emit_body, add), grid=(tokens // tile,),...  25.2 us
    ppermute x17, starting transfers between devices, swapped(): return lax.ppermute(value, axes, [(i, count - 1 - i) for i in range(count)])  22.7 us
    pallas_call x4, Pallas kernels, wgrad(): pl.pallas_call(functools.partial(wgrad_body, swap, groups, expand, count)...  21.8 us
    pallas_call x3, Pallas kernels, lift(): pl.pallas_call(functools.partial(lift_body, swaps, steps), grid_spec=pltp...  20.7 us
  transfers between devices with their start and end apart: 28, of which 16 were waited for; matrix products, arithmetic and copies ran while one was open for 2% of the time, Pallas kernels for 29%

profile of v4, /device:TPU:1, one launch (start us, length us, event | category | flops | bytes accessed | tf_op | source)
XLA Modules:
  0.0 401.5 jit_solution(6154067019383066310)
XLA Ops:
  0.6 9.5 %lift.3 = (bf16[8,2,128,1536]{3,2,1,0:T(8,128)(2,1)}, bf16[1024,512]{1,0:T(8,128)(2,1)}, bf16[1024,512]{1,0:T(8,128)(2,1)}) custom-call(s32[1]{0:T(128)} %bitcast.side_ref, bf16[1536,512]{1,0:T(8,128)(2,1)} %bitcast.45, bf16[1536,512]{1,0:T(8,128)(2,1)} %bitcast.38, bf16[2,4,256,256]{3,2,1,0:T(8,128)(2,1)} %bitcast.49, bf16[2,4,256,256]{3,2,1,0:T(8,128)(2,1)} %bitcast.51), custom_call_target="tpu_custom_call" | custom-call | flops 128849016 | bytes 188743 | tf_op jit(solution)/shard_map/lift/pallas_call | solution.py:92
  10.1 6.1 %all-to-all-start = ((bf16[8,2,128,1536]{3,2,1,0:T(8,128)(2,1)}), bf16[8,2,128,1536]{3,2,1,0:T(8,128)(2,1)}, u32[]{:S(2)}, u32[]{:S(2)}) async-start(bf16[8,2,128,1536]{3,2,1,0:T(8,128)(2,1)} %get-tuple-element.63), calls=%async_computation | async-start | bytes 12582912 | tf_op jit(solution)/shard_map/all_to_all | solution.py:342
  20.3 43.2 %collective-permute-done.1.refs_1_ = bf16[2,4,256,128]{3,2,1,0:T(8,128)(2,1)S(1)} collective-permute-done((bf16[2,4,256,128]{3,2,1,0:T(8,128)(2,1)S(1)}, bf16[2,4,256,128]{3,2,1,0:T(8,128)(2,1)S(1)}, u32[]{:S(2)}, u32[]{:S(2)}) %collective-permute-start.1) | collective-permute-done | bytes 524320 | tf_op jit(solution)/shard_map/ppermute | solution.py:332
  65.6 5.6 %lift.4 = (bf16[8,1,128,1536]{3,2,1,0:T(8,128)(2,1)}, bf16[1024,512]{1,0:T(8,128)(2,1)}) custom-call(s32[1]{0:T(128)} %constant.8.clone.1.side_ref, bf16[1536,512]{1,0:T(8,128)(2,1)} %copy-done.3, bf16[2,4,256,128]{3,2,1,0:T(8,128)(2,1)} %copy-done.17), custom_call_target="tpu_custom_call" | custom-call | flops 64424508 | bytes 94371 | tf_op jit(solution)/shard_map/lift/pallas_call | solution.py:92
  71.3 11.5 %collective-permute-done.2 = bf16[768,512]{1,0:T(8,128)(2,1)} collective-permute-done((bf16[768,512]{1,0:T(8,128)(2,1)}, bf16[768,512]{1,0:T(8,128)(2,1)}, u32[]{:S(2)}, u32[]{:S(2)}) %collective-permute-start.2) | collective-permute-done | bytes 786464 | tf_op jit(solution)/shard_map/ppermute | solution.py:332
  82.8 4.8 %all-to-all-done = bf16[8,2,128,1536]{3,2,1,0:T(8,128)(2,1)} async-done(((bf16[8,2,128,1536]{3,2,1,0:T(8,128)(2,1)}), bf16[8,2,128,1536]{3,2,1,0:T(8,128)(2,1)}, u32[]{:S(2)}, u32[]{:S(2)}) %all-to-all-start) | async-done | bytes 6291488 | tf_op jit(solution)/shard_map/all_to_all | solution.py:342
  87.6 5.3 %all-to-all-start.1 = ((bf16[8,1,128,1536]{3,2,1,0:T(8,128)(2,1)}), bf16[8,1,128,1536]{3,2,1,0:T(8,128)(2,1)}, u32[]{:S(2)}, u32[]{:S(2)}) async-start(bf16[8,1,128,1536]{3,2,1,0:T(8,128)(2,1)} %get-tuple-element.65), calls=%async_computation.1 | async-start | bytes 6291456 | tf_op jit(solution)/shard_map/all_to_all | solution.py:342
  95.7 16.5 %collective-permute-done.3 = bf16[768,512]{1,0:T(8,128)(2,1)S(1)} collective-permute-done((bf16[768,512]{1,0:T(8,128)(2,1)}, bf16[768,512]{1,0:T(8,128)(2,1)S(1)}, u32[]{:S(2)}, u32[]{:S(2)}) %collective-permute-start.3) | collective-permute-done | bytes 786464 | tf_op jit(solution)/shard_map/ppermute | solution.py:332
  112.2 11.2 %collective-permute-done.4.refs_1_ = bf16[2,4,128,256]{3,2,1,0:T(8,128)(2,1)} collective-permute-done((bf16[2,4,128,256]{3,2,1,0:T(8,128)(2,1)S(1)}, bf16[2,4,128,256]{3,2,1,0:T(8,128)(2,1)}, u32[]{:S(2)}, u32[]{:S(2)}) %collective-permute-start.4) | collective-permute-done | bytes 524320 | tf_op jit(solution)/shard_map/ppermute | solution.py:332
  123.4 5.6 %lift.5 = (bf16[8,1,128,1536]{3,2,1,0:T(8,128)(2,1)}, bf16[1024,512]{1,0:T(8,128)(2,1)}) custom-call(s32[1]{0:T(128)} %constant.8.clone.1.side_ref, bf16[1536,512]{1,0:T(8,128)(2,1)} %copy-done.2, bf16[2,4,128,256]{3,2,1,0:T(8,128)(2,1)} %collective-permute-done.4.refs_1_), custom_call_target="tpu_custom_call" | custom-call | flops 64424508 | bytes 94371 | tf_op jit(solution)/shard_map/lift/pallas_call | solution.py:92
  130.6 5.3 %all-to-all-start.2 = ((bf16[8,1,128,1536]{3,2,1,0:T(8,128)(2,1)}), bf16[8,1,128,1536]{3,2,1,0:T(8,128)(2,1)}, u32[]{:S(2)}, u32[]{:S(2)}) async-start(bf16[8,1,128,1536]{3,2,1,0:T(8,128)(2,1)} %get-tuple-element.69), calls=%async_computation.2 | async-start | bytes 6291456 | tf_op jit(solution)/shard_map/all_to_all | solution.py:342
  141.2 17.4 %forward.1 = (bf16[8,8,16,1536]{3,2,1,0:T(8,128)(2,1)}, bf16[8,8,16,1536]{3,2,1,0:T(8,128)(2,1)}) custom-call(s32[1]{0:T(128)} %bitcast.side_ref, bf16[8,2,8,16,1536]{4,3,2,1,0:T(8,128)(2,1)} %bitcast.11.ro_ref.go_ref, bf16[8,1,8,16,1536]{4,3,2,1,0:T(8,128)(2,1)} %bitcast.12.rp_ref, bf16[8,256,256]{2,1,0:T(8,128)(2,1)} %bitcast.30, bf16[8,256,256]{2,1,0:T(8,128)(2,1)} %bitcast.34), custom_call_target="tpu_custom_call" | custom-call | flops 64424508 | bytes 251658 | tf_op jit(solution)/shard_map/forward/pallas_call | solution.py:145
  158.6 15.0 %all-to-all-done.2 = bf16[8,1,128,1536]{3,2,1,0:T(8,128)(2,1)} async-done(((bf16[8,1,128,1536]{3,2,1,0:T(8,128)(2,1)}), bf16[8,1,128,1536]{3,2,1,0:T(8,128)(2,1)}, u32[]{:S(2)}, u32[]{:S(2)}) %all-to-all-start.2) | async-done | bytes 3145760 | tf_op jit(solution)/shard_map/all_to_all | solution.py:342
  173.6 5.2 %all-to-all-start.3 = ((bf16[8,1,128,1536]{3,2,1,0:T(8,128)(2,1)}), bf16[8,1,128,1536]{3,2,1,0:T(8,128)(2,1)}, u32[]{:S(2)}, u32[]{:S(2)}) async-start(bf16[8,1,128,1536]{3,2,1,0:T(8,128)(2,1)} %bitcast.55), calls=%async_computation.3 | async-start | bytes 6291456 | tf_op jit(solution)/shard_map/all_to_all | solution.py:342
  178.8 11.0 %backward.3 = (bf16[8,8,16,1536]{3,2,1,0:T(8,128)(2,1)}, bf16[2,3,256,256]{3,2,1,0:T(8,128)(2,1)}, bf16[8,8,16,768]{3,2,1,0:T(8,128)(2,1)}, bf16[8,8,16,768]{3,2,1,0:T(8,128)(2,1)}) custom-call(s32[1]{0:T(128)} %bitcast.side_ref, bf16[8,2,8,16,1536]{4,3,2,1,0:T(8,128)(2,1)} %bitcast.11.ro_ref.go_ref, bf16[8,1,8,16,1536]{4,3,2,1,0:T(8,128)(2,1)} %bitcast.12.rp_ref, ...), custom_call_target="tpu_custom_call" | custom-call | flops 60397976 | bytes 141557 | tf_op jit(solution)/shard_map/backward/pallas_call | solution.py:217
  189.8 3.0 collective-permute-start.5
  192.9 5.0 %backward.4 = (bf16[8,8,16,1536]{3,2,1,0:T(8,128)(2,1)}, bf16[2,1,256,256]{3,2,1,0:T(8,128)(2,1)}, bf16[8,8,16,768]{3,2,1,0:T(8,128)(2,1)}, bf16[8,8,16,768]{3,2,1,0:T(8,128)(2,1)}) custom-call(s32[1]{0:T(128)} %bitcast.side_ref, bf16[8,2,8,16,1536]{4,3,2,1,0:T(8,128)(2,1)} %bitcast.11.ro_ref.go_ref, ...), custom_call_target="tpu_custom_call", output_to_operand_aliasing={{0}: (7, {}), {2}: (8, {}), {3}: (9, {})} | custom-call | flops 20132660 | bytes 47185 | tf_op jit(solution)/shard_map/backward/pallas_call | solution.py:217
  197.9 14.1 %backward.5 = (bf16[8,8,16,1536]{3,2,1,0:T(8,128)(2,1)}, bf16[2,4,256,256]{3,2,1,0:T(8,128)(2,1)}, bf16[8,8,16,768]{3,2,1,0:T(8,128)(2,1)}, bf16[8,8,16,768]{3,2,1,0:T(8,128)(2,1)}) custom-call(s32[1]{0:T(128)} %bitcast.side_ref, bf16[8,2,8,16,1536]{4,3,2,1,0:T(8,128)(2,1)} %bitcast.11.ro_ref.go_ref, ...), custom_call_target="tpu_custom_call", output_to_operand_aliasing={{0}: (7, {}), {2}: (8, {}), {3}: (9, {})} | custom-call | flops 80530640 | bytes 188743 | tf_op jit(solution)/shard_map/backward/pallas_call | solution.py:217
  211.9 4.6 %all-to-all-done.3.s_ref.refs_0_.refs_1_ = bf16[8,1,128,1536]{3,2,1,0:T(8,128)(2,1)} async-done(((bf16[8,1,128,1536]{3,2,1,0:T(8,128)(2,1)}), bf16[8,1,128,1536]{3,2,1,0:T(8,128)(2,1)}, u32[]{:S(2)}, u32[]{:S(2)}) %all-to-all-start.3) | async-done | bytes 3145760 | tf_op jit(solution)/shard_map/all_to_all | solution.py:342
  216.5 5.2 %all-to-all-start.4 = ((bf16[8,1,128,1536]{3,2,1,0:T(8,128)(2,1)}), bf16[8,1,128,1536]{3,2,1,0:T(8,128)(2,1)}, u32[]{:S(2)}, u32[]{:S(2)}) async-start(bf16[8,1,128,1536]{3,2,1,0:T(8,128)(2,1)} %bitcast.54), calls=%async_computation.4 | async-start | bytes 6291456 | tf_op jit(solution)/shard_map/all_to_all | solution.py:342
  221.7 4.7 %emit.6 = bf16[1536,512]{1,0:T(8,128)(2,1)} custom-call(bf16[8,1,128,1536]{3,2,1,0:T(8,128)(2,1)} %all-to-all-done.3.s_ref.refs_0_.refs_1_, bf16[512,1024]{1,0:T(8,128)(2,1)} %bitcast.53), custom_call_target="tpu_custom_call" | custom-call | flops 32212254 | bytes 125829 | tf_op jit(solution)/shard_map/emit/pallas_call | solution.py:252
  227.7 5.4 %wgrad.4 = bf16[2,4,128,256]{3,2,1,0:T(8,128)(2,1)} custom-call(bf16[8,1,128,1536]{3,2,1,0:T(8,128)(2,1)} %all-to-all-done.3.s_ref.refs_0_.refs_1_, bf16[8,1,128,1536]{3,2,1,0:T(8,128)(2,1)} %all-to-all-done.3.s_ref.refs_0_.refs_1_, bf16[1536,512]{1,0:T(8,128)(2,1)} %copy-done.2), custom_call_target="tpu_custom_call" | custom-call | flops 32212254 | bytes 94371 | tf_op jit(solution)/shard_map/wgrad/pallas_call | solution.py:313
  233.2 29.3 %collective-permute-done.6.rest_0_ = bf16[1536,512]{1,0:T(8,128)(2,1)S(1)} collective-permute-done((bf16[1536,512]{1,0:T(8,128)(2,1)}, bf16[1536,512]{1,0:T(8,128)(2,1)S(1)}, u32[]{:S(2)}, u32[]{:S(2)}) %collective-permute-start.6) | collective-permute-done | bytes 1572896 | tf_op jit(solution)/shard_map/ppermute | solution.py:332
  263.6 5.4 %all-to-all-start.5 = ((bf16[8,1,128,1536]{3,2,1,0:T(8,128)(2,1)}), bf16[8,1,128,1536]{3,2,1,0:T(8,128)(2,1)}, u32[]{:S(2)}, u32[]{:S(2)}) async-start(bf16[8,1,128,1536]{3,2,1,0:T(8,128)(2,1)} %bitcast.29), calls=%async_computation.5 | async-start | bytes 6291456 | tf_op jit(solution)/shard_map/all_to_all | solution.py:342
  269.1 2.8 collective-permute-start.9
  272.8 2.4 collective-permute-start.8
  275.2 5.2 %emit.7 = bf16[1536,512]{1,0:T(8,128)(2,1)} custom-call(bf16[8,1,128,1536]{3,2,1,0:T(8,128)(2,1)} %all-to-all-done.4.s_ref.refs_0_.refs_1_, bf16[512,1024]{1,0:T(8,128)(2,1)} %bitcast.48, bf16[1536,512]{1,0:T(8,128)(2,1)} %copy-done.5), custom_call_target="tpu_custom_call" | custom-call | flops 32212254 | bytes 125829 | tf_op jit(solution)/shard_map/emit/pallas_call | solution.py:252
  280.4 4.8 %collective-permute-start.7 = (bf16[1536,512]{1,0:T(8,128)(2,1)}, bf16[1536,512]{1,0:T(8,128)(2,1)}, u32[]{:S(2)}, u32[]{:S(2)}) collective-permute-start(bf16[1536,512]{1,0:T(8,128)(2,1)} %emit.7), channel_id=1, source_target_pairs={{0,16},{16,32},{32,48},{1,17},{17,33},{33,49},{2,18},{18,34},{34,5... | collective-permute-start | bytes 4718600 | tf_op jit(solution)/shard_map/ppermute | solution.py:338
  285.2 5.5 %wgrad.5.ma_ref = bf16[2,4,128,256]{3,2,1,0:T(8,128)(2,1)} custom-call(bf16[8,1,128,1536]{3,2,1,0:T(8,128)(2,1)} %all-to-all-done.4.s_ref.refs_0_.refs_1_, bf16[8,1,128,1536]{3,2,1,0:T(8,128)(2,1)} %all-to-all-done.4.s_ref.refs_0_.refs_1_, bf16[1536,512]{1,0:T(8,128)(2,1)} %bitcast.39), custom_call_target="tpu_custom_call" | custom-call | flops 32212254 | bytes 94371 | tf_op jit(solution)/shard_map/wgrad/pallas_call | solution.py:313
  290.6 21.9 %collective-permute-done.8.refs_3_ = bf16[2,1,256,256]{3,2,1,0:T(8,128)(2,1)} collective-permute-done((bf16[2,1,256,256]{3,2,1,0:T(8,128)(2,1)S(1)}, bf16[2,1,256,256]{3,2,1,0:T(8,128)(2,1)}, u32[]{:S(2)}, u32[]{:S(2)}) %collective-permute-start.8) | collective-permute-done | bytes 262176 | tf_op jit(solution)/shard_map/ppermute | solution.py:332
  313.7 5.3 %all-to-all-start.6 = ((bf16[8,1,128,768]{3,2,1,0:T(8,128)(2,1)}), bf16[8,1,128,768]{3,2,1,0:T(8,128)(2,1)S(1)}, u32[]{:S(2)}, u32[]{:S(2)}) async-start(bf16[8,1,128,768]{3,2,1,0:T(8,128)(2,1)} %bitcast.19), calls=%async_computation.6 | async-start | bytes 3145728 | tf_op jit(solution)/shard_map/all_to_all | solution.py:342
  319.0 2.8 collective-permute-start.12
  321.8 3.6 emit.10
  325.8 2.7 place.2
  328.4 3.6 emit.8
  332.0 5.5 %wgrad.6 = bf16[2,4,256,128]{3,2,1,0:T(8,128)(2,1)} custom-call(bf16[8,1,128,1536]{3,2,1,0:T(8,128)(2,1)} %all-to-all-done.5.s_ref.refs_0_.refs_1_, bf16[8,1,128,1536]{3,2,1,0:T(8,128)(2,1)} %all-to-all-done.5.s_ref.refs_0_.refs_1_, bf16[1536,512]{1,0:T(8,128)(2,1)} %copy-done.3), custom_call_target="tpu_custom_call" | custom-call | flops 32212254 | bytes 94371 | tf_op jit(solution)/shard_map/wgrad/pallas_call | solution.py:313
  337.5 2.2 all-to-all-done.6.refs_0_.s_ref
  340.8 5.1 %all-to-all-start.7 = ((bf16[8,1,128,768]{3,2,1,0:T(8,128)(2,1)}), bf16[8,1,128,768]{3,2,1,0:T(8,128)(2,1)}, u32[]{:S(2)}, u32[]{:S(2)}) async-start(bf16[8,1,128,768]{3,2,1,0:T(8,128)(2,1)} %bitcast.21), calls=%async_computation.7 | async-start | bytes 3145728 | tf_op jit(solution)/shard_map/all_to_all | solution.py:342
  347.2 4.2 %collective-permute-done.14.rest_0_ = bf16[768,512]{1,0:T(8,128)(2,1)} collective-permute-done((bf16[768,512]{1,0:T(8,128)(2,1)}, bf16[768,512]{1,0:T(8,128)(2,1)}, u32[]{:S(2)}, u32[]{:S(2)}) %collective-permute-start.14) | collective-permute-done | bytes 786464 | tf_op jit(solution)/shard_map/ppermute | solution.py:332
  351.4 4.0 emit.11
  356.7 4.5 %join.1 = (f32[8,256,256]{2,1,0:T(8,128)}, f32[8,256,256]{2,1,0:T(8,128)}) custom-call(bf16[2,3,256,256]{3,2,1,0:T(8,128)(2,1)} %get-tuple-element.78.refs_0_, bf16[2,3,256,256]{3,2,1,0:T(8,128)(2,1)} %copy-done.11, bf16[2,1,256,256]{3,2,1,0:T(8,128)(2,1)} %get-tuple-element.85.refs_2_, bf16[2,1,256,256]{3,2,1,0:T(8,128)(2,1)} %collective-permute-done.8.refs_3_, ...), custom_call_target="tpu_custom_call" | custom-call | tf_op jit(solution)/shard_map/join/pallas_call | solution.py:369
  361.2 7.0 %collective-permute-done.13.rest_0_ = bf16[768,512]{1,0:T(8,128)(2,1)S(1)} collective-permute-done((bf16[768,512]{1,0:T(8,128)(2,1)}, bf16[768,512]{1,0:T(8,128)(2,1)S(1)}, u32[]{:S(2)}, u32[]{:S(2)}) %collective-permute-start.13) | collective-permute-done | bytes 786464 | tf_op jit(solution)/shard_map/ppermute | solution.py:332
  370.3 4.0 emit.9
  377.1 5.5 %wgrad.7.ma_ref = bf16[2,4,256,128]{3,2,1,0:T(8,128)(2,1)} custom-call(bf16[8,1,128,768]{3,2,1,0:T(8,128)(2,1)} %copy-done.1, bf16[8,1,128,768]{3,2,1,0:T(8,128)(2,1)} %all-to-all-done.7.s_ref.refs_1_, bf16[1536,512]{1,0:T(8,128)(2,1)} %bitcast.47), custom_call_target="tpu_custom_call" | custom-call | flops 32212254 | bytes 94371 | tf_op jit(solution)/shard_map/wgrad/pallas_call | solution.py:313
  384.4 2.9 paired.2
  387.3 2.1 place.3.rest_1_
  389.4 6.9 %collective-permute-done.17.mb_ref = bf16[2,4,256,128]{3,2,1,0:T(8,128)(2,1)S(1)} collective-permute-done((bf16[2,4,256,128]{3,2,1,0:T(8,128)(2,1)}, bf16[2,4,256,128]{3,2,1,0:T(8,128)(2,1)S(1)}, u32[]{:S(2)}, u32[]{:S(2)}) %collective-permute-start.17) | collective-permute-done | bytes 524320 | tf_op jit(solution)/shard_map/ppermute | solution.py:332
  398.1 3.5 paired.3
  (77 shorter events, 33.0 us)
Async XLA Ops:
  10.1 77.5 %all-to-all-start = ((bf16[8,2,128,1536]{3,2,1,0:T(8,128)(2,1)}), bf16[8,2,128,1536]{3,2,1,0:T(8,128)(2,1)}, u32[]{:S(2)}, u32[]{:S(2)}) async-start(bf16[8,2,128,1536]{3,2,1,0:T(8,128)(2,1)} %get-tuple-element.63), calls=%async_computation | async-start | bytes 12582912 | tf_op jit(solution)/shard_map/all_to_all | solution.py:342
  16.2 2.9 copy-start
  16.2 47.3 %collective-permute-start = (bf16[1536,512]{1,0:T(8,128)(2,1)}, bf16[1536,512]{1,0:T(8,128)(2,1)S(1)}, u32[]{:S(2)}, u32[]{:S(2)}) collective-permute-start(bf16[1536,512]{1,0:T(8,128)(2,1)} %bitcast.46), channel_id=1, source_target_pairs={{0,8},{8,0},{1,9},{9,1},{2,10},{10,2},{3,11},{11,3},{4,12},{12,4},... | collective-permute-start | bytes 4718600 | tf_op jit(solution)/shard_map/ppermute | solution.py:332
  18.8 44.8 %collective-permute-start.1 = (bf16[2,4,256,128]{3,2,1,0:T(8,128)(2,1)S(1)}, bf16[2,4,256,128]{3,2,1,0:T(8,128)(2,1)S(1)}, u32[]{:S(2)}, u32[]{:S(2)}) collective-permute-start(bf16[2,4,256,128]{3,2,1,0:T(8,128)(2,1)S(1)} %slice_select_fusion.1), channel_id=1, source_target_pairs={{0,8},{8,0},{1,9},{9,1},{2,10},{10,2},{3,11},{11,3},{4,12},{12,4},... | collective-permute-start | bytes 1572872 | tf_op jit(solution)/shard_map/ppermute | solution.py:332
  63.5 0.8 copy-start.17
  64.3 1.3 copy-start.3
  64.3 18.4 %collective-permute-start.2 = (bf16[768,512]{1,0:T(8,128)(2,1)}, bf16[768,512]{1,0:T(8,128)(2,1)}, u32[]{:S(2)}, u32[]{:S(2)}) collective-permute-start(bf16[768,512]{1,0:T(8,128)(2,1)} %get-tuple-element.58), channel_id=1, source_target_pairs={{0,8},{8,0},{1,9},{9,1},{2,10},{10,2},{3,11},{11,3},{4,12},{12,4},... | collective-permute-start | bytes 2359304 | tf_op jit(solution)/shard_map/ppermute | solution.py:332
  87.6 6.6 %copy-start.4 = (bf16[1,2,4,256,256]{4,3,2,1,0:T(8,128)(2,1)S(1)}, bf16[1,2,4,256,256]{4,3,2,1,0:T(8,128)(2,1)}, u32[]{:S(2)}) copy-start(bf16[1,2,4,256,256]{4,3,2,1,0:T(8,128)(2,1)} %param.11) | copy-start | bytes 3145732
  87.6 43.0 %all-to-all-start.1 = ((bf16[8,1,128,1536]{3,2,1,0:T(8,128)(2,1)}), bf16[8,1,128,1536]{3,2,1,0:T(8,128)(2,1)}, u32[]{:S(2)}, u32[]{:S(2)}) async-start(bf16[8,1,128,1536]{3,2,1,0:T(8,128)(2,1)} %get-tuple-element.65), calls=%async_computation.1 | async-start | bytes 6291456 | tf_op jit(solution)/shard_map/all_to_all | solution.py:342
  92.9 19.3 %collective-permute-start.3 = (bf16[768,512]{1,0:T(8,128)(2,1)}, bf16[768,512]{1,0:T(8,128)(2,1)S(1)}, u32[]{:S(2)}, u32[]{:S(2)}) collective-permute-start(bf16[768,512]{1,0:T(8,128)(2,1)} %get-tuple-element.59), channel_id=1, source_target_pairs={{0,8},{8,0},{1,9},{9,1},{2,10},{10,2},{3,11},{11,3},{4,12},{12,4},... | collective-permute-start | bytes 2359304 | tf_op jit(solution)/shard_map/ppermute | solution.py:332
  94.3 29.1 %collective-permute-start.4 = (bf16[2,4,128,256]{3,2,1,0:T(8,128)(2,1)S(1)}, bf16[2,4,128,256]{3,2,1,0:T(8,128)(2,1)}, u32[]{:S(2)}, u32[]{:S(2)}) collective-permute-start(bf16[2,4,128,256]{3,2,1,0:T(8,128)(2,1)S(1)} %slice_select_fusion), channel_id=1, source_target_pairs={{0,8},{8,0},{1,9},{9,1},{2,10},{10,2},{3,11},{11,3},{4,12},{12,4},... | collective-permute-start | bytes 1572872 | tf_op jit(solution)/shard_map/ppermute | solution.py:332
  112.2 11.2 %copy-start.2 = (bf16[1536,512]{1,0:T(8,128)(2,1)}, bf16[1536,512]{1,0:T(8,128)(2,1)S(1)}, u32[]{:S(2)}) copy-start(bf16[1536,512]{1,0:T(8,128)(2,1)S(1)} %constant_dynamic-update-slice_fusion.refs_0_.refs_2_) | copy-start | bytes 4718596
  130.6 5.3 %copy-start.7 = (bf16[1024,512]{1,0:T(8,128)(2,1)S(1)}, bf16[1024,512]{1,0:T(8,128)(2,1)}, u32[]{:S(2)}) copy-start(bf16[1024,512]{1,0:T(8,128)(2,1)} %get-tuple-element.55) | copy-start | bytes 3145732
  130.6 43.0 %all-to-all-start.2 = ((bf16[8,1,128,1536]{3,2,1,0:T(8,128)(2,1)}), bf16[8,1,128,1536]{3,2,1,0:T(8,128)(2,1)}, u32[]{:S(2)}, u32[]{:S(2)}) async-start(bf16[8,1,128,1536]{3,2,1,0:T(8,128)(2,1)} %get-tuple-element.69), calls=%async_computation.2 | async-start | bytes 6291456 | tf_op jit(solution)/shard_map/all_to_all | solution.py:342
  136.0 1.3 copy-start.6
  137.3 1.4 copy-start.8
  138.6 1.3 copy-start.9
  173.6 42.9 %all-to-all-start.3 = ((bf16[8,1,128,1536]{3,2,1,0:T(8,128)(2,1)}), bf16[8,1,128,1536]{3,2,1,0:T(8,128)(2,1)}, u32[]{:S(2)}, u32[]{:S(2)}) async-start(bf16[8,1,128,1536]{3,2,1,0:T(8,128)(2,1)} %bitcast.55), calls=%async_computation.3 | async-start | bytes 6291456 | tf_op jit(solution)/shard_map/all_to_all | solution.py:342
  189.8 22.1 %collective-permute-start.5 = (bf16[2,3,256,256]{3,2,1,0:T(8,128)(2,1)}, bf16[2,3,256,256]{3,2,1,0:T(8,128)(2,1)S(1)}, u32[]{:S(2)}, u32[]{:S(2)}) collective-permute-start(bf16[2,3,256,256]{3,2,1,0:T(8,128)(2,1)} %get-tuple-element.78.refs_0_), channel_id=1, source_target_pairs={{0,64},{64,0},{1,65},{65,1},{2,66},{66,2},{3,67},{67,3},{4,68},{68... | collective-permute-start | bytes 2359304 | tf_op jit(solution)/shard_map/ppermute | solution.py:332
  211.9 4.6 %copy-start.11 = (bf16[2,3,256,256]{3,2,1,0:T(8,128)(2,1)}, bf16[2,3,256,256]{3,2,1,0:T(8,128)(2,1)S(1)}, u32[]{:S(2)}) copy-start(bf16[2,3,256,256]{3,2,1,0:T(8,128)(2,1)S(1)} %collective-permute-done.5.refs_1_) | copy-start | bytes 2359300
  216.5 46.0 %all-to-all-start.4 = ((bf16[8,1,128,1536]{3,2,1,0:T(8,128)(2,1)}), bf16[8,1,128,1536]{3,2,1,0:T(8,128)(2,1)}, u32[]{:S(2)}, u32[]{:S(2)}) async-start(bf16[8,1,128,1536]{3,2,1,0:T(8,128)(2,1)} %bitcast.54), calls=%async_computation.4 | async-start | bytes 6291456 | tf_op jit(solution)/shard_map/all_to_all | solution.py:342
  226.4 36.1 %collective-permute-start.6 = (bf16[1536,512]{1,0:T(8,128)(2,1)}, bf16[1536,512]{1,0:T(8,128)(2,1)S(1)}, u32[]{:S(2)}, u32[]{:S(2)}) collective-permute-start(bf16[1536,512]{1,0:T(8,128)(2,1)} %emit.6), channel_id=1, source_target_pairs={{0,8},{8,0},{1,9},{9,1},{2,10},{10,2},{3,11},{11,3},{4,12},{12,4},... | collective-permute-start | bytes 4718600 | tf_op jit(solution)/shard_map/ppermute | solution.py:332
  262.5 1.1 copy-start.5
  262.5 10.3 %copy-start.18 = (bf16[2,1,256,256]{3,2,1,0:T(8,128)(2,1)S(1)}, bf16[2,1,256,256]{3,2,1,0:T(8,128)(2,1)}, u32[]{:S(2)}) copy-start(bf16[2,1,256,256]{3,2,1,0:T(8,128)(2,1)} %get-tuple-element.85.refs_2_) | copy-start | bytes 786436
  263.6 48.9 %all-to-all-start.5 = ((bf16[8,1,128,1536]{3,2,1,0:T(8,128)(2,1)}), bf16[8,1,128,1536]{3,2,1,0:T(8,128)(2,1)}, u32[]{:S(2)}, u32[]{:S(2)}) async-start(bf16[8,1,128,1536]{3,2,1,0:T(8,128)(2,1)} %bitcast.29), calls=%async_computation.5 | async-start | bytes 6291456 | tf_op jit(solution)/shard_map/all_to_all | solution.py:342
  269.1 43.5 %collective-permute-start.9 = (bf16[2,4,256,256]{3,2,1,0:T(8,128)(2,1)}, bf16[2,4,256,256]{3,2,1,0:T(8,128)(2,1)S(1)}, u32[]{:S(2)}, u32[]{:S(2)}) collective-permute-start(bf16[2,4,256,256]{3,2,1,0:T(8,128)(2,1)} %get-tuple-element.87.refs_4_), channel_id=1, source_target_pairs={{0,64},{64,0},{1,65},{65,1},{2,66},{66,2},{3,67},{67,3},{4,68},{68... | collective-permute-start | bytes 3145736 | tf_op jit(solution)/shard_map/ppermute | solution.py:332
  271.9 40.6 %collective-permute-start.10 = (bf16[2,4,128,256]{3,2,1,0:T(8,128)(2,1)}, bf16[2,4,128,256]{3,2,1,0:T(8,128)(2,1)S(1)}, u32[]{:S(2)}, u32[]{:S(2)}) collective-permute-start(bf16[2,4,128,256]{3,2,1,0:T(8,128)(2,1)} %wgrad.4), channel_id=1, source_target_pairs={{0,8},{8,0},{1,9},{9,1},{2,10},{10,2},{3,11},{11,3},{4,12},{12,4},... | collective-permute-start | bytes 1572872 | tf_op jit(solution)/shard_map/ppermute | solution.py:332
  272.2 40.3 %collective-permute-start.11 = (bf16[2,4,128,256]{3,2,1,0:T(8,128)(2,1)}, bf16[2,4,128,256]{3,2,1,0:T(8,128)(2,1)}, u32[]{:S(2)}, u32[]{:S(2)}) collective-permute-start(bf16[2,4,128,256]{3,2,1,0:T(8,128)(2,1)} %wgrad.4), channel_id=1, source_target_pairs={{0,72},{8,64},{64,8},{72,0},{1,73},{9,65},{65,9},{73,1},{2,74},{10... | collective-permute-start | bytes 1572872 | tf_op jit(solution)/shard_map/ppermute | solution.py:332
  272.8 39.7 %collective-permute-start.8 = (bf16[2,1,256,256]{3,2,1,0:T(8,128)(2,1)S(1)}, bf16[2,1,256,256]{3,2,1,0:T(8,128)(2,1)}, u32[]{:S(2)}, u32[]{:S(2)}) collective-permute-start(bf16[2,1,256,256]{3,2,1,0:T(8,128)(2,1)S(1)} %copy-done.18), channel_id=1, source_target_pairs={{0,64},{64,0},{1,65},{65,1},{2,66},{66,2},{3,67},{67,3},{4,68},{68... | collective-permute-start | bytes 786440 | tf_op jit(solution)/shard_map/ppermute | solution.py:332
  280.4 45.4 %collective-permute-start.7 = (bf16[1536,512]{1,0:T(8,128)(2,1)}, bf16[1536,512]{1,0:T(8,128)(2,1)}, u32[]{:S(2)}, u32[]{:S(2)}) collective-permute-start(bf16[1536,512]{1,0:T(8,128)(2,1)} %emit.7), channel_id=1, source_target_pairs={{0,16},{16,32},{32,48},{1,17},{17,33},{33,49},{2,18},{18,34},{34,5... | collective-permute-start | bytes 4718600 | tf_op jit(solution)/shard_map/ppermute | solution.py:338
  312.5 0.8 copy-start.15
  312.6 1.1 copy-start.10
  313.7 26.0 %all-to-all-start.6 = ((bf16[8,1,128,768]{3,2,1,0:T(8,128)(2,1)}), bf16[8,1,128,768]{3,2,1,0:T(8,128)(2,1)S(1)}, u32[]{:S(2)}, u32[]{:S(2)}) async-start(bf16[8,1,128,768]{3,2,1,0:T(8,128)(2,1)} %bitcast.19), calls=%async_computation.6 | async-start | bytes 3145728 | tf_op jit(solution)/shard_map/all_to_all | solution.py:342
  319.0 18.5 %collective-permute-start.12 = (bf16[2,4,128,256]{3,2,1,0:T(8,128)(2,1)}, bf16[2,4,128,256]{3,2,1,0:T(8,128)(2,1)}, u32[]{:S(2)}, u32[]{:S(2)}) collective-permute-start(bf16[2,4,128,256]{3,2,1,0:T(8,128)(2,1)} %wgrad.5.ma_ref), channel_id=1, source_target_pairs={{0,64},{64,0},{1,65},{65,1},{2,66},{66,2},{3,67},{67,3},{4,68},{68... | collective-permute-start | bytes 1572872 | tf_op jit(solution)/shard_map/ppermute | solution.py:332
  325.4 25.9 %collective-permute-start.14 = (bf16[768,512]{1,0:T(8,128)(2,1)}, bf16[768,512]{1,0:T(8,128)(2,1)}, u32[]{:S(2)}, u32[]{:S(2)}) collective-permute-start(bf16[768,512]{1,0:T(8,128)(2,1)} %emit.10), channel_id=1, source_target_pairs={{0,8},{8,0},{1,9},{9,1},{2,10},{10,2},{3,11},{11,3},{4,12},{12,4},... | collective-permute-start | bytes 2359304 | tf_op jit(solution)/shard_map/ppermute | solution.py:332
  339.7 1.1 copy-start.1
  340.8 29.4 %all-to-all-start.7 = ((bf16[8,1,128,768]{3,2,1,0:T(8,128)(2,1)}), bf16[8,1,128,768]{3,2,1,0:T(8,128)(2,1)}, u32[]{:S(2)}, u32[]{:S(2)}) async-start(bf16[8,1,128,768]{3,2,1,0:T(8,128)(2,1)} %bitcast.21), calls=%async_computation.7 | async-start | bytes 3145728 | tf_op jit(solution)/shard_map/all_to_all | solution.py:342
  345.9 22.2 %collective-permute-start.13 = (bf16[768,512]{1,0:T(8,128)(2,1)}, bf16[768,512]{1,0:T(8,128)(2,1)S(1)}, u32[]{:S(2)}, u32[]{:S(2)}) collective-permute-start(bf16[768,512]{1,0:T(8,128)(2,1)} %emit.8), channel_id=1, source_target_pairs={{0,8},{8,0},{1,9},{9,1},{2,10},{10,2},{3,11},{11,3},{4,12},{12,4},... | collective-permute-start | bytes 2359304 | tf_op jit(solution)/shard_map/ppermute | solution.py:332
  355.4 20.4 %collective-permute-start.18 = (bf16[768,512]{1,0:T(8,128)(2,1)}, bf16[768,512]{1,0:T(8,128)(2,1)S(1)}, u32[]{:S(2)}, u32[]{:S(2)}) collective-permute-start(bf16[768,512]{1,0:T(8,128)(2,1)} %emit.11), channel_id=1, source_target_pairs={{16,0},{32,16},{48,32},{17,1},{33,17},{49,33},{18,2},{34,18},{50,3... | collective-permute-start | bytes 2359304 | tf_op jit(solution)/shard_map/ppermute | solution.py:338
  368.1 2.1 copy-start.12
  368.1 14.4 %collective-permute-start.15 = (bf16[2,4,256,128]{3,2,1,0:T(8,128)(2,1)}, bf16[2,4,256,128]{3,2,1,0:T(8,128)(2,1)}, u32[]{:S(2)}, u32[]{:S(2)}) collective-permute-start(bf16[2,4,256,128]{3,2,1,0:T(8,128)(2,1)} %wgrad.6), channel_id=1, source_target_pairs={{0,8},{8,0},{1,9},{9,1},{2,10},{10,2},{3,11},{11,3},{4,12},{12,4},... | collective-permute-start | bytes 1572872 | tf_op jit(solution)/shard_map/ppermute | solution.py:332
  369.3 13.9 %collective-permute-start.16 = (bf16[2,4,256,128]{3,2,1,0:T(8,128)(2,1)}, bf16[2,4,256,128]{3,2,1,0:T(8,128)(2,1)}, u32[]{:S(2)}, u32[]{:S(2)}) collective-permute-start(bf16[2,4,256,128]{3,2,1,0:T(8,128)(2,1)} %wgrad.6), channel_id=1, source_target_pairs={{0,72},{8,64},{64,8},{72,0},{1,73},{9,65},{65,9},{73,1},{2,74},{10... | collective-permute-start | bytes 1572872 | tf_op jit(solution)/shard_map/ppermute | solution.py:332
  375.8 6.8 %copy-start.14 = (bf16[768,512]{1,0:T(8,128)(2,1)}, bf16[768,512]{1,0:T(8,128)(2,1)S(1)}, u32[]{:S(2)}) copy-start(bf16[768,512]{1,0:T(8,128)(2,1)S(1)} %collective-permute-done.18.value_ref) | copy-start | bytes 2359300
  375.8 20.5 %collective-permute-start.19 = (bf16[768,512]{1,0:T(8,128)(2,1)}, bf16[768,512]{1,0:T(8,128)(2,1)S(1)}, u32[]{:S(2)}, u32[]{:S(2)}) collective-permute-start(bf16[768,512]{1,0:T(8,128)(2,1)} %emit.9), channel_id=1, source_target_pairs={{16,0},{32,16},{48,32},{17,1},{33,17},{49,33},{18,2},{34,18},{50,3... | collective-permute-start | bytes 2359304 | tf_op jit(solution)/shard_map/ppermute | solution.py:338
  383.2 13.1 %collective-permute-start.17 = (bf16[2,4,256,128]{3,2,1,0:T(8,128)(2,1)}, bf16[2,4,256,128]{3,2,1,0:T(8,128)(2,1)S(1)}, u32[]{:S(2)}, u32[]{:S(2)}) collective-permute-start(bf16[2,4,256,128]{3,2,1,0:T(8,128)(2,1)} %wgrad.7.ma_ref), channel_id=1, source_target_pairs={{0,64},{64,0},{1,65},{65,1},{2,66},{66,2},{3,67},{67,3},{4,68},{68... | collective-permute-start | bytes 1572872 | tf_op jit(solution)/shard_map/ppermute | solution.py:332
  396.3 0.8 copy-start.16
  397.1 0.9 copy-start.13
